TPU v7x, 128 devices: a whole 4x4x4 slice. The times are simulated.
128 devices in a mesh: ice: 64 (over y_hi, z, x, core), hyd: 2 (over y_lo).
Axes of the slice: x: 4, y: 4 (y_hi: 2, y_lo: 2; y = y_hi * 2 + y_lo), z: 4, core: 2. Of those that a mesh axis runs over, the one named last changes fastest.
Arguments:
- viscosity: bfloat16 [20, 1024, 6144], P(None, 'ice', 'hyd'), may hold values from 0.29882812 to 3
- driving_stress: float32 [2, 1024, 6144], P(None, 'ice', 'hyd'), may hold values from -120 to 120
- ice_mask: int32 [1024, 6144], P('ice', 'hyd'), may hold values 0 or 1
- float_mask: int32 [1024, 6144], P('ice', 'hyd'), may hold values 0 or 1
- friction: float32 [1024, 6144], P('ice', 'hyd'), may hold values from 1 to 10
- geothermal: float32 [1024, 6144], P('ice', 'hyd'), may hold values from 0.2 to 2
- potential_prev: float32 [1024, 6144], P(('ice', 'hyd')), may hold values from 0.5 to 2.5
- overburden: float32 [1024, 6144], P(('ice', 'hyd')), may hold values from 1.5 to 3.5
- sheet_thick: float32 [1024, 6144], P(('ice', 'hyd')), may hold values from 0.05 to 0.5
- channel_east: int32 [1024, 6144], P(('ice', 'hyd')), may hold values 0 or 1
- channel_south: int32 [1024, 6144], P(('ice', 'hyd')), may hold values 0 or 1
- channel_area: float32 [1024, 6144], P(('ice', 'hyd')), may hold values from 0.2 to 2
Outputs:
- velocity: float32 [2, 20, 1024, 6144], P(None, None, 'ice', 'hyd')
- effective_pressure: float32 [1024, 6144], P('ice', 'hyd')
- potential: float32 [1024, 6144], P(('ice', 'hyd'))
- sheet_next: float32 [1024, 6144], P(('ice', 'hyd'))
All inputs are finite; a program needn't handle non-finite values. No bound on the sum of `ice_mask` or of `float_mask` or of `channel_east` or of `channel_south` on one device may be relied on, other than what follows from the above.
Results may differ from a plain program's by a relative error of at most 0.0004.
Values may be sent and summed in bfloat16 or wider, within the bound.
No kernel may reach another device: no remote copies, remote signals or barrier semaphores. Data moves between devices by JAX's collectives and lax.ppermute only.
A program may use at most 192 MiB of HBM per device.

v0:
```python
import jax
import jax.numpy as jnp
from jax import lax
from jax.sharding import PartitionSpec as P

KRYLOV = 2
HYD_ITERS = 3


vertical_weight = 4.0
relax_weight = 0.1
melt_factor = 0.5
sheet_conduct = 2.0
channel_conduct = 1.5
storage = 1.0
bump_height = 0.3
time_step = 0.5
speed_floor = 0.25


def with_halo(cells, sides, width):
    for axis, dim in sides:
        count = lax.axis_size(axis)
        ends = count - 1
        head = lax.slice_in_dim(cells, 0, width, axis=dim)
        tail = lax.slice_in_dim(cells, cells.shape[dim] - width, cells.shape[dim], axis=dim)
        cells = jnp.concatenate(
            [
                lax.ppermute(tail, axis, [(i, (i + 1) % count) for i in range(ends)]),
                cells,
                lax.ppermute(head, axis, [((i + 1) % count, i) for i in range(ends)]),
            ],
            axis=dim,
        )
    return cells


def shifted(value, axis, steps):
    count = lax.axis_size(axis)
    leading, last = (max(0, -steps), min(count, count - steps))
    return lax.ppermute(value, axis, [(source, source + steps) for source in range(leading, last)])


def faces_from(padded):
    center = padded[:, 1:-1, 1:-1]
    east_face = jnp.sqrt(center * padded[:, 1:-1, 2:])
    west_face = jnp.sqrt(center * padded[:, 1:-1, :-2])
    south_face = jnp.sqrt(center * padded[:, 2:, 1:-1])
    north_face = jnp.sqrt(center * padded[:, :-2, 1:-1])
    upward = jnp.sqrt(center[1:] * center[:-1])
    return (east_face, west_face, south_face, north_face, upward)


def one_component(padded, face_set, diagonal, col_factor, row_factor):
    east_face, west_face, south_face, north_face, upward = face_set
    center = padded[:, 1:-1, 1:-1]
    along_cols = east_face * (center - padded[:, 1:-1, 2:]) + west_face * (
        center - padded[:, 1:-1, :-2]
    )
    along_rows = south_face * (center - padded[:, 2:, 1:-1]) + north_face * (
        center - padded[:, :-2, 1:-1]
    )
    vertical_flux = upward * (center[1:] - center[:-1])
    vertical = jnp.pad(vertical_flux, ((1, 0), (0, 0), (0, 0))) - jnp.pad(
        vertical_flux, ((0, 1), (0, 0), (0, 0))
    )
    return (
        diagonal * center
        + col_factor * along_cols
        + row_factor * along_rows
        + vertical_weight * vertical
    )


def apply_operator(padded, face_set, diagonal):
    first = one_component(padded[0], face_set, diagonal, 4.0, 1.0)
    second = one_component(padded[1], face_set, diagonal, 1.0, 4.0)
    return jnp.stack([first, second])


def sweep(
    padded, east_face, west_face, south_face, north_face, fixed_part, overburden, sheet_thick
):
    current = padded[1:-1]
    right_value = jnp.pad(current[:, 1:], ((0, 0), (0, 1)))
    left_value = jnp.pad(current[:, :-1], ((0, 0), (1, 0)))
    gathered = (
        east_face * right_value
        + west_face * left_value
        + south_face * padded[2:]
        + north_face * padded[:-2]
    )
    conduct_sum = east_face + west_face + south_face + north_face
    creep_rate = sheet_thick * jnp.abs(overburden - current)
    return (fixed_part + creep_rate * overburden + gathered) / (storage + creep_rate + conduct_sum)


def squares(vector):
    return lax.psum(jnp.sum(vector * vector), ("ice", "hyd"))


def body(
    viscosity,
    driving_stress,
    ice_mask,
    float_mask,
    friction,
    geothermal,
    potential_prev,
    overburden,
    sheet_thick,
    channel_east,
    channel_south,
    channel_area,
):
    layers = viscosity.shape[0]
    ice_cover = ice_mask.astype(jnp.float32)
    grounded = ice_cover * (1.0 - float_mask.astype(jnp.float32))
    bottom = (jnp.arange(layers) == 0).astype(jnp.float32)[:, None, None]
    diagonal = (1.0 - ice_cover + relax_weight * ice_cover)[None] + bottom * (friction * grounded)[
        None
    ]
    forcing = jnp.broadcast_to(
        (driving_stress * ice_cover[None])[:, None], (2, layers) + ice_cover.shape
    )
    weight_half = viscosity * ice_mask.astype(jnp.bfloat16)[None]
    padded_weight = with_halo(weight_half, (("ice", 1), ("hyd", 2)), 1)
    face_set = faces_from(padded_weight.astype(jnp.float32))
    solution = jnp.zeros(forcing.shape, jnp.float32)
    residual = forcing
    direction = forcing
    norm_now = squares(residual)
    for iteration in range(KRYLOV):
        padded = with_halo(direction, (("ice", 2), ("hyd", 3)), 1)
        applied = apply_operator(padded, face_set, diagonal)
        step_size = norm_now / lax.psum(jnp.sum(direction * applied), ("ice", "hyd"))
        solution = solution + step_size * direction
        if iteration + 1 < KRYLOV:
            residual = residual - step_size * applied
            norm_next = squares(residual)
            direction = residual + norm_next / norm_now * direction
            norm_now = norm_next
    slide_sq = solution[0, 0] * solution[0, 0] + solution[1, 0] * solution[1, 0]
    slide_speed = jnp.sqrt(slide_sq + speed_floor)
    melt_rate = melt_factor * (geothermal + friction * grounded * slide_sq)
    melt_strip, speed_strip = (
        lax.all_to_all(melt_rate, "hyd", split_axis=0, concat_axis=1, tiled=True),
        lax.all_to_all(slide_speed, "hyd", split_axis=0, concat_axis=1, tiled=True),
    )
    east_face = (
        sheet_conduct * sheet_thick
        + channel_conduct * channel_east.astype(jnp.float32) * channel_area
    )
    south_face = (
        sheet_conduct * sheet_thick
        + channel_conduct * channel_south.astype(jnp.float32) * channel_area
    )
    west_face = jnp.pad(east_face[:, :-1], ((0, 0), (1, 0)))
    upper_row = shifted(south_face[-1:], ("ice", "hyd"), 1)
    north_face = jnp.concatenate([upper_row, south_face[:-1]], axis=0)
    opening = speed_strip * jnp.maximum(bump_height - sheet_thick, 0.0)
    fixed_part = storage * potential_prev + melt_strip - opening
    potential = potential_prev
    for iteration in range(HYD_ITERS):
        padded_rows = with_halo(potential, ((("ice", "hyd"), 0),), 1)
        potential = sweep(
            padded_rows,
            east_face,
            west_face,
            south_face,
            north_face,
            fixed_part,
            overburden,
            sheet_thick,
        )
    pressure = overburden - potential
    sheet_next = sheet_thick + time_step * (opening - sheet_thick * jnp.abs(pressure) * pressure)
    effective = lax.all_to_all(pressure, "hyd", split_axis=1, concat_axis=0, tiled=True)
    return (solution, effective, potential, sheet_next)


def solution(mesh):
    placed = (
        P(None, "ice", "hyd"),
        P(None, "ice", "hyd"),
        P("ice", "hyd"),
        P("ice", "hyd"),
        P("ice", "hyd"),
        P("ice", "hyd"),
        P(("ice", "hyd"), None),
        P(("ice", "hyd"), None),
        P(("ice", "hyd"), None),
        P(("ice", "hyd"), None),
        P(("ice", "hyd"), None),
        P(("ice", "hyd"), None),
    )
    return jax.shard_map(
        body,
        mesh=mesh,
        in_specs=placed,
        out_specs=(
            P(None, None, "ice", "hyd"),
            P("ice", "hyd"),
            P(("ice", "hyd"), None),
            P(("ice", "hyd"), None),
        ),
        check_vma=False,
    )
```

profile of v0, /device:TPU:16, one launch (start us, length us, event | category | flops | bytes accessed | tf_op | source)
XLA Modules:
  0.0 561.5 jit_solution(13740301686778877052)
XLA Ops:
  6.3 9.4 %collective-permute-start.1 = (f32[2,20,1,3072]{3,2,1,0:T(1,128)S(1)}, f32[2,20,1,3072]{3,2,1,0:T(1,128)S(1)}, u32[]{:S(2)}, u32[]{:S(2)}) collective-permute-start(f32[2,20,1,3072]{3,2,1,0:T(1,128)S(1)} %broadcast_in_dim.24), channel_id=1, source_target_pairs={{2,0},{4,2},{6,4},{8,6},{10,8},{12,10},{14,12},{16,14},{18,16},{20... | collective-permute-start | bytes 1474568 | tf_op jit(solution)/shard_map/ppermute | solution.py:31
  18.1 9.4 %collective-permute-start.5 = (bf16[20,1,3072]{2,1,0:T(2,128)(2,1)S(1)}, bf16[20,1,3072]{2,1,0:T(2,128)(2,1)S(1)}, u32[]{:S(2)}, u32[]{:S(2)}) collective-permute-start(bf16[20,1,3072]{2,1,0:T(2,128)(2,1)S(1)} %get-tuple-element.33), channel_id=1, source_target_pairs={{2,0},{4,2},{6,4},{8,6},{10,8},{12,10},{14,12},{16,14},{18,16},{20... | collective-permute-start | bytes 368648 | tf_op jit(solution)/shard_map/ppermute | solution.py:31
  52.1 6.3 %concatenate.45 = bf16[20,18,3074]{2,1,0:T(8,128)(2,1)} concatenate(bf16[20,18,1]{2,1,0:T(8,128)(2,1)S(1)} %collective-permute-done.6, bf16[20,18,3072]{2,1,0:T(8,128)(2,1)} %copy-done.4, bf16[20,18,1]{2,1,0:T(8,128)(2,1)S(1)} %collective-permute-done.7), dimensions={2} | concatenate | bytes 4426560 | tf_op jit(solution)/shard_map/concatenate | solution.py:27
  63.3 14.3 %concatenate.43 = f32[2,20,18,3074]{3,2,1,0:T(8,128)} concatenate(f32[2,20,18,1]{3,2,1,0:T(8,128)S(1)} %collective-permute-done.2, f32[2,20,18,3072]{3,2,1,0:T(8,128)} %copy-done.2, f32[2,20,18,1]{3,2,1,0:T(8,128)S(1)} %collective-permute-done.3), dimensions={3} | concatenate | bytes 17706240 | tf_op jit(solution)/shard_map/concatenate | solution.py:27
  77.6 9.9 %slice_bitcast_fusion.2 = (f32[20,18,3074]{2,1,0:T(8,128)}, f32[20,18,3074]{2,1,0:T(8,128)}) fusion(f32[2,20,18,3074]{3,2,1,0:T(8,128)} %concatenate.43), kind=kLoop, calls=%fused_computation.12 | loop fusion | bytes 17706240 | tf_op jit(solution)/shard_map/squeeze | solution.py:77
  87.5 16.4 %fusion.53 = (f32[19,16,3072]{2,1,0:T(8,128)}, f32[19,16,3072]{2,1,0:T(8,128)}) fusion(f32[20,18,3074]{2,1,0:T(8,128)} %get-tuple-element.21, f32[20,18,3074]{2,1,0:T(8,128)} %convert_element_type.48), kind=kLoop, calls=%fused_computation.91 | loop fusion | flops 2801664 | bytes 22413312 | tf_op jit(solution)/shard_map/mul | solution.py:63
  103.9 10.3 %fusion.52 = f32[19,16,3072]{2,1,0:T(8,128)} fusion(f32[19,16,3072]{2,1,0:T(8,128)} %get-tuple-element.17, f32[20,18,3074]{2,1,0:T(8,128)} %get-tuple-element.20), kind=kLoop, calls=%fused_computation.89 | loop fusion | flops 1867776 | bytes 14942208 | tf_op jit(solution)/shard_map/mul | solution.py:63
  114.2 15.1 %fusion.39 = (f32[1,20,16,3072]{3,2,1,0:T(8,128)}, f32[20,16,3072]{2,1,0:T(8,128)}, f32[20,16,3072]{2,1,0:T(8,128)}, f32[20,16,3072]{2,1,0:T(8,128)}, f32[20,16,3072]{2,1,0:T(8,128)}) fusion(f32[20,18,3074]{2,1,0:T(8,128)S(1)} %copy-done.1, f32[19,16,3072]{2,1,0:T(8,128)} %get-tuple-element.16, f32[16,3072]{1,0:T(8,128)S(1)} %get-tuple-element.53, ...), kind=kLoop, calls=%fused_computation.64 | loop fusion | flops 22609920 | bytes 63111248 | tf_op jit(solution)/shard_map/stack | solution.py:78
  129.3 23.6 %fusion.29 = f32[1,20,16,3072]{3,2,1,0:T(8,128)} fusion(f32[20,16,3072]{2,1,0:T(8,128)} %get-tuple-element.15, f32[20,18,3074]{2,1,0:T(8,128)} %get-tuple-element.20, f32[20,16,3072]{2,1,0:T(8,128)} %get-tuple-element.14, f32[20,16,3072]{2,1,0:T(8,128)} %get-tuple-element.13, f32[20,16,3072]{2,1,0:T(8,128)} %get-tuple-element.12, ...), kind=kLoop, calls=%fused_computation.50 | loop fusion | flops 18677760 | bytes 43450448 | tf_op jit(solution)/shard_map/stack | solution.py:78
  152.8 5.9 %multiply_reduce_fusion.1 = (f32[]{:T(128)}, f32[]{:T(128)}) fusion(f32[1,20,16,3072]{3,2,1,0:T(8,128)} %fusion.29, f32[1,20,16,3072]{3,2,1,0:T(8,128)} %get-tuple-element.11, f32[2,16,3072]{2,1,0:T(8,128)S(1)} %get-tuple-element.10, f32[2,16,3072]{2,1,0:T(8,128)S(1)} %copy-done.10), kind=kLoop, calls=%fused_computation.8 | loop fusion | flops 7864318 | bytes 8650760 | tf_op jit(solution)/shard_map/reduce_sum | solution.py:136
  158.8 67.2 %all-reduce.15 = (f32[]{:T(128)}, f32[]{:T(128)}) all-reduce(f32[]{:T(128)} %get-tuple-element.57, f32[]{:T(128)} %get-tuple-element.56), channel_id=1, replica_groups=mesh['ice'=64,'hyd'=2] {'ice','hyd'}, use_global_device_ids=true, to_apply=%region_1.0 | all-reduce | flops 2 | bytes 16 | tf_op jit(solution)/shard_map/psum | solution.py:99
  232.2 62.0 %psum.30 = f32[]{:T(128)} all-reduce(f32[]{:T(128)} %multiply_reduce_fusion), channel_id=1, replica_groups=mesh['ice'=64,'hyd'=2] {'ice','hyd'}, use_global_device_ids=true, to_apply=%region_5.6 | all-reduce | flops 1 | bytes 8 | tf_op jit(solution)/shard_map/psum | solution.py:99
  303.1 9.4 %collective-permute-start.9 = (f32[2,20,1,3072]{3,2,1,0:T(1,128)S(1)}, f32[2,20,1,3072]{3,2,1,0:T(1,128)S(1)}, u32[]{:S(2)}, u32[]{:S(2)}) collective-permute-start(f32[2,20,1,3072]{3,2,1,0:T(1,128)S(1)} %get-tuple-element.27), channel_id=1, source_target_pairs={{2,0},{4,2},{6,4},{8,6},{10,8},{12,10},{14,12},{16,14},{18,16},{20... | collective-permute-start | bytes 1474568 | tf_op jit(solution)/shard_map/ppermute | solution.py:31
  332.5 9.6 %collective-permute-start.12 = (f32[1,6144]{1,0:T(1,128)}, f32[1,6144]{1,0:T(1,128)}, u32[]{:S(2)}, u32[]{:S(2)}) collective-permute-start(f32[1,6144]{1,0:T(1,128)} %get-tuple-element.50), channel_id=1, source_target_pairs={{1,0},{2,1},{3,2},{4,3},{5,4},{6,5},{7,6},{8,7},{9,8},{10,9},{11,1... | collective-permute-start | bytes 73736 | tf_op jit(solution)/shard_map/ppermute | solution.py:31
  342.1 14.5 %concatenate.47 = f32[2,20,18,3074]{3,2,1,0:T(8,128)} concatenate(f32[2,20,18,1]{3,2,1,0:T(8,128)S(1)} %collective-permute-done.10, f32[2,20,18,3072]{3,2,1,0:T(8,128)} %copy-done.3, f32[2,20,18,1]{3,2,1,0:T(8,128)S(1)} %collective-permute-done.11), dimensions={3} | concatenate | bytes 17706240 | tf_op jit(solution)/shard_map/concatenate | solution.py:27
  356.6 8.0 %slice_bitcast_fusion.1 = (f32[20,18,3074]{2,1,0:T(8,128)}, f32[20,18,3074]{2,1,0:T(8,128)S(1)}) fusion(f32[2,20,18,3074]{3,2,1,0:T(8,128)} %concatenate.47), kind=kLoop, calls=%fused_computation.11 | loop fusion | bytes 17706240 | tf_op jit(solution)/shard_map/squeeze | solution.py:76
  364.6 13.9 %fusion.51 = (f32[19,16,3072]{2,1,0:T(8,128)}, f32[19,16,3072]{2,1,0:T(8,128)}) fusion(f32[19,16,3072]{2,1,0:T(8,128)} %get-tuple-element.17, f32[20,18,3074]{2,1,0:T(8,128)} %get-tuple-element.18, f32[20,18,3074]{2,1,0:T(8,128)S(1)} %get-tuple-element.19), kind=kLoop, calls=%fused_computation.87 | loop fusion | flops 3735552 | bytes 26148864 | tf_op jit(solution)/shard_map/mul | solution.py:63
  378.6 23.4 %fusion.17 = f32[1,20,16,3072]{3,2,1,0:T(8,128)} fusion(f32[20,16,3072]{2,1,0:T(8,128)} %get-tuple-element.15, f32[20,18,3074]{2,1,0:T(8,128)} %get-tuple-element.18, f32[20,16,3072]{2,1,0:T(8,128)} %get-tuple-element.14, f32[20,16,3072]{2,1,0:T(8,128)} %get-tuple-element.13, f32[20,16,3072]{2,1,0:T(8,128)} %get-tuple-element.12, ...), kind=kLoop, calls=%fused_computation.34 | loop fusion | flops 18677760 | bytes 43450448 | tf_op jit(solution)/shard_map/stack | solution.py:78
  402.0 23.4 %fusion.7 = f32[1,20,16,3072]{3,2,1,0:T(8,128)} fusion(f32[20,16,3072]{2,1,0:T(8,128)} %get-tuple-element.15, f32[20,18,3074]{2,1,0:T(8,128)} %copy-done, f32[20,16,3072]{2,1,0:T(8,128)} %get-tuple-element.14, f32[20,16,3072]{2,1,0:T(8,128)} %get-tuple-element.13, f32[20,16,3072]{2,1,0:T(8,128)} %get-tuple-element.12, f32[19,16,3072]{2,1,0:T(8,128)} %get-tuple-element.29, ...), kind=kLoop, calls=%fused_computation.20 | loop fusion | flops 18677760 | bytes 43450448 | tf_op jit(solution)/shard_map/stack | solution.py:78
  425.4 7.2 %fusion = f32[]{:T(128)} fusion(f32[1,20,16,3072]{3,2,1,0:T(8,128)} %fusion.7, f32[1,20,16,3072]{3,2,1,0:T(8,128)} %fusion.17, f32[2,16,3072]{2,1,0:T(8,128)S(1)} %get-tuple-element.37, f32[1,20,16,3072]{3,2,1,0:T(8,128)} %fusion.29, f32[1,20,16,3072]{3,2,1,0:T(8,128)} %get-tuple-element.11, f32[]{:T(128)S(6)} %div.18, f32[2,16,3072]{2,1,0:T(8,128)S(1)} %get-tuple-element.10), kind=kLoop, calls=%fused_computation.4 | loop fusion | flops 13762559 | bytes 16515080 | tf_op jit(solution)/shard_map/reduce_sum | solution.py:136
  434.5 66.2 %psum.31 = f32[]{:T(128)} all-reduce(f32[]{:T(128)} %fusion), channel_id=1, replica_groups=mesh['ice'=64,'hyd'=2] {'ice','hyd'}, use_global_device_ids=true, to_apply=%region_7.8 | all-reduce | flops 1 | bytes 8 | tf_op jit(solution)/shard_map/psum | solution.py:136
  533.8 5.3 collective-permute-done.16
  546.2 5.3 collective-permute-done.18
  553.4 7.2 %all_to_all.54 = f32[8,2,3072]{2,0,1:T(8,128)S(1)} all-to-all(f32[8,2,3072]{2,0,1:T(8,128)S(1)} %bitcast.60), channel_id=1, replica_groups=mesh['ice'=64,'hyd'=2] {'hyd'}, dimensions={1} | all-to-all | bytes 393216 | tf_op jit(solution)/shard_map/all_to_all | solution.py:178
  (119 shorter events, 113.0 us)
Async XLA Ops:
  1.8 25.7 %copy-start.12 = (s32[16,3072]{1,0:T(8,128)S(1)}, s32[16,3072]{1,0:T(8,128)}, u32[]{:S(2)}) copy-start(s32[16,3072]{1,0:T(8,128)} %param.14) | copy-start | bytes 589828
  1.8 25.7 %copy-start.16 = (f32[16,3072]{1,0:T(8,128)S(1)}, f32[16,3072]{1,0:T(8,128)}, u32[]{:S(2)}) copy-start(f32[16,3072]{1,0:T(8,128)} %param.16) | copy-start | bytes 589828
  4.1 33.4 %collective-permute-start = (f32[2,20,1,3072]{3,2,1,0:T(1,128)S(1)}, f32[2,20,1,3072]{3,2,1,0:T(1,128)S(1)}, u32[]{:S(2)}, u32[]{:S(2)}) collective-permute-start(f32[2,20,1,3072]{3,2,1,0:T(1,128)S(1)} %broadcast_in_dim.23), channel_id=1, source_target_pairs={{0,2},{2,4},{4,6},{6,8},{8,10},{10,12},{12,14},{14,16},{16,18},{18... | collective-permute-start | bytes 1474568 | tf_op jit(solution)/shard_map/ppermute | solution.py:29
  6.3 31.2 %collective-permute-start.1 = (f32[2,20,1,3072]{3,2,1,0:T(1,128)S(1)}, f32[2,20,1,3072]{3,2,1,0:T(1,128)S(1)}, u32[]{:S(2)}, u32[]{:S(2)}) collective-permute-start(f32[2,20,1,3072]{3,2,1,0:T(1,128)S(1)} %broadcast_in_dim.24), channel_id=1, source_target_pairs={{2,0},{4,2},{6,4},{8,6},{10,8},{12,10},{14,12},{16,14},{18,16},{20... | collective-permute-start | bytes 1474568 | tf_op jit(solution)/shard_map/ppermute | solution.py:31
  16.2 13.2 %collective-permute-start.4 = (bf16[20,1,3072]{2,1,0:T(2,128)(2,1)S(1)}, bf16[20,1,3072]{2,1,0:T(2,128)(2,1)S(1)}, u32[]{:S(2)}, u32[]{:S(2)}) collective-permute-start(bf16[20,1,3072]{2,1,0:T(2,128)(2,1)S(1)} %get-tuple-element.32), channel_id=1, source_target_pairs={{0,2},{2,4},{4,6},{6,8},{8,10},{10,12},{12,14},{14,16},{16,18},{18... | collective-permute-start | bytes 368648 | tf_op jit(solution)/shard_map/ppermute | solution.py:29
  18.1 13.1 %collective-permute-start.5 = (bf16[20,1,3072]{2,1,0:T(2,128)(2,1)S(1)}, bf16[20,1,3072]{2,1,0:T(2,128)(2,1)S(1)}, u32[]{:S(2)}, u32[]{:S(2)}) collective-permute-start(bf16[20,1,3072]{2,1,0:T(2,128)(2,1)S(1)} %get-tuple-element.33), channel_id=1, source_target_pairs={{2,0},{4,2},{6,4},{8,6},{10,8},{12,10},{14,12},{16,14},{18,16},{20... | collective-permute-start | bytes 368648 | tf_op jit(solution)/shard_map/ppermute | solution.py:31
  32.9 19.2 %collective-permute-start.6 = (bf16[20,18,1]{2,1,0:T(8,128)(2,1)S(1)}, bf16[20,18,1]{2,1,0:T(8,128)(2,1)S(1)}, u32[]{:S(2)}, u32[]{:S(2)}) collective-permute-start(bf16[20,18,1]{2,1,0:T(8,128)(2,1)S(1)} %get-tuple-element.31), channel_id=1, source_target_pairs={{0,1},{2,3},{4,5},{6,7},{8,9},{10,11},{12,13},{14,15},{16,17},{18,... | collective-permute-start | bytes 2168 | tf_op jit(solution)/shard_map/ppermute | solution.py:29
  36.1 15.9 %collective-permute-start.7 = (bf16[20,18,1]{2,1,0:T(8,128)(2,1)S(1)}, bf16[20,18,1]{2,1,0:T(8,128)(2,1)S(1)}, u32[]{:S(2)}, u32[]{:S(2)}) collective-permute-start(bf16[20,18,1]{2,1,0:T(8,128)(2,1)S(1)} %get-tuple-element.30), channel_id=1, source_target_pairs={{1,0},{3,2},{5,4},{7,6},{9,8},{11,10},{13,12},{15,14},{17,16},{19,... | collective-permute-start | bytes 2168 | tf_op jit(solution)/shard_map/ppermute | solution.py:31
  45.5 17.8 %collective-permute-start.2 = (f32[2,20,18,1]{3,2,1,0:T(8,128)S(1)}, f32[2,20,18,1]{3,2,1,0:T(8,128)S(1)}, u32[]{:S(2)}, u32[]{:S(2)}) collective-permute-start(f32[2,20,18,1]{3,2,1,0:T(8,128)S(1)} %get-tuple-element.25), channel_id=1, source_target_pairs={{0,1},{2,3},{4,5},{6,7},{8,9},{10,11},{12,13},{14,15},{16,17},{18,... | collective-permute-start | bytes 8648 | tf_op jit(solution)/shard_map/ppermute | solution.py:29
  50.1 13.2 %collective-permute-start.3 = (f32[2,20,18,1]{3,2,1,0:T(8,128)S(1)}, f32[2,20,18,1]{3,2,1,0:T(8,128)S(1)}, u32[]{:S(2)}, u32[]{:S(2)}) collective-permute-start(f32[2,20,18,1]{3,2,1,0:T(8,128)S(1)} %get-tuple-element.24), channel_id=1, source_target_pairs={{1,0},{3,2},{5,4},{7,6},{9,8},{11,10},{13,12},{15,14},{17,16},{19,... | collective-permute-start | bytes 8648 | tf_op jit(solution)/shard_map/ppermute | solution.py:31
  301.2 16.9 %collective-permute-start.8 = (f32[2,20,1,3072]{3,2,1,0:T(1,128)S(1)}, f32[2,20,1,3072]{3,2,1,0:T(1,128)S(1)}, u32[]{:S(2)}, u32[]{:S(2)}) collective-permute-start(f32[2,20,1,3072]{3,2,1,0:T(1,128)S(1)} %get-tuple-element.26), channel_id=1, source_target_pairs={{0,2},{2,4},{4,6},{6,8},{8,10},{10,12},{12,14},{14,16},{16,18},{18... | collective-permute-start | bytes 1474568 | tf_op jit(solution)/shard_map/ppermute | solution.py:29
  303.1 15.7 %collective-permute-start.9 = (f32[2,20,1,3072]{3,2,1,0:T(1,128)S(1)}, f32[2,20,1,3072]{3,2,1,0:T(1,128)S(1)}, u32[]{:S(2)}, u32[]{:S(2)}) collective-permute-start(f32[2,20,1,3072]{3,2,1,0:T(1,128)S(1)} %get-tuple-element.27), channel_id=1, source_target_pairs={{2,0},{4,2},{6,4},{8,6},{10,8},{12,10},{14,12},{16,14},{18,16},{20... | collective-permute-start | bytes 1474568 | tf_op jit(solution)/shard_map/ppermute | solution.py:31
  313.2 208.8 %collective-permute-start.13 = (f32[1,6144]{1,0:T(1,128)}, f32[1,6144]{1,0:T(1,128)}, u32[]{:S(2)}, u32[]{:S(2)}) collective-permute-start(f32[1,6144]{1,0:T(1,128)} %slice.376), channel_id=1, source_target_pairs={{0,1},{1,2},{2,3},{3,4},{4,5},{5,6},{6,7},{7,8},{8,9},{9,10},{10,1... | collective-permute-start | bytes 73736 | tf_op jit(solution)/shard_map/ppermute | solution.py:41
  325.9 16.3 %collective-permute-start.10 = (f32[2,20,18,1]{3,2,1,0:T(8,128)S(1)}, f32[2,20,18,1]{3,2,1,0:T(8,128)S(1)}, u32[]{:S(2)}, u32[]{:S(2)}) collective-permute-start(f32[2,20,18,1]{3,2,1,0:T(8,128)S(1)} %get-tuple-element.23), channel_id=1, source_target_pairs={{0,1},{2,3},{4,5},{6,7},{8,9},{10,11},{12,13},{14,15},{16,17},{18,... | collective-permute-start | bytes 8648 | tf_op jit(solution)/shard_map/ppermute | solution.py:29
  330.6 11.5 %collective-permute-start.11 = (f32[2,20,18,1]{3,2,1,0:T(8,128)S(1)}, f32[2,20,18,1]{3,2,1,0:T(8,128)S(1)}, u32[]{:S(2)}, u32[]{:S(2)}) collective-permute-start(f32[2,20,18,1]{3,2,1,0:T(8,128)S(1)} %get-tuple-element.22), channel_id=1, source_target_pairs={{1,0},{3,2},{5,4},{7,6},{9,8},{11,10},{13,12},{15,14},{17,16},{19,... | collective-permute-start | bytes 8648 | tf_op jit(solution)/shard_map/ppermute | solution.py:31
  332.5 189.5 %collective-permute-start.12 = (f32[1,6144]{1,0:T(1,128)}, f32[1,6144]{1,0:T(1,128)}, u32[]{:S(2)}, u32[]{:S(2)}) collective-permute-start(f32[1,6144]{1,0:T(1,128)} %get-tuple-element.50), channel_id=1, source_target_pairs={{1,0},{2,1},{3,2},{4,3},{5,4},{6,5},{7,6},{8,7},{9,8},{10,9},{11,1... | collective-permute-start | bytes 73736 | tf_op jit(solution)/shard_map/ppermute | solution.py:31
  425.4 76.6 %copy-start.11 = (f32[2,16,3072]{2,1,0:T(8,128)S(1)}, f32[2,16,3072]{2,1,0:T(8,128)}, u32[]{:S(2)}) copy-start(f32[2,16,3072]{2,1,0:T(8,128)} %get-tuple-element.36) | copy-start | bytes 1179652
  432.6 89.4 %collective-permute-start.14 = (f32[1,6144]{1,0:T(1,128)}, f32[1,6144]{1,0:T(1,128)S(1)}, u32[]{:S(2)}, u32[]{:S(2)}) collective-permute-start(f32[1,6144]{1,0:T(1,128)} %get-tuple-element.51), channel_id=1, source_target_pairs={{0,1},{1,2},{2,3},{3,4},{4,5},{5,6},{6,7},{7,8},{8,9},{9,10},{10,1... | collective-permute-start | bytes 73736 | tf_op jit(solution)/shard_map/ppermute | solution.py:29
  510.2 8.2 %all-to-all-start = ((f32[2,8,3072]{2,1,0:T(8,128)}), f32[2,8,3072]{2,1,0:T(8,128)S(1)}, u32[]{:S(2)}, u32[]{:S(2)}) async-start(f32[2,8,3072]{2,1,0:T(8,128)} %fusion.76), calls=%async_computation | async-start | bytes 393216 | tf_op jit(solution)/shard_map/all_to_all | solution.py:147
  518.4 8.2 %all-to-all-start.1 = ((f32[2,8,3072]{2,1,0:T(8,128)}), f32[2,8,3072]{2,1,0:T(8,128)S(1)}, u32[]{:S(2)}, u32[]{:S(2)}) async-start(f32[2,8,3072]{2,1,0:T(8,128)} %sqrt_bitcast_fusion), calls=%async_computation.1 | async-start | bytes 393216 | tf_op jit(solution)/shard_map/all_to_all | solution.py:148
  527.8 6.0 %collective-permute-start.15 = (f32[1,6144]{1,0:T(1,128)S(1)}, f32[1,6144]{1,0:T(1,128)S(1)}, u32[]{:S(2)}, u32[]{:S(2)}) collective-permute-start(f32[1,6144]{1,0:T(1,128)S(1)} %get-tuple-element.46), channel_id=1, source_target_pairs={{1,0},{2,1},{3,2},{4,3},{5,4},{6,5},{7,6},{8,7},{9,8},{10,9},{11,1... | collective-permute-start | bytes 73736 | tf_op jit(solution)/shard_map/ppermute | solution.py:31
  529.7 9.4 %collective-permute-start.16 = (f32[1,6144]{1,0:T(1,128)S(1)}, f32[1,6144]{1,0:T(1,128)S(1)}, u32[]{:S(2)}, u32[]{:S(2)}) collective-permute-start(f32[1,6144]{1,0:T(1,128)S(1)} %get-tuple-element.47), channel_id=1, source_target_pairs={{0,1},{1,2},{2,3},{3,4},{4,5},{5,6},{6,7},{7,8},{8,9},{9,10},{10,1... | collective-permute-start | bytes 73736 | tf_op jit(solution)/shard_map/ppermute | solution.py:29
  540.2 6.0 %collective-permute-start.17 = (f32[1,6144]{1,0:T(1,128)S(1)}, f32[1,6144]{1,0:T(1,128)S(1)}, u32[]{:S(2)}, u32[]{:S(2)}) collective-permute-start(f32[1,6144]{1,0:T(1,128)S(1)} %get-tuple-element.42), channel_id=1, source_target_pairs={{1,0},{2,1},{3,2},{4,3},{5,4},{6,5},{7,6},{8,7},{9,8},{10,9},{11,1... | collective-permute-start | bytes 73736 | tf_op jit(solution)/shard_map/ppermute | solution.py:31
  542.2 9.4 %collective-permute-start.18 = (f32[1,6144]{1,0:T(1,128)S(1)}, f32[1,6144]{1,0:T(1,128)S(1)}, u32[]{:S(2)}, u32[]{:S(2)}) collective-permute-start(f32[1,6144]{1,0:T(1,128)S(1)} %get-tuple-element.43), channel_id=1, source_target_pairs={{0,1},{1,2},{2,3},{3,4},{4,5},{5,6},{6,7},{7,8},{8,9},{9,10},{10,1... | collective-permute-start | bytes 73736 | tf_op jit(solution)/shard_map/ppermute | solution.py:29
  (19 other events, 254.7 us)
where the time goes:
time: 568 us; the launch traced here: 561 us
  blocking collectives  202 us (36%)
  other arithmetic  175 us (31%)
  starting transfers between devices  85.3 us (15%)
  local copies, waits for them, and re-layouts  70.3 us (12%)
  waiting for transfers between devices  22.7 us (4%)
    psum x2, blocking collectives, squares(): return lax.psum(jnp.sum(vector * vector), ('ice', 'hyd'))  129 us
    another operation x4, other arithmetic, apply_operator(): return jnp.stack([first, second])  85.4 us
    psum x1, blocking collectives, body(): lax.psum(jnp.sum(direction * applied), ('ice', 'hyd'))  66.2 us
    ppermute x9, starting transfers between devices, with_halo(): lax.ppermute(head, axis, [((i + 1) % count, i) for i in range(ends)])  45.6 us
    mul x3, other arithmetic, one_component(): vertical_flux = upward * (center[1:] - center[:-1])  40.6 us
    concatenate x3, local copies, waits for them, and re-layouts, with_halo(): jnp.concatenate([lax.ppermute(tail, axis, [(i, (i + 1) % count) for i in...  35.1 us
    ppermute x9, starting transfers between devices, with_halo(): lax.ppermute(tail, axis, [(i, (i + 1) % count) for i in range(ends)])  28.1 us
    reduce_sum x2, other arithmetic, body(): jnp.sum(direction * applied)  13.2 us
  transfers between devices with their start and end apart: 21, of which 7 were waited for; matrix products, arithmetic and copies ran while one was open for 21% of the time, Pallas kernels for 0%

commit v1 on v0

v1 whole, which is shorter than its diff:
```python
import functools

import jax
import jax.numpy as jnp
from jax import lax
from jax.experimental import pallas as pl
from jax.experimental.pallas import tpu as pltpu
from jax.sharding import PartitionSpec as P

HYD_ITERS = 3
vertical_weight = 4.0
relax_weight = 0.1
melt_factor = 0.5
sheet_conduct = 2.0
channel_conduct = 1.5
storage = 1.0
bump_height = 0.3
time_step = 0.5
speed_floor = 0.25

AXES = ("ice", "hyd")
F32 = jnp.float32
LANES = 128
CHUNK = 512
FACTORS = ((4.0, 1.0), (1.0, 4.0))
FIELDS = 24
F0, FG, MASK = 20, 22, 23


def whole(space=pltpu.VMEM):
    return pl.BlockSpec(memory_space=space)


def shape_of(*dims):
    return jax.ShapeDtypeStruct(dims, F32)


def lane_index(rows, cols):
    return lax.broadcasted_iota(jnp.int32, (rows, cols), 1)


def row_index(rows, cols):
    return lax.broadcasted_iota(jnp.int32, (rows, cols), 0)


def east_of(value, right):
    cols = value.shape[1]
    joined = jnp.concatenate([value, right], axis=1)
    return pltpu.roll(joined, cols + LANES - 1, 1)[:, :cols]


def west_of(value, left):
    joined = jnp.concatenate([left, value], axis=1)
    return pltpu.roll(joined, 1, 1)[:, LANES:]


def south_of(value, below):
    rows, cols = value.shape
    return jnp.where(row_index(rows, cols) == rows - 1, below, pltpu.roll(value, rows - 1, 0))


def north_of(value, above):
    rows, cols = value.shape
    return jnp.where(row_index(rows, cols) == 0, above, pltpu.roll(value, 1, 0))


def root(weight):
    weight = weight.astype(F32)
    return weight * lax.rsqrt(weight)


def edge_kernel(half, visc, drive, mask, floating, friction, force, fric, message):
    layers, rows, cols = visc.shape
    cover = mask[...].astype(F32)
    grounded = cover * (1.0 - floating[...].astype(F32))
    fric[...] = friction[...] * grounded
    for comp in range(2):
        force[comp] = drive[comp] * cover
    left_half = half[0] == 0
    first = jnp.where(left_half, LANES - 2, 0)
    lane = lane_index(rows, LANES)
    keep = (lane >= first) & (lane < first + 2)

    def edge(read):
        return jnp.where(left_half, read(slice(cols - LANES, cols)), read(slice(0, LANES)))

    edge_cover = edge(lambda part: mask[:, part]).astype(F32)
    fields = [
        root(edge(lambda part, layer=layer: visc[layer, :, part].astype(F32))) * edge_cover
        for layer in range(layers)
    ]
    fields += [edge(lambda part, comp=comp: force[comp, :, part]) for comp in range(2)]
    fields += [edge(lambda part: fric[:, part]), edge_cover]
    total = jnp.zeros((rows, LANES), F32)
    for index, field in enumerate(fields):
        part = jnp.where(keep, field, 0.0)
        total += pltpu.roll(part, 2 * index, 1) if index else part
    message[...] = total


def root_kernel(visc, mask, force, fric, roots, lines):
    layers, rows, cols = visc.shape
    for start in range(0, cols, CHUNK):
        part = slice(start, start + CHUNK)
        cover = mask[:, part].astype(F32)

        def step(layer, carry, part=part, cover=cover):
            value = root(visc[layer, :, part]) * cover
            roots[layer, :, part] = value
            for slot, row in enumerate((0, 1, rows - 1)):
                lines[slot, pl.ds(layer, 1), part] = value[row : row + 1]
            return carry

        lax.fori_loop(0, layers, step, 0, unroll=2)
        for slot, row in enumerate((0, 1, rows - 1)):
            for comp in range(2):
                lines[slot, F0 + comp : F0 + comp + 1, part] = force[comp, row : row + 1, part]
            lines[slot, FG : FG + 1, part] = fric[row : row + 1, part]
            lines[slot, MASK : MASK + 1, part] = cover[row : row + 1]


def unpack_kernel(half, message, lines, block, to_south, to_north):
    rows = message.shape[0]
    cols = lines.shape[2]
    first = jnp.where(half[0] == 0, 0, LANES - 2)
    lane = lane_index(rows, LANES)
    keep = (lane >= first) & (lane < first + 2)
    packed = message[...]
    to_north[:, :, :cols] = lines[0:2]
    to_south[:, :cols] = lines[2]
    for index in range(FIELDS):
        part = pltpu.roll(packed, LANES - 2 * index, 1) if index else packed
        part = jnp.where(keep, part, 0.0)
        block[index] = part
        to_north[0, index : index + 1, cols:] = part[0:1]
        to_north[1, index : index + 1, cols:] = part[1:2]
        to_south[index : index + 1, cols:] = part[rows - 1 : rows]


def line_of(ref, layer, start, size):
    if size > LANES:
        return ref[pl.ds(layer, 1), start : start + size]
    return ref[pl.ds(layer, 1), start - LANES : start + size][:, LANES:]


def fold(value):
    total = None
    for row in range(0, value.shape[0], 8):
        for col in range(0, value.shape[1], LANES):
            part = value[row : row + 8, col : col + LANES]
            total = part if total is None else total + part
    return total


def relax(cover):
    return (1.0 - cover) + relax_weight * cover


def operator_kernel(
    roots, force, fric, mask, block, above, below, lines, image, sums, slopes, scaled, diag, line, edge
):
    layers, rows, cols = roots.shape
    chunks = [(start, CHUNK) for start in range(0, cols, CHUNK)]

    def columns(read_own, read_block, start, size):
        if start == cols:
            return read_block(), read_own(slice(cols - LANES, cols)), jnp.zeros((rows, LANES), F32)
        left = read_own(slice(start - LANES, start)) if start else read_block()
        stop = start + size
        right = read_own(slice(stop, stop + LANES)) if stop < cols else read_block()
        return read_own(slice(start, stop)), left, right

    squares = jnp.zeros((8, LANES), F32)
    for start, size in chunks + [(cols, LANES)]:
        part = slice(start, start + size)
        own = start < cols
        cover = mask[:, part].astype(F32) if own else block[MASK]
        drag = fric[:, part] if own else block[FG]
        plain = relax(cover)
        if own:
            diag[0, :, part] = plain
            diag[1, :, part] = plain + drag
        for comp, (col_factor, row_factor) in enumerate(FACTORS):
            here, left, right = columns(
                lambda cut, comp=comp: force[comp, :, cut], lambda comp=comp: block[F0 + comp], start, size
            )
            up = above[F0 + comp : F0 + comp + 1, part]
            down = below[0, F0 + comp : F0 + comp + 1, part]
            slopes[4 * comp, :, part] = col_factor * (here - east_of(here, right))
            slopes[4 * comp + 1, :, part] = col_factor * (here - west_of(here, left))
            slopes[4 * comp + 2, :, part] = row_factor * (here - south_of(here, down))
            slopes[4 * comp + 3, :, part] = row_factor * (here - north_of(here, up))
            scaled[0, comp, :, part] = plain * here
            scaled[1, comp, :, part] = (plain + drag) * here
            if own:
                squares += fold(here * here)

    for start, size in chunks:
        part = slice(start, start + size)
        stop = start + size
        before = slice(start - LANES, start) if start else slice(cols, cols + LANES)
        after = slice(stop, stop + LANES)
        here = below[0, 0:layers, part]
        east = here * east_of(here, below[0, 0:layers, after])
        west = here * west_of(here, below[0, 0:layers, before])
        south = here * below[1, 0:layers, part]
        north = here * lines[2, 0:layers, part]
        cover = below[0, MASK : MASK + 1, part]
        lowest = jnp.where(row_index(layers, size) == 0, below[0, FG : FG + 1, part], 0.0)
        full = relax(cover) + lowest
        for comp, (col_factor, row_factor) in enumerate(FACTORS):
            row = slice(F0 + comp, F0 + comp + 1)
            mid = below[0, row, part]
            line[comp, 0:layers, part] = full * mid + (
                col_factor
                * (
                    east * (mid - east_of(mid, below[0, row, after]))
                    + west * (mid - west_of(mid, below[0, row, before]))
                )
                + row_factor
                * (south * (mid - below[1, row, part]) + north * (mid - lines[2, row, part]))
            )

    def layer_step(layer, carry):
        kind = jnp.where(layer == 0, 1, 0)
        lower = jnp.maximum(layer - 1, 0)
        for start, size in chunks + [(cols, LANES)]:
            part = slice(start, start + size)
            here, left, right = columns(
                lambda cut: roots[layer, :, cut], lambda: block[layer], start, size
            )
            east = east_of(here, right)
            west = west_of(here, left)
            south = south_of(here, line_of(below.at[0], layer, start, size))
            north = north_of(here, line_of(above, layer, start, size))
            for comp in range(2):
                flux = (
                    east * slopes[4 * comp, :, part]
                    + west * slopes[4 * comp + 1, :, part]
                    + south * slopes[4 * comp + 2, :, part]
                    + north * slopes[4 * comp + 3, :, part]
                )
                value = scaled[kind, comp, :, part] + here * flux
                if start < cols:
                    image[comp, layer, :, part] = value
                else:
                    edge[comp] = value
        cross, square, energy = carry
        for start, size in chunks:
            part = slice(start, start + size)
            stop = start + size
            here = roots[layer, :, part]
            right = roots[layer, :, stop : stop + LANES] if stop < cols else block[layer]
            east = east_of(here, right)
            south = south_of(here, line_of(below.at[0], layer, start, size))
            beneath = roots[lower, :, part]
            to_east, to_south, to_lower, size_sq, product = 0.0, 0.0, 0.0, 0.0, 0.0
            for comp, (col_factor, row_factor) in enumerate(FACTORS):
                value = image[comp, layer, :, part]
                right = image[comp, layer, :, stop : stop + LANES] if stop < cols else edge[comp]
                step = value - east_of(value, right)
                step = step * step
                to_east += step if col_factor == 1.0 else col_factor * step
                step = value - south_of(value, line_of(line.at[comp], layer, start, size))
                step = step * step
                to_south += step if row_factor == 1.0 else row_factor * step
                step = value - image[comp, lower, :, part]
                to_lower += step * step
                size_sq += value * value
                product += value * force[comp, :, part]
            faces = here * (east * to_east + south * to_south + beneath * (vertical_weight * to_lower))
            cross += fold(product)
            square += fold(size_sq)
            energy += fold(faces + diag[kind, :, part] * size_sq)
        return cross, square, energy

    zero = jnp.zeros((8, LANES), F32)
    cross, square, energy = lax.fori_loop(0, layers, layer_step, (zero, zero, zero))
    lane = lane_index(8, LANES)
    packed = jnp.zeros((8, LANES), F32)
    for index, part in enumerate((layers * squares, cross, square, energy)):
        packed = jnp.where(lane == index, jnp.sum(part), packed)
    sums[...] = packed


def velocity_kernel(weights, force, image, out, staged, done):
    layers = image.shape[1]
    first, second = weights[0], weights[1]

    def copy(layer):
        return pltpu.make_async_copy(staged.at[:, layer], out.at[:, layer], done.at[layer])

    def step(layer, carry):
        for comp in range(2):
            staged[comp, layer] = first * force[comp] + second * image[comp, layer]
        copy(layer).start()
        return carry

    lax.fori_loop(0, layers, step, 0)

    def finish(layer, carry):
        copy(layer).wait()
        return carry

    lax.fori_loop(0, layers, finish, 0)


def call(kernel, out_shape, n_in, scratch=(), smem=(), out_space=pltpu.VMEM, **kwargs):
    outs = out_shape if isinstance(out_shape, (list, tuple)) else (out_shape,)
    specs = tuple(whole(out_space) for _ in outs)
    return pl.pallas_call(
        kernel,
        out_shape=out_shape,
        in_specs=[whole(pltpu.SMEM) if i in smem else whole() for i in range(n_in)],
        out_specs=specs if isinstance(out_shape, (list, tuple)) else specs[0],
        scratch_shapes=list(scratch),
        compiler_params=pltpu.CompilerParams(vmem_limit_bytes=48 << 20),
        **kwargs,
    )


def moved(value, axis, steps):
    count = lax.axis_size(axis)
    leading, last = (max(0, -steps), min(count, count - steps))
    return lax.ppermute(value, axis, [(source, source + steps) for source in range(leading, last)])


def with_rows(cells):
    return jnp.concatenate([moved(cells[-1:], AXES, 1), cells, moved(cells[:1], AXES, -1)], axis=0)


def sweep(padded, east_face, west_face, south_face, north_face, fixed_part, overburden, sheet_thick):
    current = padded[1:-1]
    right_value = jnp.pad(current[:, 1:], ((0, 0), (0, 1)))
    left_value = jnp.pad(current[:, :-1], ((0, 0), (1, 0)))
    gathered = (
        east_face * right_value
        + west_face * left_value
        + south_face * padded[2:]
        + north_face * padded[:-2]
    )
    conduct_sum = east_face + west_face + south_face + north_face
    creep_rate = sheet_thick * jnp.abs(overburden - current)
    return (fixed_part + creep_rate * overburden + gathered) / (storage + creep_rate + conduct_sum)


def body(
    viscosity,
    driving_stress,
    ice_mask,
    float_mask,
    friction,
    geothermal,
    potential_prev,
    overburden,
    sheet_thick,
    channel_east,
    channel_south,
    channel_area,
):
    layers, rows, cols = viscosity.shape
    half = lax.axis_index("hyd").astype(jnp.int32)[None]
    swap = [(0, 1), (1, 0)]
    force, fric, message = call(
        edge_kernel, [shape_of(2, rows, cols), shape_of(rows, cols), shape_of(rows, LANES)], 6, smem=(0,)
    )(half, viscosity, driving_stress, ice_mask, float_mask, friction)
    received = lax.ppermute(message, "hyd", swap)
    roots, lines = call(root_kernel, [shape_of(layers, rows, cols), shape_of(3, FIELDS, cols)], 4)(
        viscosity, ice_mask, force, fric
    )
    wide = cols + LANES
    block, to_south, to_north = call(
        unpack_kernel,
        [shape_of(FIELDS, rows, LANES), shape_of(FIELDS, wide), shape_of(2, FIELDS, wide)],
        3,
        smem=(0,),
    )(half, received, lines)
    above = moved(to_south, "ice", 1)
    below = moved(to_north, "ice", -1)
    image, sums = call(
        operator_kernel,
        [shape_of(2, layers, rows, cols), shape_of(8, LANES)],
        8,
        scratch=[
            pltpu.VMEM((8, rows, wide), F32),
            pltpu.VMEM((2, 2, rows, wide), F32),
            pltpu.VMEM((2, rows, cols), F32),
            pltpu.VMEM((2, FIELDS, cols), F32),
            pltpu.VMEM((2, rows, LANES), F32),
        ],
    )(roots, force, fric, ice_mask, block, above, below, lines)
    count = lax.axis_size("ice") * lax.axis_size("hyd")
    spread = jnp.broadcast_to(sums[0:1], (count, LANES))
    gathered = lax.all_to_all(spread, AXES, 0, 0, tiled=True)
    total = jnp.sum(gathered, axis=0)
    norm, cross, square, energy = total[0], total[1], total[2], total[3]
    step_one = norm / cross
    norm_next = step_one * (step_one * square - 2.0 * cross) + norm
    ratio = norm_next / norm
    lead = 1.0 + ratio
    curve = lead * lead * cross - 2.0 * lead * step_one * square + step_one * step_one * energy
    step_two = norm_next / curve
    weights = jnp.stack([step_one + step_two * lead, -step_two * step_one])
    velocity = pl.pallas_call(
        velocity_kernel,
        out_shape=shape_of(2, layers, rows, cols),
        in_specs=[whole(pltpu.SMEM), whole(), whole()],
        out_specs=whole(pl.ANY),
        scratch_shapes=[pltpu.VMEM((2, layers, rows, cols), F32), pltpu.SemaphoreType.DMA((layers,))],
        compiler_params=pltpu.CompilerParams(vmem_limit_bytes=48 << 20),
    )(weights, force, image)

    low = weights[0] * force + weights[1] * image[:, 0]
    slide_sq = low[0] * low[0] + low[1] * low[1]
    slide_speed = jnp.sqrt(slide_sq + speed_floor)
    melt_rate = melt_factor * (geothermal + fric * slide_sq)
    pair = jnp.stack([melt_rate, slide_speed])
    strip_rows = rows // 2
    is_left = half[0] == 0
    mine = jnp.where(is_left, pair[:, :strip_rows], pair[:, strip_rows:])
    theirs = jnp.where(is_left, pair[:, strip_rows:], pair[:, :strip_rows])
    theirs = lax.ppermute(theirs, "hyd", swap)
    strip = jnp.concatenate(
        [jnp.where(is_left, mine, theirs), jnp.where(is_left, theirs, mine)], axis=2
    )
    melt_strip, speed_strip = strip[0], strip[1]
    east_face = sheet_conduct * sheet_thick + channel_conduct * channel_east.astype(F32) * channel_area
    south_face = sheet_conduct * sheet_thick + channel_conduct * channel_south.astype(F32) * channel_area
    west_face = jnp.pad(east_face[:, :-1], ((0, 0), (1, 0)))
    north_face = jnp.concatenate([moved(south_face[-1:], AXES, 1), south_face[:-1]], axis=0)
    opening = speed_strip * jnp.maximum(bump_height - sheet_thick, 0.0)
    fixed_part = storage * potential_prev + melt_strip - opening
    potential = potential_prev
    for iteration in range(HYD_ITERS):
        potential = sweep(
            with_rows(potential),
            east_face,
            west_face,
            south_face,
            north_face,
            fixed_part,
            overburden,
            sheet_thick,
        )
    pressure = overburden - potential
    sheet_next = sheet_thick + time_step * (opening - sheet_thick * jnp.abs(pressure) * pressure)
    keep = jnp.where(is_left, pressure[:, :cols], pressure[:, cols:])
    give = jnp.where(is_left, pressure[:, cols:], pressure[:, :cols])
    got = lax.ppermute(give, "hyd", swap)
    effective = jnp.concatenate([jnp.where(is_left, keep, got), jnp.where(is_left, got, keep)], axis=0)
    return (velocity, effective, potential, sheet_next)


def solution(mesh):
    tiles = P("ice", "hyd")
    layered = P(None, "ice", "hyd")
    strips = P(("ice", "hyd"), None)
    return jax.shard_map(
        body,
        mesh=mesh,
        in_specs=(layered, layered, tiles, tiles, tiles, tiles) + (strips,) * 6,
        out_specs=(P(None, None, "ice", "hyd"), tiles, strips, strips),
        check_vma=False,
    )
```

time: 568 us -> 119 us (0.21)
  the two profiles are of different devices: /device:TPU:16 before, /device:TPU:103 now
where the time goes in v1:
time: 119 us; the launch traced here: 118 us
  starting transfers between devices  54.9 us (46%)
  Pallas kernels  27.1 us (23%)
  waiting for transfers between devices  14.8 us (12%)
  local copies, waits for them, and re-layouts  9.51 us (8%)
  between operations  6.89 us (6%)
  other arithmetic  5.08 us (4%)
    ppermute x9, starting transfers between devices, moved(): lax.ppermute(value, axis, [(source, source + steps) for source in range(l...  33.1 us
    pallas_call x1, Pallas kernels, body(): call(operator_kernel, [shape_of(2, layers, rows, cols), shape_of(8, LANES...  16.7 us
    ppermute x9, waiting for transfers between devices, moved(): lax.ppermute(value, axis, [(source, source + steps) for source in range(l...  11.8 us
    all_to_all x1, starting transfers between devices, body(): gathered = lax.all_to_all(spread, AXES, 0, 0, tiled=True)  8.41 us
    unnamed x24, local copies, waits for them, and re-layouts  7.8 us
    pallas_call x1, Pallas kernels, body(): pl.pallas_call(velocity_kernel, out_shape=shape_of(2, layers, rows, cols)...  6.57 us
    ppermute x1, starting transfers between devices, body(): got = lax.ppermute(give, 'hyd', swap)  6.33 us
    ppermute x1, starting transfers between devices, body(): theirs = lax.ppermute(theirs, 'hyd', swap)  5.76 us
  transfers between devices with their start and end apart: 13, of which 5 were waited for; matrix products, arithmetic and copies ran while one was open for 4% of the time, Pallas kernels for 23%

profile of v1, /device:TPU:103, one launch (start us, length us, event | category | flops | bytes accessed | tf_op | source)
XLA Modules:
  0.0 118.3 jit_solution(9575126625380156517)
XLA Ops:
  0.6 1.5 %copy-done = bf16[20,16,3072]{2,1,0:T(8,128)(2,1)S(1)} copy-done((bf16[20,16,3072]{2,1,0:T(8,128)(2,1)S(1)}, bf16[20,16,3072]{2,1,0:T(8,128)(2,1)}, u32[]{:S(2)}) %copy-start) | copy-done | bytes 1966104
  6.2 1.3 %collective-permute-start = (f32[16,128]{1,0:T(8,128)S(1)}, f32[16,128]{1,0:T(8,128)S(1)}, u32[]{:S(2)}, u32[]{:S(2)}) collective-permute-start(f32[16,128]{1,0:T(8,128)S(1)} %get-tuple-element.17), channel_id=1, source_target_pairs={{0,1},{1,0},{2,3},{3,2},{4,5},{5,4},{6,7},{7,6},{8,9},{9,8},{10,11... | collective-permute-start | bytes 24584 | tf_op jit(solution)/shard_map/ppermute | solution.py:367
  7.5 1.5 %copy-done.1 = bf16[20,16,3072]{2,1,0:T(8,128)(2,1)S(1)} copy-done((bf16[20,16,3072]{2,1,0:T(8,128)(2,1)S(1)}, bf16[20,16,3072]{2,1,0:T(8,128)(2,1)}, u32[]{:S(2)}) %copy-start.1) | copy-done | bytes 1966104
  10.0 3.5 %shard_map.148 = (f32[20,16,3072]{2,1,0:T(8,128)}, f32[3,24,3072]{2,1,0:T(8,128)S(1)}) custom-call(bf16[20,16,3072]{2,1,0:T(8,128)(2,1)S(1)} %copy-done.1, s32[16,3072]{1,0:T(8,128)S(1)} %copy-done.3, f32[2,16,3072]{2,1,0:T(8,128)S(1)} %get-tuple-element.14.force, f32[16,3072]{1,0:T(8,128)S(1)} %get-tuple-element.15.fric), custom_call_target="tpu_custom_call" | custom-call | tf_op jit(solution)/shard_map/pallas_call | solution.py:368
  13.6 3.0 %collective-permute-start.2 = (f32[2,24,3200]{2,1,0:T(8,128)S(1)}, f32[2,24,3200]{2,1,0:T(8,128)S(1)}, u32[]{:S(2)}, u32[]{:S(2)}) collective-permute-start(f32[2,24,3200]{2,1,0:T(8,128)S(1)} %get-tuple-element.21), channel_id=1, source_target_pairs={{2,0},{4,2},{6,4},{8,6},{10,8},{12,10},{14,12},{16,14},{18,16},{20... | collective-permute-start | bytes 1843208 | tf_op jit(solution)/shard_map/ppermute | solution.py:325
  16.6 8.4 %collective-permute-start.1 = (f32[24,3200]{1,0:T(8,128)S(1)}, f32[24,3200]{1,0:T(8,128)S(1)}, u32[]{:S(2)}, u32[]{:S(2)}) collective-permute-start(f32[24,3200]{1,0:T(8,128)S(1)} %get-tuple-element.20), channel_id=1, source_target_pairs={{0,2},{2,4},{4,6},{6,8},{8,10},{10,12},{12,14},{14,16},{16,18},{18... | collective-permute-start | bytes 921608 | tf_op jit(solution)/shard_map/ppermute | solution.py:325
  25.1 1.3 %multiply_add_fusion.2 = (f32[8,6144]{1,0:T(8,128)S(1)}, f32[8,6144]{1,0:T(8,128)S(1)}) fusion(f32[8,6144]{1,0:T(8,128)} %param.23, s32[8,6144]{1,0:T(8,128)} %param.21, f32[8,6144]{1,0:T(8,128)} %param.20, s32[8,6144]{1,0:T(8,128)} %param.22), kind=kLoop, calls=%fused_computation.50 | loop fusion | flops 442368 | bytes 1179648 | tf_op jit(solution)/shard_map/add | solution.py:427
  26.4 2.1 %collective-permute-start.5 = (f32[1,6144]{1,0:T(1,128)S(1)}, f32[1,6144]{1,0:T(1,128)S(1)}, u32[]{:S(2)}, u32[]{:S(2)}) collective-permute-start(f32[1,6144]{1,0:T(1,128)S(1)} %slice.162), channel_id=1, source_target_pairs={{0,1},{1,2},{2,3},{3,4},{4,5},{5,6},{6,7},{7,8},{8,9},{9,10},{10,1... | collective-permute-start | bytes 73736 | tf_op jit(solution)/shard_map/ppermute | solution.py:325
  28.8 2.2 %collective-permute-done.2.below = f32[2,24,3200]{2,1,0:T(8,128)S(1)} collective-permute-done((f32[2,24,3200]{2,1,0:T(8,128)S(1)}, f32[2,24,3200]{2,1,0:T(8,128)S(1)}, u32[]{:S(2)}, u32[]{:S(2)}) %collective-permute-start.2) | collective-permute-done | bytes 614432 | tf_op jit(solution)/shard_map/ppermute | solution.py:325
  31.1 16.7 %shard_map.150 = (f32[2,20,16,3072]{3,2,1,0:T(8,128)}, f32[8,128]{1,0:T(8,128)S(1)}) custom-call(f32[20,16,3072]{2,1,0:T(8,128)} %get-tuple-element.16.roots, f32[2,16,3072]{2,1,0:T(8,128)S(1)} %get-tuple-element.14.force, f32[16,3072]{1,0:T(8,128)S(1)} %get-tuple-element.15.fric, s32[16,3072]{1,0:T(8,128)S(1)} %copy-done.4, ...), custom_call_target="tpu_custom_call" | custom-call | tf_op jit(solution)/shard_map/pallas_call | solution.py:380
  48.5 8.4 %all-to-all-start = ((f32[128,1,128]{2,1,0:T(1,128)}), f32[128,1,128]{2,1,0:T(1,128)S(1)}, u32[]{:S(2)}, u32[]{:S(2)}) async-start(f32[128,1,128]{2,1,0:T(1,128)} %broadcast_in_dim.9), calls=%async_computation | async-start | bytes 131072 | tf_op jit(solution)/shard_map/all_to_all | solution.py:394
  56.9 3.4 %collective-permute-start.4 = (f32[1,6144]{1,0:T(1,128)S(1)}, f32[1,6144]{1,0:T(1,128)S(1)}, u32[]{:S(2)}, u32[]{:S(2)}) collective-permute-start(f32[1,6144]{1,0:T(1,128)S(1)} %get-tuple-element.45), channel_id=1, source_target_pairs={{1,0},{2,1},{3,2},{4,3},{5,4},{6,5},{7,6},{8,7},{9,8},{10,9},{11,1... | collective-permute-start | bytes 73736 | tf_op jit(solution)/shard_map/ppermute | solution.py:325
  60.4 1.9 %collective-permute-start.6 = (f32[1,6144]{1,0:T(1,128)S(1)}, f32[1,6144]{1,0:T(1,128)S(1)}, u32[]{:S(2)}, u32[]{:S(2)}) collective-permute-start(f32[1,6144]{1,0:T(1,128)S(1)} %get-tuple-element.46), channel_id=1, source_target_pairs={{0,1},{1,2},{2,3},{3,4},{4,5},{5,6},{6,7},{7,8},{8,9},{9,10},{10,1... | collective-permute-start | bytes 73736 | tf_op jit(solution)/shard_map/ppermute | solution.py:325
  70.1 5.8 %collective-permute-start.3 = (f32[2,8,3072]{2,1,0:T(8,128)S(1)}, f32[2,8,3072]{2,1,0:T(8,128)S(1)}, u32[]{:S(2)}, u32[]{:S(2)}) collective-permute-start(f32[2,8,3072]{2,1,0:T(8,128)S(1)} %broadcast_select_fusion.2), channel_id=1, source_target_pairs={{0,1},{1,0},{2,3},{3,2},{4,5},{5,4},{6,7},{7,6},{8,9},{9,8},{10,11... | collective-permute-start | bytes 589832 | tf_op jit(solution)/shard_map/ppermute | solution.py:422
  76.0 2.9 %collective-permute-done.3 = f32[2,8,3072]{2,1,0:T(8,128)S(1)} collective-permute-done((f32[2,8,3072]{2,1,0:T(8,128)S(1)}, f32[2,8,3072]{2,1,0:T(8,128)S(1)}, u32[]{:S(2)}, u32[]{:S(2)}) %collective-permute-start.3) | collective-permute-done | bytes 196640 | tf_op jit(solution)/shard_map/ppermute | solution.py:422
  79.4 1.9 %collective-permute-start.7 = (f32[1,6144]{1,0:T(1,128)S(1)}, f32[1,6144]{1,0:T(1,128)S(1)}, u32[]{:S(2)}, u32[]{:S(2)}) collective-permute-start(f32[1,6144]{1,0:T(1,128)S(1)} %get-tuple-element.41), channel_id=1, source_target_pairs={{1,0},{2,1},{3,2},{4,3},{5,4},{6,5},{7,6},{8,7},{9,8},{10,9},{11,1... | collective-permute-start | bytes 73736 | tf_op jit(solution)/shard_map/ppermute | solution.py:325
  81.3 3.4 %collective-permute-start.8 = (f32[1,6144]{1,0:T(1,128)S(1)}, f32[1,6144]{1,0:T(1,128)S(1)}, u32[]{:S(2)}, u32[]{:S(2)}) collective-permute-start(f32[1,6144]{1,0:T(1,128)S(1)} %get-tuple-element.42), channel_id=1, source_target_pairs={{0,1},{1,2},{2,3},{3,4},{4,5},{5,6},{6,7},{7,8},{8,9},{9,10},{10,1... | collective-permute-start | bytes 73736 | tf_op jit(solution)/shard_map/ppermute | solution.py:325
  84.8 1.6 %collective-permute-done.8 = f32[1,6144]{1,0:T(1,128)S(1)} collective-permute-done((f32[1,6144]{1,0:T(1,128)S(1)}, f32[1,6144]{1,0:T(1,128)S(1)}, u32[]{:S(2)}, u32[]{:S(2)}) %collective-permute-start.8) | collective-permute-done | bytes 24608 | tf_op jit(solution)/shard_map/ppermute | solution.py:325
  86.8 7.0 %collective-permute-start.10 = (f32[1,6144]{1,0:T(1,128)S(1)}, f32[1,6144]{1,0:T(1,128)S(1)}, u32[]{:S(2)}, u32[]{:S(2)}) collective-permute-start(f32[1,6144]{1,0:T(1,128)S(1)} %get-tuple-element.38), channel_id=1, source_target_pairs={{0,1},{1,2},{2,3},{3,4},{4,5},{5,6},{6,7},{7,8},{8,9},{9,10},{10,1... | collective-permute-start | bytes 73736 | tf_op jit(solution)/shard_map/ppermute | solution.py:325
  93.8 1.9 %collective-permute-start.9 = (f32[1,6144]{1,0:T(1,128)S(1)}, f32[1,6144]{1,0:T(1,128)S(1)}, u32[]{:S(2)}, u32[]{:S(2)}) collective-permute-start(f32[1,6144]{1,0:T(1,128)S(1)} %get-tuple-element.37), channel_id=1, source_target_pairs={{1,0},{2,1},{3,2},{4,3},{5,4},{6,5},{7,6},{8,7},{9,8},{10,9},{11,1... | collective-permute-start | bytes 73736 | tf_op jit(solution)/shard_map/ppermute | solution.py:325
  95.9 7.6 %collective-permute-done.9 = f32[1,6144]{1,0:T(1,128)S(1)} collective-permute-done((f32[1,6144]{1,0:T(1,128)S(1)}, f32[1,6144]{1,0:T(1,128)S(1)}, u32[]{:S(2)}, u32[]{:S(2)}) %collective-permute-start.9) | collective-permute-done | bytes 24608 | tf_op jit(solution)/shard_map/ppermute | solution.py:325
  103.5 1.1 multiply_add_fusion
  104.6 6.3 %collective-permute-start.11 = (f32[8,3072]{1,0:T(8,128)S(1)}, f32[8,3072]{1,0:T(8,128)S(1)}, u32[]{:S(2)}, u32[]{:S(2)}) collective-permute-start(f32[8,3072]{1,0:T(8,128)S(1)} %slice_select_fusion), channel_id=1, source_target_pairs={{0,1},{1,0},{2,3},{3,2},{4,5},{5,4},{6,7},{7,6},{8,9},{9,8},{10,11... | collective-permute-start | bytes 294920 | tf_op jit(solution)/shard_map/ppermute | solution.py:449
  111.0 6.6 %shard_map.151 = f32[2,20,16,3072]{3,2,1,0:T(8,128)} custom-call(f32[2]{0:T(128)S(1)} %pad_maximum_fusion.10.weights, f32[2,16,3072]{2,1,0:T(8,128)S(1)} %get-tuple-element.14.force, f32[2,20,16,3072]{3,2,1,0:T(8,128)} %get-tuple-element.23.image), custom_call_target="tpu_custom_call" | custom-call | tf_op jit(solution)/shard_map/pallas_call | solution.py:404
  (55 shorter events, 9.8 us)
Async XLA Ops:
  0.6 1.5 %copy-start = (bf16[20,16,3072]{2,1,0:T(8,128)(2,1)S(1)}, bf16[20,16,3072]{2,1,0:T(8,128)(2,1)}, u32[]{:S(2)}) copy-start(bf16[20,16,3072]{2,1,0:T(8,128)(2,1)} %visc.3) | copy-start | bytes 5898244
  2.2 0.9 copy-start.2
  3.1 1.0 copy-start.5
  4.1 0.9 copy-start.6
  5.0 0.9 copy-start.7
  6.0 25.1 %copy-start.4 = (s32[16,3072]{1,0:T(8,128)S(1)}, s32[16,3072]{1,0:T(8,128)}, u32[]{:S(2)}) copy-start(s32[16,3072]{1,0:T(8,128)} %mask.5) | copy-start | bytes 589828
  6.0 50.9 %copy-start.9 = (f32[8,6144]{1,0:T(8,128)S(1)}, f32[8,6144]{1,0:T(8,128)}, u32[]{:S(2)}) copy-start(f32[8,6144]{1,0:T(8,128)} %param.18) | copy-start | bytes 589828
  6.0 64.1 %copy-start.11 = (f32[16,3072]{1,0:T(8,128)S(1)}, f32[16,3072]{1,0:T(8,128)}, u32[]{:S(2)}) copy-start(f32[16,3072]{1,0:T(8,128)} %param.17) | copy-start | bytes 589828
  6.2 7.3 %collective-permute-start = (f32[16,128]{1,0:T(8,128)S(1)}, f32[16,128]{1,0:T(8,128)S(1)}, u32[]{:S(2)}, u32[]{:S(2)}) collective-permute-start(f32[16,128]{1,0:T(8,128)S(1)} %get-tuple-element.17), channel_id=1, source_target_pairs={{0,1},{1,0},{2,3},{3,2},{4,5},{5,4},{6,7},{7,6},{8,9},{9,8},{10,11... | collective-permute-start | bytes 24584 | tf_op jit(solution)/shard_map/ppermute | solution.py:367
  7.5 1.5 %copy-start.1 = (bf16[20,16,3072]{2,1,0:T(8,128)(2,1)S(1)}, bf16[20,16,3072]{2,1,0:T(8,128)(2,1)}, u32[]{:S(2)}) copy-start(bf16[20,16,3072]{2,1,0:T(8,128)(2,1)} %visc.3) | copy-start | bytes 5898244
  13.5 65.5 %copy-start.8 = (f32[8,6144]{1,0:T(8,128)S(1)}, f32[8,6144]{1,0:T(8,128)}, u32[]{:S(2)}) copy-start(f32[8,6144]{1,0:T(8,128)} %param.20) | copy-start | bytes 589828
  13.5 65.5 %copy-start.10 = (f32[8,6144]{1,0:T(8,128)S(1)}, f32[8,6144]{1,0:T(8,128)}, u32[]{:S(2)}) copy-start(f32[8,6144]{1,0:T(8,128)} %param.19) | copy-start | bytes 589828
  13.6 17.4 %collective-permute-start.2 = (f32[2,24,3200]{2,1,0:T(8,128)S(1)}, f32[2,24,3200]{2,1,0:T(8,128)S(1)}, u32[]{:S(2)}, u32[]{:S(2)}) collective-permute-start(f32[2,24,3200]{2,1,0:T(8,128)S(1)} %get-tuple-element.21), channel_id=1, source_target_pairs={{2,0},{4,2},{6,4},{8,6},{10,8},{12,10},{14,12},{16,14},{18,16},{20... | collective-permute-start | bytes 1843208 | tf_op jit(solution)/shard_map/ppermute | solution.py:325
  16.6 12.2 %collective-permute-start.1 = (f32[24,3200]{1,0:T(8,128)S(1)}, f32[24,3200]{1,0:T(8,128)S(1)}, u32[]{:S(2)}, u32[]{:S(2)}) collective-permute-start(f32[24,3200]{1,0:T(8,128)S(1)} %get-tuple-element.20), channel_id=1, source_target_pairs={{0,2},{2,4},{4,6},{6,8},{8,10},{10,12},{12,14},{14,16},{16,18},{18... | collective-permute-start | bytes 921608 | tf_op jit(solution)/shard_map/ppermute | solution.py:325
  26.4 52.6 %collective-permute-start.5 = (f32[1,6144]{1,0:T(1,128)S(1)}, f32[1,6144]{1,0:T(1,128)S(1)}, u32[]{:S(2)}, u32[]{:S(2)}) collective-permute-start(f32[1,6144]{1,0:T(1,128)S(1)} %slice.162), channel_id=1, source_target_pairs={{0,1},{1,2},{2,3},{3,4},{4,5},{5,6},{6,7},{7,8},{8,9},{9,10},{10,1... | collective-permute-start | bytes 73736 | tf_op jit(solution)/shard_map/ppermute | solution.py:325
  48.5 13.8 %all-to-all-start = ((f32[128,1,128]{2,1,0:T(1,128)}), f32[128,1,128]{2,1,0:T(1,128)S(1)}, u32[]{:S(2)}, u32[]{:S(2)}) async-start(f32[128,1,128]{2,1,0:T(1,128)} %broadcast_in_dim.9), calls=%async_computation | async-start | bytes 131072 | tf_op jit(solution)/shard_map/all_to_all | solution.py:394
  56.9 22.1 %collective-permute-start.4 = (f32[1,6144]{1,0:T(1,128)S(1)}, f32[1,6144]{1,0:T(1,128)S(1)}, u32[]{:S(2)}, u32[]{:S(2)}) collective-permute-start(f32[1,6144]{1,0:T(1,128)S(1)} %get-tuple-element.45), channel_id=1, source_target_pairs={{1,0},{2,1},{3,2},{4,3},{5,4},{6,5},{7,6},{8,7},{9,8},{10,9},{11,1... | collective-permute-start | bytes 73736 | tf_op jit(solution)/shard_map/ppermute | solution.py:325
  60.4 18.6 %collective-permute-start.6 = (f32[1,6144]{1,0:T(1,128)S(1)}, f32[1,6144]{1,0:T(1,128)S(1)}, u32[]{:S(2)}, u32[]{:S(2)}) collective-permute-start(f32[1,6144]{1,0:T(1,128)S(1)} %get-tuple-element.46), channel_id=1, source_target_pairs={{0,1},{1,2},{2,3},{3,4},{4,5},{5,6},{6,7},{7,8},{8,9},{9,10},{10,1... | collective-permute-start | bytes 73736 | tf_op jit(solution)/shard_map/ppermute | solution.py:325
  70.1 8.8 %collective-permute-start.3 = (f32[2,8,3072]{2,1,0:T(8,128)S(1)}, f32[2,8,3072]{2,1,0:T(8,128)S(1)}, u32[]{:S(2)}, u32[]{:S(2)}) collective-permute-start(f32[2,8,3072]{2,1,0:T(8,128)S(1)} %broadcast_select_fusion.2), channel_id=1, source_target_pairs={{0,1},{1,0},{2,3},{3,2},{4,5},{5,4},{6,7},{7,6},{8,9},{9,8},{10,11... | collective-permute-start | bytes 589832 | tf_op jit(solution)/shard_map/ppermute | solution.py:422
  79.4 5.4 %collective-permute-start.7 = (f32[1,6144]{1,0:T(1,128)S(1)}, f32[1,6144]{1,0:T(1,128)S(1)}, u32[]{:S(2)}, u32[]{:S(2)}) collective-permute-start(f32[1,6144]{1,0:T(1,128)S(1)} %get-tuple-element.41), channel_id=1, source_target_pairs={{1,0},{2,1},{3,2},{4,3},{5,4},{6,5},{7,6},{8,7},{9,8},{10,9},{11,1... | collective-permute-start | bytes 73736 | tf_op jit(solution)/shard_map/ppermute | solution.py:325
  81.3 5.1 %collective-permute-start.8 = (f32[1,6144]{1,0:T(1,128)S(1)}, f32[1,6144]{1,0:T(1,128)S(1)}, u32[]{:S(2)}, u32[]{:S(2)}) collective-permute-start(f32[1,6144]{1,0:T(1,128)S(1)} %get-tuple-element.42), channel_id=1, source_target_pairs={{0,1},{1,2},{2,3},{3,4},{4,5},{5,6},{6,7},{7,8},{8,9},{9,10},{10,1... | collective-permute-start | bytes 73736 | tf_op jit(solution)/shard_map/ppermute | solution.py:325
  86.8 9.1 %collective-permute-start.10 = (f32[1,6144]{1,0:T(1,128)S(1)}, f32[1,6144]{1,0:T(1,128)S(1)}, u32[]{:S(2)}, u32[]{:S(2)}) collective-permute-start(f32[1,6144]{1,0:T(1,128)S(1)} %get-tuple-element.38), channel_id=1, source_target_pairs={{0,1},{1,2},{2,3},{3,4},{4,5},{5,6},{6,7},{7,8},{8,9},{9,10},{10,1... | collective-permute-start | bytes 73736 | tf_op jit(solution)/shard_map/ppermute | solution.py:325
  93.8 9.6 %collective-permute-start.9 = (f32[1,6144]{1,0:T(1,128)S(1)}, f32[1,6144]{1,0:T(1,128)S(1)}, u32[]{:S(2)}, u32[]{:S(2)}) collective-permute-start(f32[1,6144]{1,0:T(1,128)S(1)} %get-tuple-element.37), channel_id=1, source_target_pairs={{1,0},{2,1},{3,2},{4,3},{5,4},{6,5},{7,6},{8,7},{9,8},{10,9},{11,1... | collective-permute-start | bytes 73736 | tf_op jit(solution)/shard_map/ppermute | solution.py:325
  104.6 13.0 %collective-permute-start.11 = (f32[8,3072]{1,0:T(8,128)S(1)}, f32[8,3072]{1,0:T(8,128)S(1)}, u32[]{:S(2)}, u32[]{:S(2)}) collective-permute-start(f32[8,3072]{1,0:T(8,128)S(1)} %slice_select_fusion), channel_id=1, source_target_pairs={{0,1},{1,0},{2,3},{3,2},{4,5},{5,4},{6,7},{7,6},{8,9},{9,8},{10,11... | collective-permute-start | bytes 294920 | tf_op jit(solution)/shard_map/ppermute | solution.py:449
  (1 other events, 0.9 us)

commit v2 on v1

v2 whole, which is shorter than its diff:
```python
import functools

import jax
import jax.numpy as jnp
from jax import lax
from jax.experimental import pallas as pl
from jax.experimental.pallas import tpu as pltpu
from jax.sharding import PartitionSpec as P

HYD_ITERS = 3
vertical_weight = 4.0
relax_weight = 0.1
melt_factor = 0.5
sheet_conduct = 2.0
channel_conduct = 1.5
storage = 1.0
bump_height = 0.3
time_step = 0.5
speed_floor = 0.25

AXES = ("ice", "hyd")
F32 = jnp.float32
LANES = 128
CHUNK = 512
FETCH = 1536
FACTORS = ((4.0, 1.0), (1.0, 4.0))
FIELDS = 24
F0, FG, MASK = 20, 22, 23


def whole(space=pltpu.VMEM):
    return pl.BlockSpec(memory_space=space)


def shape_of(*dims):
    return jax.ShapeDtypeStruct(dims, F32)


def lane_index(rows, cols):
    return lax.broadcasted_iota(jnp.int32, (rows, cols), 1)


def row_index(rows, cols):
    return lax.broadcasted_iota(jnp.int32, (rows, cols), 0)


def east_of(value, right):
    cols = value.shape[1]
    joined = jnp.concatenate([value, right], axis=1)
    return pltpu.roll(joined, cols + LANES - 1, 1)[:, :cols]


def west_of(value, left):
    joined = jnp.concatenate([left, value], axis=1)
    return pltpu.roll(joined, 1, 1)[:, LANES:]


def south_of(value, below):
    rows, cols = value.shape
    return jnp.where(row_index(rows, cols) == rows - 1, below, pltpu.roll(value, rows - 1, 0))


def north_of(value, above):
    rows, cols = value.shape
    return jnp.where(row_index(rows, cols) == 0, above, pltpu.roll(value, 1, 0))


def root(weight):
    weight = weight.astype(F32)
    return weight * lax.rsqrt(weight)


def edge_kernel(half, visc, drive, mask, floating, friction, message, w, d, m, fl, fr, done):
    layers, rows, cols = visc.shape
    left_half = half[0] == 0
    start = pl.multiple_of(jnp.where(left_half, cols - LANES, 0), LANES)
    cut = pl.ds(start, LANES)
    copies = [
        pltpu.make_async_copy(source.at[..., cut], target, done.at[index])
        for index, (source, target) in enumerate(
            ((visc, w), (drive, d), (mask, m), (floating, fl), (friction, fr))
        )
    ]
    for copy in copies:
        copy.start()
    for copy in copies:
        copy.wait()
    first = jnp.where(left_half, LANES - 2, 0)
    lane = lane_index(rows, LANES)
    keep = (lane >= first) & (lane < first + 2)
    cover = m[...].astype(F32)
    fields = [root(w[layer]) * cover for layer in range(layers)]
    fields += [d[comp] * cover for comp in range(2)]
    fields += [fr[...] * (cover * (1.0 - fl[...].astype(F32))), cover]
    total = jnp.zeros((rows, LANES), F32)
    for index, field in enumerate(fields):
        part = jnp.where(keep, field, 0.0)
        total += pltpu.roll(part, 2 * index, 1) if index else part
    message[...] = total


def root_kernel(
    visc, drive, mask, floating, friction, roots, lines, force, fric, covers, w, d, m, fl, fr, done
):
    layers, rows, cols = visc.shape
    starts = list(range(0, cols, FETCH))

    def copies(index):
        part = slice(starts[index], starts[index] + FETCH)
        return [
            pltpu.make_async_copy(source.at[..., part], target.at[..., part], done.at[index, slot])
            for slot, (source, target) in enumerate(
                ((visc, w), (drive, d), (mask, m), (floating, fl), (friction, fr))
            )
        ]

    for index in range(len(starts)):
        for copy in copies(index):
            copy.start()
    for index, begin in enumerate(starts):
        for copy in copies(index):
            copy.wait()
        for start in range(begin, begin + FETCH, CHUNK):
            part = slice(start, start + CHUNK)
            cover = m[:, part].astype(F32)
            grounded = cover * (1.0 - fl[:, part].astype(F32))
            drag = fr[:, part] * grounded
            fric[:, part] = drag
            covers[:, part] = cover
            pushes = [d[comp, :, part] * cover for comp in range(2)]
            for comp in range(2):
                force[comp, :, part] = pushes[comp]

            def step(layer, carry, part=part, cover=cover):
                value = root(w[layer, :, part]) * cover
                roots[layer, :, part] = value
                for slot, row in enumerate((0, 1, rows - 1)):
                    lines[slot, pl.ds(layer, 1), part] = value[row : row + 1]
                return carry

            lax.fori_loop(0, layers, step, 0, unroll=2)
            for slot, row in enumerate((0, 1, rows - 1)):
                for comp in range(2):
                    lines[slot, F0 + comp : F0 + comp + 1, part] = pushes[comp][row : row + 1]
                lines[slot, FG : FG + 1, part] = drag[row : row + 1]
                lines[slot, MASK : MASK + 1, part] = cover[row : row + 1]


def unpack_kernel(half, message, lines, fringe, block, to_south, to_north):
    rows = message.shape[0]
    cols = lines.shape[2]
    first = jnp.where(half[0] == 0, 0, LANES - 2)
    lane = lane_index(rows, LANES)
    keep = (lane >= first) & (lane < first + 2)
    packed = message[...]
    to_north[0:FIELDS, :cols] = lines[0]
    to_north[FIELDS : 2 * FIELDS, :cols] = lines[1]
    to_north[2 * FIELDS :, :cols] = fringe[0]
    to_south[0:FIELDS, :cols] = lines[2]
    to_south[FIELDS:, :cols] = fringe[1]
    to_north[2 * FIELDS :, cols:] = jnp.zeros((16, LANES), F32)
    to_south[FIELDS:, cols:] = jnp.zeros((16, LANES), F32)
    for index in range(FIELDS):
        part = pltpu.roll(packed, LANES - 2 * index, 1) if index else packed
        part = jnp.where(keep, part, 0.0)
        block[index] = part
        to_north[index : index + 1, cols:] = part[0:1]
        to_north[FIELDS + index : FIELDS + index + 1, cols:] = part[1:2]
        to_south[index : index + 1, cols:] = part[rows - 1 : rows]


def line_of(ref, layer, start, size):
    if size > LANES:
        return ref[pl.ds(layer, 1), start : start + size]
    return ref[pl.ds(layer, 1), start - LANES : start + size][:, LANES:]


def fold(value):
    total = None
    for row in range(0, value.shape[0], 8):
        for col in range(0, value.shape[1], LANES):
            part = value[row : row + 8, col : col + LANES]
            total = part if total is None else total + part
    return total


def relax(cover):
    return (1.0 - cover) + relax_weight * cover


def operator_kernel(
    roots, force, fric, mask, block, above, below, lines, image, sums, slopes, scaled, diag, line, edge
):
    layers, rows, cols = roots.shape
    chunks = [(start, CHUNK) for start in range(0, cols, CHUNK)]

    def columns(read_own, read_block, start, size):
        if start == cols:
            return read_block(), read_own(slice(cols - LANES, cols)), jnp.zeros((rows, LANES), F32)
        left = read_own(slice(start - LANES, start)) if start else read_block()
        stop = start + size
        right = read_own(slice(stop, stop + LANES)) if stop < cols else read_block()
        return read_own(slice(start, stop)), left, right

    squares = jnp.zeros((8, LANES), F32)
    for start, size in chunks + [(cols, LANES)]:
        part = slice(start, start + size)
        own = start < cols
        cover = mask[:, part] if own else block[MASK]
        drag = fric[:, part] if own else block[FG]
        plain = relax(cover)
        if own:
            diag[0, :, part] = plain
            diag[1, :, part] = plain + drag
        for comp, (col_factor, row_factor) in enumerate(FACTORS):
            here, left, right = columns(
                lambda cut, comp=comp: force[comp, :, cut], lambda comp=comp: block[F0 + comp], start, size
            )
            up = above[F0 + comp : F0 + comp + 1, part]
            down = below[F0 + comp : F0 + comp + 1, part]
            slopes[4 * comp, :, part] = col_factor * (here - east_of(here, right))
            slopes[4 * comp + 1, :, part] = col_factor * (here - west_of(here, left))
            slopes[4 * comp + 2, :, part] = row_factor * (here - south_of(here, down))
            slopes[4 * comp + 3, :, part] = row_factor * (here - north_of(here, up))
            scaled[0, comp, :, part] = plain * here
            scaled[1, comp, :, part] = (plain + drag) * here
            if own:
                squares += fold(here * here)

    for start, size in chunks:
        part = slice(start, start + size)
        stop = start + size
        before = slice(start - LANES, start) if start else slice(cols, cols + LANES)
        after = slice(stop, stop + LANES)
        here = below[0:layers, part]
        east = here * east_of(here, below[0:layers, after])
        west = here * west_of(here, below[0:layers, before])
        south = here * below[FIELDS : FIELDS + layers, part]
        north = here * lines[2, 0:layers, part]
        cover = below[MASK : MASK + 1, part]
        drag = jnp.where(row_index(layers, size) == 0, below[FG : FG + 1, part], 0.0)
        full = relax(cover) + drag
        for comp, (col_factor, row_factor) in enumerate(FACTORS):
            row = slice(F0 + comp, F0 + comp + 1)
            under = slice(FIELDS + F0 + comp, FIELDS + F0 + comp + 1)
            mid = below[row, part]
            line[comp, 0:layers, part] = full * mid + (
                col_factor
                * (
                    east * (mid - east_of(mid, below[row, after]))
                    + west * (mid - west_of(mid, below[row, before]))
                )
                + row_factor
                * (south * (mid - below[under, part]) + north * (mid - lines[2, row, part]))
            )

    def layer_step(layer, carry):
        kind = jnp.where(layer == 0, 1, 0)
        lower = jnp.maximum(layer - 1, 0)
        for start, size in chunks + [(cols, LANES)]:
            part = slice(start, start + size)
            here, left, right = columns(
                lambda cut: roots[layer, :, cut], lambda: block[layer], start, size
            )
            east = east_of(here, right)
            west = west_of(here, left)
            south = south_of(here, line_of(below, layer, start, size))
            north = north_of(here, line_of(above, layer, start, size))
            for comp in range(2):
                flux = (
                    east * slopes[4 * comp, :, part]
                    + west * slopes[4 * comp + 1, :, part]
                    + south * slopes[4 * comp + 2, :, part]
                    + north * slopes[4 * comp + 3, :, part]
                )
                value = scaled[kind, comp, :, part] + here * flux
                if start < cols:
                    image[comp, layer, :, part] = value
                else:
                    edge[comp] = value
        cross, square, energy = carry
        for start, size in chunks:
            part = slice(start, start + size)
            stop = start + size
            here = roots[layer, :, part]
            right = roots[layer, :, stop : stop + LANES] if stop < cols else block[layer]
            east = east_of(here, right)
            south = south_of(here, line_of(below, layer, start, size))
            beneath = roots[lower, :, part]
            to_east, to_south, to_lower, size_sq, product = 0.0, 0.0, 0.0, 0.0, 0.0
            for comp, (col_factor, row_factor) in enumerate(FACTORS):
                value = image[comp, layer, :, part]
                right = image[comp, layer, :, stop : stop + LANES] if stop < cols else edge[comp]
                step = value - east_of(value, right)
                step = step * step
                to_east += step if col_factor == 1.0 else col_factor * step
                step = value - south_of(value, line_of(line.at[comp], layer, start, size))
                step = step * step
                to_south += step if row_factor == 1.0 else row_factor * step
                step = value - image[comp, lower, :, part]
                to_lower += step * step
                size_sq += value * value
                product += value * force[comp, :, part]
            faces = here * (east * to_east + south * to_south + beneath * (vertical_weight * to_lower))
            cross += fold(product)
            square += fold(size_sq)
            energy += fold(faces + diag[kind, :, part] * size_sq)
        return cross, square, energy

    zero = jnp.zeros((8, LANES), F32)
    cross, square, energy = lax.fori_loop(0, layers, layer_step, (zero, zero, zero))
    lane = lane_index(1, LANES)
    packed = jnp.zeros((1, LANES), F32)
    for index, part in enumerate((layers * squares, cross, square, energy)):
        packed = jnp.where(lane == index, jnp.sum(part), packed)
    sums[...] = jnp.broadcast_to(packed[None], sums.shape)


def krylov_weights(gathered):
    total = jnp.sum(gathered, axis=0)
    lane = lane_index(1, LANES)

    def moment(index):
        return jnp.sum(jnp.where(lane == index, total, 0.0), axis=1, keepdims=True)

    norm, cross, square, energy = (moment(index) for index in range(4))
    step_one = norm / cross
    norm_next = step_one * (step_one * square - 2.0 * cross) + norm
    lead = 1.0 + norm_next / norm
    curve = lead * lead * cross - 2.0 * lead * step_one * square + step_one * step_one * energy
    step_two = norm_next / curve
    return step_one + step_two * lead, -step_two * step_one


def placed(value, source_row, target_row):
    rows, cols = value.shape
    moved_rows = pltpu.roll(value, (rows - source_row) % rows, 0) if source_row % rows else value
    kept = jnp.where(row_index(rows, cols) < 3, moved_rows, 0.0)
    return pltpu.roll(kept, target_row % rows, 0) if target_row % rows else kept


def strip_kernel(info, *refs):
    sources, outs = refs[:12], refs[12:17]
    own, tile, pair, cross, fringe = outs
    buffers, done = refs[17:29], refs[29]
    copies = [
        pltpu.make_async_copy(source.at[0] if slot == 6 else source, target, done.at[slot])
        for slot, (source, target) in enumerate(zip(sources, buffers))
    ]
    for copy in copies:
        copy.start()
    for copy in copies:
        copy.wait()
    prev, burden, sheet, chan_east, chan_south, area, w, d, m, fl, fr, geo = buffers
    left = info[0] == 0
    wide = prev.shape[1]
    cols = w.shape[1]
    half_cols = cols // 2
    for start in range(0, wide, CHUNK):
        part = slice(start, start + CHUNK)
        base = sheet_conduct * sheet[:, part]
        fields = [
            prev[:, part],
            burden[:, part],
            sheet[:, part],
            base + channel_conduct * chan_east[:, part].astype(F32) * area[:, part],
            base + channel_conduct * chan_south[:, part].astype(F32) * area[:, part],
        ]
        first, last = None, None
        for index, field in enumerate(fields):
            own[index, :, part] = field
            both = jnp.concatenate([field, field], axis=0)
            head, tail = placed(both, 0, 3 * index), placed(both, 5, 3 * index)
            first = head if first is None else first + head
            last = tail if last is None else last + tail
        pair[:, part] = jnp.where(left, last, first)
        cross[:, part] = jnp.where(left, first, last)
    for start in range(0, cols, CHUNK):
        part = slice(start, start + CHUNK)

        def shifted_part(offset, start=start):
            return slice(wide + offset + start, wide + offset + start + CHUNK)

        cover = m[:, part].astype(F32)
        fields = [
            root(w[:, part]) * cover,
            d[0, :, part] * cover,
            d[1, :, part] * cover,
            fr[:, part] * (cover * (1.0 - fl[:, part].astype(F32))),
            geo[:, part],
        ]
        first, last, middle, halves = None, None, None, []
        for index, field in enumerate(fields):
            tile[index, :, part] = field
            head, tail = placed(field, 0, 3 * index), placed(field, 13, 3 * index)
            inner = jnp.where(left, placed(field, 5, 3 * index), placed(field, 8, 3 * index))
            first = head if first is None else first + head
            last = tail if last is None else last + tail
            middle = inner if middle is None else middle + inner
            halves.append(jnp.where(left, field[8:16], field[0:8]))
        fringe[0, :, part] = first
        fringe[1, :, part] = last
        cross[:, shifted_part(0)] = jnp.where(left, first, last)
        pair[:, shifted_part(0)] = jnp.concatenate(halves[0:2], axis=0)
        pair[:, shifted_part(cols)] = jnp.concatenate(halves[2:4], axis=0)
        pair[:, shifted_part(2 * cols)] = middle
        row = 0 if start < half_cols else 8
        place = wide + 3 * cols + start % half_cols
        pair[row : row + 8, place : place + CHUNK] = halves[4]


def assemble_kernel(info, own, tile, pair, cross, above, below, low, plan, base, hyd):
    left = info[0] == 0
    wide = own.shape[2]
    cols = tile.shape[2]
    half_cols = cols // 2
    row = row_index(16, CHUNK)
    in_north = row >= 13
    in_south = (row >= 8) & (row <= 10)
    blank = jnp.zeros((8, CHUNK), F32)

    def circle(main, index, mine, theirs):
        north = jnp.where(left, theirs, mine)
        south = jnp.where(left, mine, theirs)
        north = pltpu.roll(north, (13 - 3 * index) % 16, 0)
        south = pltpu.roll(south, (8 - 3 * index) % 16, 0)
        both = jnp.concatenate([main, blank], axis=0)
        return jnp.where(in_north, north, jnp.where(in_south, south, both))

    for start in range(0, wide, CHUNK):
        part = slice(start, start + CHUNK)
        from_pair, from_cross = pair[:, part], cross[:, part]
        for index in range(5):
            hyd[index, :, part] = circle(own[index, :, part], index, from_pair, from_cross)
    for start in range(0, cols, CHUNK):
        part = slice(start, start + CHUNK)
        middle = pair[:, wide + 2 * cols + start : wide + 2 * cols + start + CHUNK]
        outer = cross[:, wide + start : wide + start + CHUNK]
        north, south = above[FIELDS : FIELDS + 16, part], below[2 * FIELDS : 2 * FIELDS + 16, part]
        replaced = (left & in_north) | (jnp.logical_not(left) & in_south)
        for index in range(5):
            field = tile[index, :, part]
            swapped = jnp.concatenate([field[8:16], field[0:8]], axis=0)
            here = jnp.where(left, field, swapped)
            fringe = jnp.where(
                left,
                pltpu.roll(north, (13 - 3 * index) % 16, 0),
                pltpu.roll(south, (8 - 3 * index) % 16, 0),
            )
            here = jnp.where(replaced, fringe, here)
            if index < 4:
                place = wide + (index // 2) * cols + start
                top = (index % 2) * 8
            else:
                place = wide + 3 * cols + start % half_cols
                top = 0 if start < half_cols else 8
            there = circle(pair[top : top + 8, place : place + CHUNK], index, middle, outer)
            base[index, :, part] = jnp.where(left, here, there)
            base[index, :, cols + start : cols + start + CHUNK] = jnp.where(left, there, here)

    def neighbours(ref, start):
        stop = start + CHUNK
        zero = jnp.zeros((16, LANES), F32)
        here = ref[:, start:stop]
        right = ref[:, stop : stop + LANES] if stop < wide else zero
        leftward = ref[:, start - LANES : start] if start else zero
        return here, east_of(here, right), west_of(here, leftward), pltpu.roll(here, 15, 0), pltpu.roll(here, 1, 0)

    for start in range(0, wide, CHUNK):
        part = slice(start, start + CHUNK)
        here, east, west, south, north = neighbours(base.at[0], start)
        drag = base[3, :, part]
        diagonal = relax(jnp.where(here > 0.0, 1.0, 0.0)) + drag
        for comp, (col_factor, row_factor) in enumerate(FACTORS):
            mid, mid_e, mid_w, mid_s, mid_n = neighbours(base.at[1 + comp], start)
            low[comp, :, part] = mid
            low[2 + comp, :, part] = diagonal * mid + here * (
                col_factor * (east * (mid - mid_e) + west * (mid - mid_w))
                + row_factor * (south * (mid - mid_s) + north * (mid - mid_n))
            )
        low[4, :, part] = drag
        low[5, :, part] = base[4, :, part]
        prev, prev_e, prev_w, prev_s, prev_n = neighbours(hyd.at[0], start)
        burden, sheet = hyd[1, :, part], hyd[2, :, part]
        to_east, _, to_west, _, _ = neighbours(hyd.at[3], start)
        to_south = hyd[4, :, part]
        to_north = pltpu.roll(to_south, 1, 0)
        total = storage + (to_east + to_west + to_south + to_north)
        creep = sheet * jnp.abs(burden - prev)
        known = storage * prev + creep * burden
        known += to_east * prev_e + to_west * prev_w + to_south * prev_s + to_north * prev_n
        for index, value in enumerate(
            (storage * prev, burden, sheet, to_east, to_west, to_south, to_north, total, known, total + creep)
        ):
            plan[index, :, part] = value


def hydrology_kernel(info, gathered, low, plan, weights, potential, sheet_next, keep, give, now, then, fixed, opens):
    first, second = krylov_weights(gathered[...])
    weights[0] = jnp.broadcast_to(first, (8, LANES))
    weights[1] = jnp.broadcast_to(second, (8, LANES))
    left = info[0] == 0
    wide = low.shape[2]
    cols = wide // 2
    row = row_index(16, CHUNK)
    outside = ((info[1] == 1) & (row >= 13)) | ((info[2] == 1) & (row >= 8) & (row <= 10))
    for start in range(0, wide, CHUNK):
        part = slice(start, start + CHUNK)
        one = first * low[0, :, part] + second * low[2, :, part]
        two = first * low[1, :, part] + second * low[3, :, part]
        slide_sq = one * one + two * two
        lifted = slide_sq + speed_floor
        speed = lifted * lax.rsqrt(lifted)
        melt = melt_factor * (low[5, :, part] + low[4, :, part] * slide_sq)
        opening = speed * jnp.maximum(bump_height - plan[2, :, part], 0.0)
        opens[:, part] = opening[0:8]
        gain = melt - opening
        fixed[:, part] = plan[0, :, part] + gain
        now[:, part] = jnp.where(outside, 0.0, (plan[8, :, part] + gain) / plan[9, :, part])

    def relaxed(ref, start):
        part = slice(start, start + CHUNK)
        stop = start + CHUNK
        zero = jnp.zeros((16, LANES), F32)
        here = ref[:, part]
        east = east_of(here, ref[:, stop : stop + LANES] if stop < wide else zero)
        west = west_of(here, ref[:, start - LANES : start] if start else zero)
        burden = plan[1, :, part]
        creep = plan[2, :, part] * jnp.abs(burden - here)
        top = fixed[:, part] + creep * burden
        top += plan[3, :, part] * east + plan[4, :, part] * west
        top += plan[5, :, part] * pltpu.roll(here, 15, 0) + plan[6, :, part] * pltpu.roll(here, 1, 0)
        return top / (plan[7, :, part] + creep)

    here, there = now, then
    for _ in range(HYD_ITERS - 2):
        for start in range(0, wide, CHUNK):
            there[:, start : start + CHUNK] = jnp.where(outside, 0.0, relaxed(here, start))
        here, there = there, here
    for start in range(0, cols, CHUNK):
        sides = []
        for begin in (start, cols + start):
            part = slice(begin, begin + CHUNK)
            value = relaxed(here, begin)[0:8]
            sheet = plan[2, 0:8, part]
            pressure = plan[1, 0:8, part] - value
            potential[:, part] = value
            sheet_next[:, part] = sheet + time_step * (
                opens[:, part] - sheet * jnp.abs(pressure) * pressure
            )
            sides.append(pressure)
        part = slice(start, start + CHUNK)
        keep[:, part] = jnp.where(left, sides[0], sides[1])
        give[:, part] = jnp.where(left, sides[1], sides[0])


def velocity_kernel(weights, force, image, out, staged, done):
    layers = image.shape[1]
    first, second = weights[0, 0:1, 0:1], weights[1, 0:1, 0:1]

    def copy(layer):
        return pltpu.make_async_copy(staged.at[:, layer], out.at[:, layer], done.at[layer])

    def step(layer, carry):
        for comp in range(2):
            staged[comp, layer] = first * force[comp] + second * image[comp, layer]
        copy(layer).start()
        return carry

    lax.fori_loop(0, layers, step, 0)

    def finish(layer, carry):
        copy(layer).wait()
        return carry

    lax.fori_loop(0, layers, finish, 0)


def call(kernel, out_shape, n_in, scratch=(), smem=(), far=(), out_space=pltpu.VMEM, **kwargs):
    outs = out_shape if isinstance(out_shape, (list, tuple)) else (out_shape,)
    specs = tuple(whole(out_space) for _ in outs)
    return pl.pallas_call(
        kernel,
        out_shape=out_shape,
        in_specs=[
            whole(pltpu.SMEM if i in smem else pltpu.HBM if i in far else pltpu.VMEM) for i in range(n_in)
        ],
        out_specs=specs if isinstance(out_shape, (list, tuple)) else specs[0],
        scratch_shapes=list(scratch),
        compiler_params=pltpu.CompilerParams(vmem_limit_bytes=22 << 20),
        **kwargs,
    )


def moved(value, axis, steps):
    count = lax.axis_size(axis)
    leading, last = (max(0, -steps), min(count, count - steps))
    return lax.ppermute(value, axis, [(source, source + steps) for source in range(leading, last)])


def body(
    viscosity,
    driving_stress,
    ice_mask,
    float_mask,
    friction,
    geothermal,
    potential_prev,
    overburden,
    sheet_thick,
    channel_east,
    channel_south,
    channel_area,
):
    layers, rows, cols = viscosity.shape
    side, band = lax.axis_index("hyd"), lax.axis_index("ice")
    bands = lax.axis_size("ice")
    info = jnp.stack([side, (side == 0) & (band == 0), (side == 1) & (band == bands - 1)]).astype(jnp.int32)
    swap = [(0, 1), (1, 0)]
    fixed_inputs = (
        potential_prev,
        overburden,
        sheet_thick,
        channel_east,
        channel_south,
        channel_area,
        viscosity,
        driving_stress,
        ice_mask,
        float_mask,
        friction,
        geothermal,
    )
    placed_inputs = tuple(pltpu.with_memory_space_constraint(array, pltpu.HBM) for array in fixed_inputs)
    raw = placed_inputs[6:11]
    types = (jnp.bfloat16, F32, jnp.int32, jnp.int32, F32)

    def buffers(last):
        return [pltpu.VMEM(array.shape[:-1] + (last,), kind) for array, kind in zip(raw, types)]

    message = call(
        edge_kernel,
        shape_of(rows, LANES),
        6,
        scratch=buffers(LANES) + [pltpu.SemaphoreType.DMA((5,))],
        smem=(0,),
        far=range(1, 6),
    )(info, *raw)
    received = lax.ppermute(message, "hyd", swap)
    strip_rows, full = potential_prev.shape
    own, tile, pair, cross, fringe = call(
        strip_kernel,
        [
            shape_of(5, strip_rows, full),
            shape_of(5, rows, cols),
            shape_of(rows, full + 3 * cols + cols // 2),
            shape_of(rows, full + cols),
            shape_of(2, rows, cols),
        ],
        13,
        scratch=[
            pltpu.VMEM(array.shape[1:] if slot == 6 else array.shape, array.dtype)
            for slot, array in enumerate(fixed_inputs)
        ]
        + [pltpu.SemaphoreType.DMA((12,))],
        smem=(0,),
        far=range(1, 13),
    )(info, *placed_inputs)
    pair_in = lax.ppermute(pair, "hyd", swap)
    meet = [(2 * index + 1, 2 * index + 2) for index in range(bands - 1)]
    cross_in = lax.ppermute(cross, AXES, meet + [(high, low) for low, high in meet])
    roots, lines, force, fric, cover = call(
        root_kernel,
        [shape_of(layers, rows, cols), shape_of(3, FIELDS, cols), shape_of(2, rows, cols), shape_of(rows, cols), shape_of(rows, cols)],
        5,
        scratch=buffers(cols) + [pltpu.SemaphoreType.DMA((cols // FETCH, 5))],
        far=range(5),
    )(*raw)
    wide = cols + LANES
    block, to_south, to_north = call(
        unpack_kernel,
        [shape_of(FIELDS, rows, LANES), shape_of(FIELDS + 16, wide), shape_of(2 * FIELDS + 16, wide)],
        4,
        smem=(0,),
    )(info, received, lines, fringe)
    above = moved(to_south, "ice", 1)
    below = moved(to_north, "ice", -1)
    count = lax.axis_size("ice") * lax.axis_size("hyd")
    image, sums = call(
        operator_kernel,
        [shape_of(2, layers, rows, cols), shape_of(count, 1, LANES)],
        8,
        scratch=[
            pltpu.VMEM((8, rows, wide), F32),
            pltpu.VMEM((2, 2, rows, wide), F32),
            pltpu.VMEM((2, rows, cols), F32),
            pltpu.VMEM((2, FIELDS, cols), F32),
            pltpu.VMEM((2, rows, LANES), F32),
        ],
    )(roots, force, fric, cover, block, above, below, lines)
    gathered = lax.all_to_all(sums, AXES, 0, 0, tiled=True)
    low, plan = call(
        assemble_kernel,
        [shape_of(6, rows, full), shape_of(10, rows, full)],
        7,
        scratch=[pltpu.VMEM((5, rows, full), F32), pltpu.VMEM((5, rows, full), F32)],
        smem=(0,),
    )(info, own, tile, pair_in, cross_in, above, below)
    weights, potential, sheet_next, keep, give = call(
        hydrology_kernel,
        [
            shape_of(2, 8, LANES),
            shape_of(strip_rows, full),
            shape_of(strip_rows, full),
            shape_of(strip_rows, cols),
            shape_of(strip_rows, cols),
        ],
        4,
        scratch=[pltpu.VMEM((rows, full), F32)] * 3 + [pltpu.VMEM((strip_rows, full), F32)],
        smem=(0,),
    )(info, gathered, low, plan)
    got = lax.ppermute(give, "hyd", swap)
    velocity = pl.pallas_call(
        velocity_kernel,
        out_shape=shape_of(2, layers, rows, cols),
        in_specs=[whole(), whole(), whole()],
        out_specs=whole(pltpu.HBM),
        scratch_shapes=[pltpu.VMEM((2, layers, rows, cols), F32), pltpu.SemaphoreType.DMA((layers,))],
        compiler_params=pltpu.CompilerParams(vmem_limit_bytes=22 << 20),
    )(weights, force, pltpu.with_memory_space_constraint(image, pltpu.VMEM))

    is_left = side == 0
    effective = jnp.concatenate([jnp.where(is_left, keep, got), jnp.where(is_left, got, keep)], axis=0)
    return (velocity, effective, potential, sheet_next)


def solution(mesh):
    tiles = P("ice", "hyd")
    layered = P(None, "ice", "hyd")
    strips = P(("ice", "hyd"), None)
    return jax.shard_map(
        body,
        mesh=mesh,
        in_specs=(layered, layered, tiles, tiles, tiles, tiles) + (strips,) * 6,
        out_specs=(P(None, None, "ice", "hyd"), tiles, strips, strips),
        check_vma=False,
    )
```

time: 119 us -> 112 us (0.941)
  the two profiles are of different devices: /device:TPU:103 before, /device:TPU:16 now
where the time goes in v2:
time: 112 us; the launch traced here: 110 us
  waiting for transfers between devices  35.4 us (32%)
  Pallas kernels  31.4 us (28%)
  starting transfers between devices  21.4 us (19%)
  local copies, waits for them, and re-layouts  20 us (18%)
    unnamed x32, local copies, waits for them, and re-layouts  20 us
    ppermute x1, waiting for transfers between devices, body(): received = lax.ppermute(message, 'hyd', swap)  19.2 us
    ppermute x2, waiting for transfers between devices, moved(): lax.ppermute(value, axis, [(source, source + steps) for source in range(l...  16.2 us
    pallas_call x1, Pallas kernels, body(): call(operator_kernel, [shape_of(2, layers, rows, cols), shape_of(count, 1...  13.5 us
    ppermute x2, starting transfers between devices, moved(): lax.ppermute(value, axis, [(source, source + steps) for source in range(l...  9.06 us
    all_to_all x1, starting transfers between devices, body(): gathered = lax.all_to_all(sums, AXES, 0, 0, tiled=True)  5.5 us
    pallas_call x1, Pallas kernels, body(): call(strip_kernel, [shape_of(5, strip_rows, full), shape_of(5, rows, cols...  4.25 us
    ppermute x1, starting transfers between devices, body(): lax.ppermute(cross, AXES, meet + [(high, low) for low, high in meet])  3.55 us
  transfers between devices with their start and end apart: 7, of which 2 were waited for; matrix products, arithmetic and copies ran while one was open for 0% of the time, Pallas kernels for 22%

profile of v2, /device:TPU:16, one launch (start us, length us, event | category | flops | bytes accessed | tf_op | source)
XLA Modules:
  0.0 109.8 jit_solution(4220991528901521614)
XLA Ops:
  0.7 4.3 %shard_map.149 = (f32[5,8,6144]{2,1,0:T(8,128)S(1)}, f32[5,16,3072]{2,1,0:T(8,128)S(1)}, f32[16,16896]{1,0:T(8,128)}, f32[16,9216]{1,0:T(8,128)S(1)}, f32[2,16,3072]{2,1,0:T(8,128)S(1)}) custom-call(s32[3]{0:T(128)S(1)} %pad_add_fusion.half.info, f32[8,6144]{1,0:T(8,128)} %refs_0_.1, f32[8,6144]{1,0:T(8,128)} %refs_1_.1, f32[8,6144]{1,0:T(8,128)} %refs_2_.1, ...), custom_call_target="tpu_custom_call" | custom-call | tf_op jit(solution)/shard_map/pallas_call | solution.py:651
  6.0 1.3 %collective-permute-start.3 = (f32[16,16896]{1,0:T(8,128)}, f32[16,16896]{1,0:T(8,128)S(1)}, u32[]{:S(2)}, u32[]{:S(2)}) collective-permute-start(f32[16,16896]{1,0:T(8,128)} %get-tuple-element.38), channel_id=1, source_target_pairs={{0,1},{1,0},{2,3},{3,2},{4,5},{5,4},{6,7},{7,6},{8,9},{9,8},{10,11... | collective-permute-start | bytes 3244040 | tf_op jit(solution)/shard_map/ppermute | solution.py:669
  7.2 1.6 %shard_map.148 = f32[16,128]{1,0:T(8,128)S(1)} custom-call(s32[3]{0:T(128)S(1)} %pad_add_fusion.half.info, bf16[20,16,3072]{2,1,0:T(8,128)(2,1)} %refs_6_.1, f32[2,16,3072]{2,1,0:T(8,128)} %refs_7_.1, s32[16,3072]{1,0:T(8,128)} %refs_8_.1, s32[16,3072]{1,0:T(8,128)} %refs_9_.1, f32[16,3072]{1,0:T(8,128)} %refs_10_.1), custom_call_target="tpu_custom_call" | custom-call | tf_op jit(solution)/shard_map/pallas_call | solution.py:641
  9.7 3.0 %shard_map.147 = (f32[20,16,3072]{2,1,0:T(8,128)S(1)}, f32[3,24,3072]{2,1,0:T(8,128)S(1)}, f32[2,16,3072]{2,1,0:T(8,128)S(1)}, f32[16,3072]{1,0:T(8,128)S(1)}, f32[16,3072]{1,0:T(8,128)S(1)}) custom-call(bf16[20,16,3072]{2,1,0:T(8,128)(2,1)} %refs_6_.1, f32[2,16,3072]{2,1,0:T(8,128)} %refs_7_.1, s32[16,3072]{1,0:T(8,128)} %refs_8_.1, s32[16,3072]{1,0:T(8,128)} %refs_9_.1, ...), custom_call_target="tpu_custom_call" | custom-call | tf_op jit(solution)/shard_map/pallas_call | solution.py:672
  12.7 19.2 %collective-permute-done.message = f32[16,128]{1,0:T(8,128)S(1)} collective-permute-done((f32[16,128]{1,0:T(8,128)S(1)}, f32[16,128]{1,0:T(8,128)S(1)}, u32[]{:S(2)}, u32[]{:S(2)}) %collective-permute-start) | collective-permute-done | bytes 8224 | tf_op jit(solution)/shard_map/ppermute | solution.py:649
  32.6 6.5 %collective-permute-start.2 = (f32[64,3200]{1,0:T(8,128)S(1)}, f32[64,3200]{1,0:T(8,128)S(1)}, u32[]{:S(2)}, u32[]{:S(2)}) collective-permute-start(f32[64,3200]{1,0:T(8,128)S(1)} %get-tuple-element.34), channel_id=1, source_target_pairs={{2,0},{4,2},{6,4},{8,6},{10,8},{12,10},{14,12},{16,14},{18,16},{20... | collective-permute-start | bytes 2457608 | tf_op jit(solution)/shard_map/ppermute | solution.py:598
  39.1 3.6 %collective-permute-start.4 = (f32[16,9216]{1,0:T(8,128)S(1)}, f32[16,9216]{1,0:T(8,128)S(1)}, u32[]{:S(2)}, u32[]{:S(2)}) collective-permute-start(f32[16,9216]{1,0:T(8,128)S(1)} %get-tuple-element.39), channel_id=1, source_target_pairs={{1,2},{3,4},{5,6},{7,8},{9,10},{11,12},{13,14},{15,16},{17,18},{19... | collective-permute-start | bytes 1769480 | tf_op jit(solution)/shard_map/ppermute | solution.py:671
  42.7 2.6 %collective-permute-start.1 = (f32[40,3200]{1,0:T(8,128)S(1)}, f32[40,3200]{1,0:T(8,128)S(1)}, u32[]{:S(2)}, u32[]{:S(2)}) collective-permute-start(f32[40,3200]{1,0:T(8,128)S(1)} %get-tuple-element.33), channel_id=1, source_target_pairs={{0,2},{2,4},{4,6},{6,8},{8,10},{10,12},{12,14},{14,16},{16,18},{18... | collective-permute-start | bytes 1536008 | tf_op jit(solution)/shard_map/ppermute | solution.py:598
  45.3 16.2 %collective-permute-done.1.above = f32[40,3200]{1,0:T(8,128)S(1)} collective-permute-done((f32[40,3200]{1,0:T(8,128)S(1)}, f32[40,3200]{1,0:T(8,128)S(1)}, u32[]{:S(2)}, u32[]{:S(2)}) %collective-permute-start.1) | collective-permute-done | bytes 512032 | tf_op jit(solution)/shard_map/ppermute | solution.py:598
  61.5 13.5 %shard_map.151 = (f32[2,20,16,3072]{3,2,1,0:T(8,128)S(1)}, f32[128,1,128]{2,1,0:T(1,128)}) custom-call(f32[20,16,3072]{2,1,0:T(8,128)S(1)} %get-tuple-element.26.roots, f32[2,16,3072]{2,1,0:T(8,128)S(1)} %get-tuple-element.27.force, f32[16,3072]{1,0:T(8,128)S(1)} %get-tuple-element.28.fric, f32[16,3072]{1,0:T(8,128)S(1)} %get-tuple-element.29.mask, ...), custom_call_target="tpu_custom_call" | custom-call | tf_op jit(solution)/shard_map/pallas_call | solution.py:689
  75.0 3.2 %copy-done = f32[2,20,16,3072]{3,2,1,0:T(8,128)} copy-done((f32[2,20,16,3072]{3,2,1,0:T(8,128)}, f32[2,20,16,3072]{3,2,1,0:T(8,128)S(1)}, u32[]{:S(2)}) %copy-start) | copy-done | bytes 7864344
  78.2 5.5 %all-to-all-start = ((f32[128,1,128]{2,1,0:T(1,128)}), f32[128,1,128]{2,1,0:T(1,128)S(1)}, u32[]{:S(2)}, u32[]{:S(2)}) async-start(f32[128,1,128]{2,1,0:T(1,128)} %get-tuple-element.35), calls=%async_computation | async-start | bytes 131072 | tf_op jit(solution)/shard_map/all_to_all | solution.py:701
  85.6 1.0 copy-done.5
  86.6 1.2 %copy-done.9 = f32[16,16896]{1,0:T(8,128)S(1)} copy-done((f32[16,16896]{1,0:T(8,128)S(1)}, f32[16,16896]{1,0:T(8,128)}, u32[]{:S(2)}) %copy-start.9) | copy-done | bytes 1081368
  87.9 1.2 %copy-done.11 = f32[5,8,6144]{2,1,0:T(8,128)S(1)} copy-done((f32[5,8,6144]{2,1,0:T(8,128)S(1)}, f32[5,8,6144]{2,1,0:T(8,128)}, u32[]{:S(2)}) %copy-start.11) | copy-done | bytes 983064
  89.1 1.2 %copy-done.13 = f32[5,16,3072]{2,1,0:T(8,128)S(1)} copy-done((f32[5,16,3072]{2,1,0:T(8,128)S(1)}, f32[5,16,3072]{2,1,0:T(8,128)}, u32[]{:S(2)}) %copy-start.13) | copy-done | bytes 983064
  90.3 1.1 copy-done.15
  91.3 2.5 %shard_map.152 = (f32[6,16,6144]{2,1,0:T(8,128)S(1)}, f32[10,16,6144]{2,1,0:T(8,128)S(1)}) custom-call(s32[3]{0:T(128)S(1)} %pad_add_fusion.half.info, f32[5,8,6144]{2,1,0:T(8,128)S(1)} %copy-done.11, f32[5,16,3072]{2,1,0:T(8,128)S(1)} %copy-done.13, f32[16,16896]{1,0:T(8,128)S(1)} %copy-done.9, f32[16,9216]{1,0:T(8,128)S(1)} %copy-done.15, ...), custom_call_target="tpu_custom_call" | custom-call | tf_op jit(solution)/shard_map/pallas_call | solution.py:702
  93.8 1.9 %copy-done.2 = f32[10,16,6144]{2,1,0:T(8,128)} copy-done((f32[10,16,6144]{2,1,0:T(8,128)}, f32[10,16,6144]{2,1,0:T(8,128)S(1)}, u32[]{:S(2)}) %copy-start.2) | copy-done | bytes 3932184
  95.7 2.1 %copy-done.3 = f32[10,16,6144]{2,1,0:T(8,128)S(1)} copy-done((f32[10,16,6144]{2,1,0:T(8,128)S(1)}, f32[10,16,6144]{2,1,0:T(8,128)}, u32[]{:S(2)}) %copy-start.3) | copy-done | bytes 3932184
  97.8 2.5 %shard_map.153 = (f32[2,8,128]{2,1,0:T(8,128)S(1)}, f32[8,6144]{1,0:T(8,128)}, f32[8,6144]{1,0:T(8,128)}, f32[8,3072]{1,0:T(8,128)S(1)}, f32[8,3072]{1,0:T(8,128)S(1)}) custom-call(s32[3]{0:T(128)S(1)} %pad_add_fusion.half.info, f32[128,1,128]{2,1,0:T(1,128)S(1)} %all-to-all-done.gathered, f32[6,16,6144]{2,1,0:T(8,128)S(1)} %get-tuple-element.40.low, ...), custom_call_target="tpu_custom_call" | custom-call | tf_op jit(solution)/shard_map/pallas_call | solution.py:709
  100.3 1.2 %collective-permute-start.5 = (f32[8,3072]{1,0:T(8,128)S(1)}, f32[8,3072]{1,0:T(8,128)S(1)}, u32[]{:S(2)}, u32[]{:S(2)}) collective-permute-start(f32[8,3072]{1,0:T(8,128)S(1)} %get-tuple-element.45), channel_id=1, source_target_pairs={{0,1},{1,0},{2,3},{3,2},{4,5},{5,4},{6,7},{7,6},{8,9},{9,8},{10,11... | collective-permute-start | bytes 294920 | tf_op jit(solution)/shard_map/ppermute | solution.py:722
  101.5 3.2 %copy-done.1 = f32[2,20,16,3072]{3,2,1,0:T(8,128)S(1)} copy-done((f32[2,20,16,3072]{3,2,1,0:T(8,128)S(1)}, f32[2,20,16,3072]{3,2,1,0:T(8,128)}, u32[]{:S(2)}) %copy-start.1) | copy-done | bytes 7864344
  105.7 3.4 %shard_map.154 = f32[2,20,16,3072]{3,2,1,0:T(8,128)} custom-call(f32[2,8,128]{2,1,0:T(8,128)S(1)} %get-tuple-element.42.weights, f32[2,16,3072]{2,1,0:T(8,128)S(1)} %copy-done.7, f32[2,20,16,3072]{3,2,1,0:T(8,128)S(1)} %copy-done.1), custom_call_target="tpu_custom_call" | custom-call | tf_op jit(solution)/shard_map/pallas_call | solution.py:723
  (33 shorter events, 6.1 us)
Async XLA Ops:
  5.0 1.0 copy-start.10
  6.0 2.9 %copy-start.12 = (f32[5,16,3072]{2,1,0:T(8,128)}, f32[5,16,3072]{2,1,0:T(8,128)S(1)}, u32[]{:S(2)}) copy-start(f32[5,16,3072]{2,1,0:T(8,128)S(1)} %get-tuple-element.37.tile) | copy-start | bytes 2949124
  6.0 78.6 %collective-permute-start.3 = (f32[16,16896]{1,0:T(8,128)}, f32[16,16896]{1,0:T(8,128)S(1)}, u32[]{:S(2)}, u32[]{:S(2)}) collective-permute-start(f32[16,16896]{1,0:T(8,128)} %get-tuple-element.38), channel_id=1, source_target_pairs={{0,1},{1,0},{2,3},{3,2},{4,5},{5,4},{6,7},{7,6},{8,9},{9,8},{10,11... | collective-permute-start | bytes 3244040 | tf_op jit(solution)/shard_map/ppermute | solution.py:669
  8.9 23.1 %collective-permute-start = (f32[16,128]{1,0:T(8,128)S(1)}, f32[16,128]{1,0:T(8,128)S(1)}, u32[]{:S(2)}, u32[]{:S(2)}) collective-permute-start(f32[16,128]{1,0:T(8,128)S(1)} %shard_map.148), channel_id=1, source_target_pairs={{0,1},{1,0},{2,3},{3,2},{4,5},{5,4},{6,7},{7,6},{8,9},{9,8},{10,11... | collective-permute-start | bytes 24584 | tf_op jit(solution)/shard_map/ppermute | solution.py:649
  12.7 62.3 %copy-start.6 = (f32[2,16,3072]{2,1,0:T(8,128)}, f32[2,16,3072]{2,1,0:T(8,128)S(1)}, u32[]{:S(2)}) copy-start(f32[2,16,3072]{2,1,0:T(8,128)S(1)} %get-tuple-element.27.force) | copy-start | bytes 1179652
  32.6 28.9 %collective-permute-start.2 = (f32[64,3200]{1,0:T(8,128)S(1)}, f32[64,3200]{1,0:T(8,128)S(1)}, u32[]{:S(2)}, u32[]{:S(2)}) collective-permute-start(f32[64,3200]{1,0:T(8,128)S(1)} %get-tuple-element.34), channel_id=1, source_target_pairs={{2,0},{4,2},{6,4},{8,6},{10,8},{12,10},{14,12},{16,14},{18,16},{20... | collective-permute-start | bytes 2457608 | tf_op jit(solution)/shard_map/ppermute | solution.py:598
  39.1 44.6 %collective-permute-start.4 = (f32[16,9216]{1,0:T(8,128)S(1)}, f32[16,9216]{1,0:T(8,128)S(1)}, u32[]{:S(2)}, u32[]{:S(2)}) collective-permute-start(f32[16,9216]{1,0:T(8,128)S(1)} %get-tuple-element.39), channel_id=1, source_target_pairs={{1,2},{3,4},{5,6},{7,8},{9,10},{11,12},{13,14},{15,16},{17,18},{19... | collective-permute-start | bytes 1769480 | tf_op jit(solution)/shard_map/ppermute | solution.py:671
  42.7 18.8 %collective-permute-start.1 = (f32[40,3200]{1,0:T(8,128)S(1)}, f32[40,3200]{1,0:T(8,128)S(1)}, u32[]{:S(2)}, u32[]{:S(2)}) collective-permute-start(f32[40,3200]{1,0:T(8,128)S(1)} %get-tuple-element.33), channel_id=1, source_target_pairs={{0,2},{2,4},{4,6},{6,8},{8,10},{10,12},{12,14},{14,16},{16,18},{18... | collective-permute-start | bytes 1536008 | tf_op jit(solution)/shard_map/ppermute | solution.py:598
  61.5 13.5 %copy-start.4 = (f32[40,3200]{1,0:T(8,128)}, f32[40,3200]{1,0:T(8,128)S(1)}, u32[]{:S(2)}) copy-start(f32[40,3200]{1,0:T(8,128)S(1)} %collective-permute-done.1.above) | copy-start | bytes 1536004
  75.0 3.2 %copy-start = (f32[2,20,16,3072]{3,2,1,0:T(8,128)}, f32[2,20,16,3072]{3,2,1,0:T(8,128)S(1)}, u32[]{:S(2)}) copy-start(f32[2,20,16,3072]{3,2,1,0:T(8,128)S(1)} %get-tuple-element.43.image) | copy-start | bytes 23592964
  78.2 17.4 %all-to-all-start = ((f32[128,1,128]{2,1,0:T(1,128)}), f32[128,1,128]{2,1,0:T(1,128)S(1)}, u32[]{:S(2)}, u32[]{:S(2)}) async-start(f32[128,1,128]{2,1,0:T(1,128)} %get-tuple-element.35), calls=%async_computation | async-start | bytes 131072 | tf_op jit(solution)/shard_map/all_to_all | solution.py:701
  83.8 0.8 copy-start.14
  84.6 1.0 copy-start.8
  85.6 1.0 copy-start.5
  86.6 1.2 %copy-start.9 = (f32[16,16896]{1,0:T(8,128)S(1)}, f32[16,16896]{1,0:T(8,128)}, u32[]{:S(2)}) copy-start(f32[16,16896]{1,0:T(8,128)} %copy-done.8) | copy-start | bytes 3244036
  87.9 1.2 %copy-start.11 = (f32[5,8,6144]{2,1,0:T(8,128)S(1)}, f32[5,8,6144]{2,1,0:T(8,128)}, u32[]{:S(2)}) copy-start(f32[5,8,6144]{2,1,0:T(8,128)} %copy-done.10) | copy-start | bytes 2949124
  89.1 1.2 %copy-start.13 = (f32[5,16,3072]{2,1,0:T(8,128)S(1)}, f32[5,16,3072]{2,1,0:T(8,128)}, u32[]{:S(2)}) copy-start(f32[5,16,3072]{2,1,0:T(8,128)} %copy-done.12) | copy-start | bytes 2949124
  90.3 1.1 copy-start.15
  93.8 1.9 %copy-start.2 = (f32[10,16,6144]{2,1,0:T(8,128)}, f32[10,16,6144]{2,1,0:T(8,128)S(1)}, u32[]{:S(2)}) copy-start(f32[10,16,6144]{2,1,0:T(8,128)S(1)} %get-tuple-element.41.plan) | copy-start | bytes 11796484
  95.7 2.1 %copy-start.3 = (f32[10,16,6144]{2,1,0:T(8,128)S(1)}, f32[10,16,6144]{2,1,0:T(8,128)}, u32[]{:S(2)}) copy-start(f32[10,16,6144]{2,1,0:T(8,128)} %copy-done.2) | copy-start | bytes 11796484
  100.3 8.8 %collective-permute-start.5 = (f32[8,3072]{1,0:T(8,128)S(1)}, f32[8,3072]{1,0:T(8,128)S(1)}, u32[]{:S(2)}, u32[]{:S(2)}) collective-permute-start(f32[8,3072]{1,0:T(8,128)S(1)} %get-tuple-element.45), channel_id=1, source_target_pairs={{0,1},{1,0},{2,3},{3,2},{4,5},{5,4},{6,7},{7,6},{8,9},{9,8},{10,11... | collective-permute-start | bytes 294920 | tf_op jit(solution)/shard_map/ppermute | solution.py:722
  101.5 3.2 %copy-start.1 = (f32[2,20,16,3072]{3,2,1,0:T(8,128)S(1)}, f32[2,20,16,3072]{3,2,1,0:T(8,128)}, u32[]{:S(2)}) copy-start(f32[2,20,16,3072]{3,2,1,0:T(8,128)} %copy-done) | copy-start | bytes 23592964
  104.7 1.0 copy-start.7

commit v3 on v2

--- a/solution.py
+++ b/solution.py
@@ -6,6 +6,7 @@
 from jax.experimental import pallas as pl
 from jax.experimental.pallas import tpu as pltpu
 from jax.sharding import PartitionSpec as P
+
 
 HYD_ITERS = 3
 vertical_weight = 4.0
@@ -100,7 +101,25 @@
 
 
 def root_kernel(
-    visc, drive, mask, floating, friction, roots, lines, force, fric, covers, w, d, m, fl, fr, done
+    visc,
+    drive,
+    mask,
+    floating,
+    friction,
+    geothermal,
+    roots,
+    lines,
+    force,
+    fric,
+    covers,
+    fringe,
+    w,
+    d,
+    m,
+    fl,
+    fr,
+    geo,
+    done,
 ):
     layers, rows, cols = visc.shape
     starts = list(range(0, cols, FETCH))
@@ -110,7 +129,7 @@
         return [
             pltpu.make_async_copy(source.at[..., part], target.at[..., part], done.at[index, slot])
             for slot, (source, target) in enumerate(
-                ((visc, w), (drive, d), (mask, m), (floating, fl), (friction, fr))
+                ((visc, w), (drive, d), (mask, m), (floating, fl), (friction, fr), (geothermal, geo))
             )
         ]
 
@@ -144,6 +163,10 @@
                     lines[slot, F0 + comp : F0 + comp + 1, part] = pushes[comp][row : row + 1]
                 lines[slot, FG : FG + 1, part] = drag[row : row + 1]
                 lines[slot, MASK : MASK + 1, part] = cover[row : row + 1]
+            fields = [roots[0, :, part], pushes[0], pushes[1], drag, geo[:, part]]
+            for slot, row in enumerate((0, rows - 3)):
+                parts = [placed(field, row, 3 * index) for index, field in enumerate(fields)]
+                fringe[slot, :, part] = functools.reduce(jnp.add, parts)
 
 
 def unpack_kernel(half, message, lines, fringe, block, to_south, to_north):
@@ -340,9 +363,9 @@
 
 
 def strip_kernel(info, *refs):
-    sources, outs = refs[:12], refs[12:17]
-    own, tile, pair, cross, fringe = outs
-    buffers, done = refs[17:29], refs[29]
+    sources, outs = refs[:12], refs[12:16]
+    own, tile, pair, cross = outs
+    buffers, done = refs[16:28], refs[28]
     copies = [
         pltpu.make_async_copy(source.at[0] if slot == 6 else source, target, done.at[slot])
         for slot, (source, target) in enumerate(zip(sources, buffers))
@@ -398,8 +421,6 @@
             last = tail if last is None else last + tail
             middle = inner if middle is None else middle + inner
             halves.append(jnp.where(left, field[8:16], field[0:8]))
-        fringe[0, :, part] = first
-        fringe[1, :, part] = last
         cross[:, shifted_part(0)] = jnp.where(left, first, last)
         pair[:, shifted_part(0)] = jnp.concatenate(halves[0:2], axis=0)
         pair[:, shifted_part(cols)] = jnp.concatenate(halves[2:4], axis=0)
@@ -436,18 +457,20 @@
         part = slice(start, start + CHUNK)
         middle = pair[:, wide + 2 * cols + start : wide + 2 * cols + start + CHUNK]
         outer = cross[:, wide + start : wide + start + CHUNK]
-        north, south = above[FIELDS : FIELDS + 16, part], below[2 * FIELDS : 2 * FIELDS + 16, part]
+        beyond = jnp.where(
+            left, above[FIELDS : FIELDS + 16, part], below[2 * FIELDS : 2 * FIELDS + 16, part]
+        )
         replaced = (left & in_north) | (jnp.logical_not(left) & in_south)
         for index in range(5):
             field = tile[index, :, part]
             swapped = jnp.concatenate([field[8:16], field[0:8]], axis=0)
             here = jnp.where(left, field, swapped)
-            fringe = jnp.where(
+            far = jnp.where(
                 left,
-                pltpu.roll(north, (13 - 3 * index) % 16, 0),
-                pltpu.roll(south, (8 - 3 * index) % 16, 0),
+                pltpu.roll(beyond, (13 - 3 * index) % 16, 0),
+                pltpu.roll(beyond, (8 - 3 * index) % 16, 0),
             )
-            here = jnp.where(replaced, fringe, here)
+            here = jnp.where(replaced, far, here)
             if index < 4:
                 place = wide + (index // 2) * cols + start
                 top = (index % 2) * 8
@@ -495,10 +518,14 @@
             plan[index, :, part] = value
 
 
-def hydrology_kernel(info, gathered, low, plan, weights, potential, sheet_next, keep, give, now, then, fixed, opens):
+def weights_kernel(gathered, weights):
     first, second = krylov_weights(gathered[...])
     weights[0] = jnp.broadcast_to(first, (8, LANES))
     weights[1] = jnp.broadcast_to(second, (8, LANES))
+
+
+def hydrology_kernel(info, weights, low, plan, potential, sheet_next, keep, give, now, then, fixed, opens):
+    first, second = weights[0, 0:1, 0:1], weights[1, 0:1, 0:1]
     left = info[0] == 0
     wide = low.shape[2]
     cols = wide // 2
@@ -647,15 +674,31 @@
         far=range(1, 6),
     )(info, *raw)
     received = lax.ppermute(message, "hyd", swap)
+    roots, lines, force, fric, cover, fringe = call(
+        root_kernel,
+        [shape_of(layers, rows, cols), shape_of(3, FIELDS, cols), shape_of(2, rows, cols), shape_of(rows, cols), shape_of(rows, cols), shape_of(2, rows, cols)],
+        6,
+        scratch=buffers(cols) + [pltpu.VMEM((rows, cols), F32), pltpu.SemaphoreType.DMA((cols // FETCH, 6))],
+        far=range(6),
+    )(*placed_inputs[6:])
+    wide = cols + LANES
+    block, to_south, to_north = call(
+        unpack_kernel,
+        [shape_of(FIELDS, rows, LANES), shape_of(FIELDS + 16, wide), shape_of(2 * FIELDS + 16, wide)],
+        4,
+        smem=(0,),
+    )(info, received, lines, fringe)
+    to_south, to_north, late = lax.optimization_barrier((to_south, to_north, info))
+    above = moved(to_south, "ice", 1)
+    below = moved(to_north, "ice", -1)
     strip_rows, full = potential_prev.shape
-    own, tile, pair, cross, fringe = call(
+    own, tile, pair, cross = call(
         strip_kernel,
         [
             shape_of(5, strip_rows, full),
             shape_of(5, rows, cols),
             shape_of(rows, full + 3 * cols + cols // 2),
             shape_of(rows, full + cols),
-            shape_of(2, rows, cols),
         ],
         13,
         scratch=[
@@ -665,26 +708,10 @@
         + [pltpu.SemaphoreType.DMA((12,))],
         smem=(0,),
         far=range(1, 13),
-    )(info, *placed_inputs)
+    )(late, *placed_inputs)
     pair_in = lax.ppermute(pair, "hyd", swap)
     meet = [(2 * index + 1, 2 * index + 2) for index in range(bands - 1)]
     cross_in = lax.ppermute(cross, AXES, meet + [(high, low) for low, high in meet])
-    roots, lines, force, fric, cover = call(
-        root_kernel,
-        [shape_of(layers, rows, cols), shape_of(3, FIELDS, cols), shape_of(2, rows, cols), shape_of(rows, cols), shape_of(rows, cols)],
-        5,
-        scratch=buffers(cols) + [pltpu.SemaphoreType.DMA((cols // FETCH, 5))],
-        far=range(5),
-    )(*raw)
-    wide = cols + LANES
-    block, to_south, to_north = call(
-        unpack_kernel,
-        [shape_of(FIELDS, rows, LANES), shape_of(FIELDS + 16, wide), shape_of(2 * FIELDS + 16, wide)],
-        4,
-        smem=(0,),
-    )(info, received, lines, fringe)
-    above = moved(to_south, "ice", 1)
-    below = moved(to_north, "ice", -1)
     count = lax.axis_size("ice") * lax.axis_size("hyd")
     image, sums = call(
         operator_kernel,
@@ -699,6 +726,7 @@
         ],
     )(roots, force, fric, cover, block, above, below, lines)
     gathered = lax.all_to_all(sums, AXES, 0, 0, tiled=True)
+    weights = call(weights_kernel, shape_of(2, 8, LANES), 1)(gathered)
     low, plan = call(
         assemble_kernel,
         [shape_of(6, rows, full), shape_of(10, rows, full)],
@@ -706,10 +734,9 @@
         scratch=[pltpu.VMEM((5, rows, full), F32), pltpu.VMEM((5, rows, full), F32)],
         smem=(0,),
     )(info, own, tile, pair_in, cross_in, above, below)
-    weights, potential, sheet_next, keep, give = call(
+    potential, sheet_next, keep, give = call(
         hydrology_kernel,
         [
-            shape_of(2, 8, LANES),
             shape_of(strip_rows, full),
             shape_of(strip_rows, full),
             shape_of(strip_rows, cols),
@@ -718,7 +745,7 @@
         4,
         scratch=[pltpu.VMEM((rows, full), F32)] * 3 + [pltpu.VMEM((strip_rows, full), F32)],
         smem=(0,),
-    )(info, gathered, low, plan)
+    )(info, weights, low, plan)
     got = lax.ppermute(give, "hyd", swap)
     velocity = pl.pallas_call(
         velocity_kernel,
@@ -738,6 +765,7 @@
     tiles = P("ice", "hyd")
     layered = P(None, "ice", "hyd")
     strips = P(("ice", "hyd"), None)
+
     return jax.shard_map(
         body,
         mesh=mesh,

time: 112 us -> 80.1 us (0.72)
  the two profiles are of different devices: /device:TPU:16 before, /device:TPU:0 now
where the time goes in v3:
time: 80.1 us; the launch traced here: 79.9 us
  blocking collectives  36 us (45%)
  Pallas kernels  30.5 us (38%)
  starting transfers between devices  9.74 us (12%)
  waiting for transfers between devices  2.07 us (3%)
    all_to_all x1, blocking collectives, body(): gathered = lax.all_to_all(sums, AXES, 0, 0, tiled=True)  36 us
    pallas_call x1, Pallas kernels, body(): call(operator_kernel, [shape_of(2, layers, rows, cols), shape_of(count, 1...  13.2 us
    ppermute x2, starting transfers between devices, moved(): lax.ppermute(value, axis, [(source, source + steps) for source in range(l...  6.23 us
    pallas_call x1, Pallas kernels, body(): call(strip_kernel, [shape_of(5, strip_rows, full), shape_of(5, rows, cols...  3.41 us
    pallas_call x1, Pallas kernels, body(): pl.pallas_call(velocity_kernel, out_shape=shape_of(2, layers, rows, cols)...  3.39 us
    pallas_call x1, Pallas kernels, body(): call(root_kernel, [shape_of(layers, rows, cols), shape_of(3, FIELDS, cols...  3.31 us
    pallas_call x1, Pallas kernels, body(): call(assemble_kernel, [shape_of(6, rows, full), shape_of(10, rows, full)]...  2.44 us
    pallas_call x1, Pallas kernels, body(): call(hydrology_kernel, [shape_of(strip_rows, full), shape_of(strip_rows,...  2.24 us
  transfers between devices with their start and end apart: 6, of which 2 were waited for; matrix products, arithmetic and copies ran while one was open for 0% of the time, Pallas kernels for 25%

profile of v3, /device:TPU:0, one launch (start us, length us, event | category | flops | bytes accessed | tf_op | source)
XLA Modules:
  0.0 79.9 jit_solution(17877407642895881368)
XLA Ops:
  0.6 0.1 pad_add_fusion.half.info
  0.7 1.6 %shard_map.148 = f32[16,128]{1,0:T(8,128)S(1)} custom-call(s32[3]{0:T(128)S(1)} %pad_add_fusion.half.info, bf16[20,16,3072]{2,1,0:T(8,128)(2,1)} %refs_6_.1, f32[2,16,3072]{2,1,0:T(8,128)} %refs_7_.1, s32[16,3072]{1,0:T(8,128)} %refs_8_.1, s32[16,3072]{1,0:T(8,128)} %refs_9_.1, f32[16,3072]{1,0:T(8,128)} %refs_10_.1), custom_call_target="tpu_custom_call" | custom-call | tf_op jit(solution)/shard_map/pallas_call | solution.py:668
  2.3 1.8 %collective-permute-start = (f32[16,128]{1,0:T(8,128)S(1)}, f32[16,128]{1,0:T(8,128)S(1)}, u32[]{:S(2)}, u32[]{:S(2)}) collective-permute-start(f32[16,128]{1,0:T(8,128)S(1)} %shard_map.148), channel_id=1, source_target_pairs={{0,1},{1,0},{2,3},{3,2},{4,5},{5,4},{6,7},{7,6},{8,9},{9,8},{10,11... | collective-permute-start | bytes 24584 | tf_op jit(solution)/shard_map/ppermute | solution.py:676
  4.1 3.3 %shard_map.147 = (f32[20,16,3072]{2,1,0:T(8,128)S(1)}, f32[3,24,3072]{2,1,0:T(8,128)S(1)}, f32[2,16,3072]{2,1,0:T(8,128)S(1)}, f32[16,3072]{1,0:T(8,128)S(1)}, f...) custom-call(bf16[20,16,3072]{2,1,0:T(8,128)(2,1)} %refs_6_.1, f32[2,16,3072]{2,1,0:T(8,128)} %refs_7_.1, ...), custom_call_target="tpu_custom_call" | custom-call | tf_op jit(solution)/shard_map/pallas_call | solution.py:677
  7.4 0.0 collective-permute-done.message
  7.4 0.7 shard_map.149
  8.1 3.4 %shard_map.153 = (f32[5,8,6144]{2,1,0:T(8,128)S(1)}, f32[5,16,3072]{2,1,0:T(8,128)S(1)}, f32[16,16896]{1,0:T(8,128)S(1)}, f32[16,9216]{1,0:T(8,128)S(1)}) custom-call(s32[3]{0:T(128)S(1)} %pad_add_fusion.half.info, f32[8,6144]{1,0:T(8,128)} %refs_0_.1, f32[8,6144]{1,0:T(8,128)} %refs_1_.1, f32[8,6144]{1,0:T(8,128)} %refs_2_.1, s32[8,6144]{1,0:T(8,128)} %refs_3_.1, ...), custom_call_target="tpu_custom_call" | custom-call | tf_op jit(solution)/shard_map/pallas_call | solution.py:695
  11.5 0.4 collective-permute-start.3
  11.9 1.3 %collective-permute-start.2 = (f32[64,3200]{1,0:T(8,128)S(1)}, f32[64,3200]{1,0:T(8,128)S(1)}, u32[]{:S(2)}, u32[]{:S(2)}) collective-permute-start(f32[64,3200]{1,0:T(8,128)S(1)} %get-tuple-element.38), channel_id=1, source_target_pairs={{2,0},{4,2},{6,4},{8,6},{10,8},{12,10},{14,12},{16,14},{18,16},{20... | collective-permute-start | bytes 2457608 | tf_op jit(solution)/shard_map/ppermute | solution.py:625
  13.2 0.7 collective-permute-start.4
  13.9 4.9 %collective-permute-start.1 = (f32[40,3200]{1,0:T(8,128)S(1)}, f32[40,3200]{1,0:T(8,128)S(1)}, u32[]{:S(2)}, u32[]{:S(2)}) collective-permute-start(f32[40,3200]{1,0:T(8,128)S(1)} %get-tuple-element.37), channel_id=1, source_target_pairs={{0,2},{2,4},{4,6},{6,8},{8,10},{10,12},{12,14},{14,16},{16,18},{18... | collective-permute-start | bytes 1536008 | tf_op jit(solution)/shard_map/ppermute | solution.py:625
  18.9 1.5 %collective-permute-done.1.above = f32[40,3200]{1,0:T(8,128)S(1)} collective-permute-done((f32[40,3200]{1,0:T(8,128)S(1)}, f32[40,3200]{1,0:T(8,128)S(1)}, u32[]{:S(2)}, u32[]{:S(2)}) %collective-permute-start.1) | collective-permute-done | bytes 512032 | tf_op jit(solution)/shard_map/ppermute | solution.py:625
  20.4 0.0 collective-permute-done.2.below
  20.4 13.2 %shard_map.150 = (f32[2,20,16,3072]{3,2,1,0:T(8,128)S(1)}, f32[128,1,128]{2,1,0:T(1,128)S(1)}) custom-call(f32[20,16,3072]{2,1,0:T(8,128)S(1)} %get-tuple-element.28.roots, f32[2,16,3072]{2,1,0:T(8,128)S(1)} %get-tuple-element.29.force, f32[16,3072]{1,0:T(8,128)S(1)} %get-tuple-element.30.fric, f32[16,3072]{1,0:T(8,128)S(1)} %get-tuple-element.31.mask, ...), custom_call_target="tpu_custom_call" | custom-call | tf_op jit(solution)/shard_map/pallas_call | solution.py:716
  33.6 36.0 %all_to_all.5.gathered = f32[128,1,128]{2,1,0:T(1,128)S(1)} all-to-all(f32[128,1,128]{2,1,0:T(1,128)S(1)} %get-tuple-element.39), channel_id=1, replica_groups=mesh['ice'=64,'hyd'=2] {'ice','hyd'}, dimensions={0} | all-to-all | bytes 131072 | tf_op jit(solution)/shard_map/all_to_all | solution.py:728
  69.6 0.2 shard_map.151.weights
  69.9 0.0 collective-permute-done.4.cross
  69.9 0.0 collective-permute-done.3.pair
  69.9 2.4 %shard_map.154 = (f32[6,16,6144]{2,1,0:T(8,128)S(1)}, f32[10,16,6144]{2,1,0:T(8,128)S(1)}) custom-call(s32[3]{0:T(128)S(1)} %pad_add_fusion.half.info, f32[5,8,6144]{2,1,0:T(8,128)S(1)} %get-tuple-element.42.own, f32[5,16,3072]{2,1,0:T(8,128)S(1)} %get-tuple-element.43.tile, f32[16,16896]{1,0:T(8,128)S(1)} %collective-permute-done.3.pair, ...), custom_call_target="tpu_custom_call" | custom-call | tf_op jit(solution)/shard_map/pallas_call | solution.py:730
  72.3 2.2 %shard_map.155 = (f32[8,6144]{1,0:T(8,128)}, f32[8,6144]{1,0:T(8,128)}, f32[8,3072]{1,0:T(8,128)S(1)}, f32[8,3072]{1,0:T(8,128)S(1)}) custom-call(s32[3]{0:T(128)S(1)} %pad_add_fusion.half.info, f32[2,8,128]{2,1,0:T(8,128)S(1)} %shard_map.151.weights, f32[6,16,6144]{2,1,0:T(8,128)S(1)} %get-tuple-element.46.low, f32[10,16,6144]{2,1,0:T(8,128)S(1)} %get-tuple-element.47.plan), custom_call_target="tpu_custom_call" | custom-call | tf_op jit(solution)/shard_map/pallas_call | solution.py:737
  74.6 0.6 collective-permute-start.5
  75.2 3.4 %shard_map.152 = f32[2,20,16,3072]{3,2,1,0:T(8,128)} custom-call(f32[2,8,128]{2,1,0:T(8,128)S(1)} %shard_map.151.weights, f32[2,16,3072]{2,1,0:T(8,128)S(1)} %get-tuple-element.29.force, f32[2,20,16,3072]{3,2,1,0:T(8,128)S(1)} %get-tuple-element.40.image), custom_call_target="tpu_custom_call" | custom-call | tf_op jit(solution)/shard_map/pallas_call | solution.py:750
  78.6 0.6 collective-permute-done.5
  79.2 0.7 pad_maximum_fusion
  (1 shorter events, 0.0 us)
Async XLA Ops:
  2.3 5.1 %collective-permute-start = (f32[16,128]{1,0:T(8,128)S(1)}, f32[16,128]{1,0:T(8,128)S(1)}, u32[]{:S(2)}, u32[]{:S(2)}) collective-permute-start(f32[16,128]{1,0:T(8,128)S(1)} %shard_map.148), channel_id=1, source_target_pairs={{0,1},{1,0},{2,3},{3,2},{4,5},{5,4},{6,7},{7,6},{8,9},{9,8},{10,11... | collective-permute-start | bytes 24584 | tf_op jit(solution)/shard_map/ppermute | solution.py:676
  11.5 58.3 %collective-permute-start.3 = (f32[16,16896]{1,0:T(8,128)S(1)}, f32[16,16896]{1,0:T(8,128)S(1)}, u32[]{:S(2)}, u32[]{:S(2)}) collective-permute-start(f32[16,16896]{1,0:T(8,128)S(1)} %get-tuple-element.44), channel_id=1, source_target_pairs={{0,1},{1,0},{2,3},{3,2},{4,5},{5,4},{6,7},{7,6},{8,9},{9,8},{10,11... | collective-permute-start | bytes 3244040 | tf_op jit(solution)/shard_map/ppermute | solution.py:712
  11.9 8.4 %collective-permute-start.2 = (f32[64,3200]{1,0:T(8,128)S(1)}, f32[64,3200]{1,0:T(8,128)S(1)}, u32[]{:S(2)}, u32[]{:S(2)}) collective-permute-start(f32[64,3200]{1,0:T(8,128)S(1)} %get-tuple-element.38), channel_id=1, source_target_pairs={{2,0},{4,2},{6,4},{8,6},{10,8},{12,10},{14,12},{16,14},{18,16},{20... | collective-permute-start | bytes 2457608 | tf_op jit(solution)/shard_map/ppermute | solution.py:625
  13.2 56.6 %collective-permute-start.4 = (f32[16,9216]{1,0:T(8,128)S(1)}, f32[16,9216]{1,0:T(8,128)S(1)}, u32[]{:S(2)}, u32[]{:S(2)}) collective-permute-start(f32[16,9216]{1,0:T(8,128)S(1)} %get-tuple-element.45), channel_id=1, source_target_pairs={{1,2},{3,4},{5,6},{7,8},{9,10},{11,12},{13,14},{15,16},{17,18},{19... | collective-permute-start | bytes 1769480 | tf_op jit(solution)/shard_map/ppermute | solution.py:714
  13.9 6.4 %collective-permute-start.1 = (f32[40,3200]{1,0:T(8,128)S(1)}, f32[40,3200]{1,0:T(8,128)S(1)}, u32[]{:S(2)}, u32[]{:S(2)}) collective-permute-start(f32[40,3200]{1,0:T(8,128)S(1)} %get-tuple-element.37), channel_id=1, source_target_pairs={{0,2},{2,4},{4,6},{6,8},{8,10},{10,12},{12,14},{14,16},{16,18},{18... | collective-permute-start | bytes 1536008 | tf_op jit(solution)/shard_map/ppermute | solution.py:625
  74.6 4.6 %collective-permute-start.5 = (f32[8,3072]{1,0:T(8,128)S(1)}, f32[8,3072]{1,0:T(8,128)S(1)}, u32[]{:S(2)}, u32[]{:S(2)}) collective-permute-start(f32[8,3072]{1,0:T(8,128)S(1)} %get-tuple-element.49), channel_id=1, source_target_pairs={{0,1},{1,0},{2,3},{3,2},{4,5},{5,4},{6,7},{7,6},{8,9},{9,8},{10,11... | collective-permute-start | bytes 294920 | tf_op jit(solution)/shard_map/ppermute | solution.py:749

commit v4 on v3

--- a/solution.py
+++ b/solution.py
@@ -9,7 +9,6 @@
 
 
 HYD_ITERS = 3
-vertical_weight = 4.0
 relax_weight = 0.1
 melt_factor = 0.5
 sheet_conduct = 2.0
@@ -54,16 +53,6 @@
 def west_of(value, left):
     joined = jnp.concatenate([left, value], axis=1)
     return pltpu.roll(joined, 1, 1)[:, LANES:]
-
-
-def south_of(value, below):
-    rows, cols = value.shape
-    return jnp.where(row_index(rows, cols) == rows - 1, below, pltpu.roll(value, rows - 1, 0))
-
-
-def north_of(value, above):
-    rows, cols = value.shape
-    return jnp.where(row_index(rows, cols) == 0, above, pltpu.roll(value, 1, 0))
 
 
 def root(weight):
@@ -211,130 +200,219 @@
     return (1.0 - cover) + relax_weight * cover
 
 
-def operator_kernel(
-    roots, force, fric, mask, block, above, below, lines, image, sums, slopes, scaled, diag, line, edge
+def south_rows(value, below):
+    upper, lower = value[0:8], value[8:16]
+    last = row_index(8, value.shape[1]) == 7
+    next_row = pltpu.roll(lower, 7, 0)
+    return jnp.concatenate(
+        [jnp.where(last, next_row, pltpu.roll(upper, 7, 0)), jnp.where(last, below, next_row)], axis=0
+    )
+
+
+def north_rows(value, above):
+    upper, lower = value[0:8], value[8:16]
+    first = row_index(8, value.shape[1]) == 0
+    previous = pltpu.roll(upper, 1, 0)
+    return jnp.concatenate(
+        [jnp.where(first, above, previous), jnp.where(first, previous, pltpu.roll(lower, 1, 0))], axis=0
+    )
+
+
+def columns(read_own, read_block, start, size, cols, rows):
+    if start == cols:
+        return read_block(), read_own(slice(cols - LANES, cols)), jnp.zeros((rows, LANES), F32)
+    left = read_own(slice(start - LANES, start)) if start else read_block()
+    stop = start + size
+    right = read_own(slice(stop, stop + LANES)) if stop < cols else read_block()
+    return read_own(slice(start, stop)), left, right
+
+
+def image_kernel(roots, force, fric, mask, block, image, to_east, to_south, slopes, scaled):
+    layers, rows, cols = roots.shape
+    chunks = [(start, CHUNK) for start in range(0, cols, CHUNK)]
+    for start, size in chunks:
+        part = slice(start, start + size)
+        nothing = jnp.zeros((1, size), F32)
+        plain = relax(mask[:, part])
+        for comp, (col_factor, row_factor) in enumerate(FACTORS):
+            here, left, right = columns(
+                lambda cut, comp=comp: force[comp, :, cut],
+                lambda comp=comp: block[F0 + comp],
+                start,
+                size,
+                cols,
+                rows,
+            )
+            slopes[4 * comp, :, part] = col_factor * (here - east_of(here, right))
+            slopes[4 * comp + 1, :, part] = col_factor * (here - west_of(here, left))
+            slopes[4 * comp + 2, :, part] = row_factor * (here - south_rows(here, nothing))
+            slopes[4 * comp + 3, :, part] = row_factor * (here - north_rows(here, nothing))
+            scaled[0, comp, :, part] = plain * here
+            scaled[1, comp, :, part] = (plain + fric[:, part]) * here
+
+    def layer_step(layer, carry):
+        kind = jnp.where(layer == 0, 1, 0)
+        for start, size in chunks:
+            part = slice(start, start + size)
+            nothing = jnp.zeros((1, size), F32)
+            here, left, right = columns(
+                lambda cut: roots[layer, :, cut], lambda: block[layer], start, size, cols, rows
+            )
+            east = here * east_of(here, right)
+            west = here * west_of(here, left)
+            south = here * south_rows(here, nothing)
+            north = north_rows(south, nothing)
+            to_east[layer, :, part] = east
+            to_south[layer, :, part] = south
+            for comp in range(2):
+                image[comp, layer, :, part] = scaled[kind, comp, :, part] + (
+                    east * slopes[4 * comp, :, part]
+                    + west * slopes[4 * comp + 1, :, part]
+                    + south * slopes[4 * comp + 2, :, part]
+                    + north * slopes[4 * comp + 3, :, part]
+                )
+        return carry
+
+    lax.fori_loop(0, layers, layer_step, 0)
+
+
+def moment_kernel(
+    roots,
+    force,
+    fric,
+    mask,
+    block,
+    above,
+    below,
+    lines,
+    started,
+    to_east,
+    faces_before,
+    image,
+    faces,
+    sums,
+    line,
+    edge,
+    repair,
+    outer,
+    totals,
 ):
     layers, rows, cols = roots.shape
     chunks = [(start, CHUNK) for start in range(0, cols, CHUNK)]
-
-    def columns(read_own, read_block, start, size):
-        if start == cols:
-            return read_block(), read_own(slice(cols - LANES, cols)), jnp.zeros((rows, LANES), F32)
-        left = read_own(slice(start - LANES, start)) if start else read_block()
-        stop = start + size
-        right = read_own(slice(stop, stop + LANES)) if stop < cols else read_block()
-        return read_own(slice(start, stop)), left, right
-
-    squares = jnp.zeros((8, LANES), F32)
-    for start, size in chunks + [(cols, LANES)]:
-        part = slice(start, start + size)
-        own = start < cols
-        cover = mask[:, part] if own else block[MASK]
-        drag = fric[:, part] if own else block[FG]
-        plain = relax(cover)
-        if own:
-            diag[0, :, part] = plain
-            diag[1, :, part] = plain + drag
-        for comp, (col_factor, row_factor) in enumerate(FACTORS):
-            here, left, right = columns(
-                lambda cut, comp=comp: force[comp, :, cut], lambda comp=comp: block[F0 + comp], start, size
-            )
-            up = above[F0 + comp : F0 + comp + 1, part]
-            down = below[F0 + comp : F0 + comp + 1, part]
-            slopes[4 * comp, :, part] = col_factor * (here - east_of(here, right))
-            slopes[4 * comp + 1, :, part] = col_factor * (here - west_of(here, left))
-            slopes[4 * comp + 2, :, part] = row_factor * (here - south_of(here, down))
-            slopes[4 * comp + 3, :, part] = row_factor * (here - north_of(here, up))
-            scaled[0, comp, :, part] = plain * here
-            scaled[1, comp, :, part] = (plain + drag) * here
-            if own:
-                squares += fold(here * here)
+    block_part = slice(cols, cols + LANES)
 
     for start, size in chunks:
         part = slice(start, start + size)
         stop = start + size
-        before = slice(start - LANES, start) if start else slice(cols, cols + LANES)
+        before = slice(start - LANES, start) if start else block_part
         after = slice(stop, stop + LANES)
         here = below[0:layers, part]
+        top = lines[0, 0:layers, part] * above[0:layers, part]
+        north = here * lines[2, 0:layers, part]
+        outer[0:layers, part] = north
         east = here * east_of(here, below[0:layers, after])
         west = here * west_of(here, below[0:layers, before])
         south = here * below[FIELDS : FIELDS + layers, part]
-        north = here * lines[2, 0:layers, part]
-        cover = below[MASK : MASK + 1, part]
         drag = jnp.where(row_index(layers, size) == 0, below[FG : FG + 1, part], 0.0)
-        full = relax(cover) + drag
+        full = relax(below[MASK : MASK + 1, part]) + drag
         for comp, (col_factor, row_factor) in enumerate(FACTORS):
             row = slice(F0 + comp, F0 + comp + 1)
             under = slice(FIELDS + F0 + comp, FIELDS + F0 + comp + 1)
             mid = below[row, part]
+            rise = row_factor * (mid - lines[2, row, part])
+            repair[comp, 0:layers, part] = top * (row_factor * (lines[0, row, part] - above[row, part]))
+            repair[2 + comp, 0:layers, part] = north * (-rise)
             line[comp, 0:layers, part] = full * mid + (
                 col_factor
                 * (
                     east * (mid - east_of(mid, below[row, after]))
                     + west * (mid - west_of(mid, below[row, before]))
                 )
-                + row_factor
-                * (south * (mid - below[under, part]) + north * (mid - lines[2, row, part]))
+                + (row_factor * south * (mid - below[under, part]) + north * rise)
             )
+        for index in range(3):
+            totals[index, :, part] = jnp.zeros((rows, size), F32)
+
+    nothing = jnp.zeros((rows, LANES), F32)
+    side_slopes = []
+    for comp, (col_factor, row_factor) in enumerate(FACTORS):
+        here = block[F0 + comp]
+        left = force[comp, :, cols - LANES : cols]
+        up = above[F0 + comp : F0 + comp + 1, block_part]
+        down = below[F0 + comp : F0 + comp + 1, block_part]
+        side_slopes.append(
+            (
+                col_factor * (here - east_of(here, nothing)),
+                col_factor * (here - west_of(here, left)),
+                row_factor * (here - south_rows(here, down)),
+                row_factor * (here - north_rows(here, up)),
+            )
+        )
+    side_plain = relax(block[MASK])
 
     def layer_step(layer, carry):
-        kind = jnp.where(layer == 0, 1, 0)
         lower = jnp.maximum(layer - 1, 0)
-        for start, size in chunks + [(cols, LANES)]:
+        here = block[layer]
+        east = here * east_of(here, nothing)
+        west = here * west_of(here, roots[layer, :, cols - LANES : cols])
+        south = here * south_rows(here, line_of(below, layer, cols, LANES))
+        north = here * north_rows(here, line_of(above, layer, cols, LANES))
+        full = side_plain + jnp.where(layer == 0, 1.0, 0.0) * block[FG]
+        for comp in range(2):
+            slope = side_slopes[comp]
+            edge[comp] = full * block[F0 + comp] + (
+                (east * slope[0] + west * slope[1]) + (south * slope[2] + north * slope[3])
+            )
+        for start, size in chunks:
             part = slice(start, start + size)
-            here, left, right = columns(
-                lambda cut: roots[layer, :, cut], lambda: block[layer], start, size
-            )
-            east = east_of(here, right)
-            west = west_of(here, left)
-            south = south_of(here, line_of(below, layer, start, size))
-            north = north_of(here, line_of(above, layer, start, size))
+            faces[layer, rows - 1 : rows, part] = outer[pl.ds(layer, 1), part]
             for comp in range(2):
-                flux = (
-                    east * slopes[4 * comp, :, part]
-                    + west * slopes[4 * comp + 1, :, part]
-                    + south * slopes[4 * comp + 2, :, part]
-                    + north * slopes[4 * comp + 3, :, part]
+                image[comp, layer, 0:1, part] = (
+                    image[comp, layer, 0:1, part] + repair[comp, pl.ds(layer, 1), part]
                 )
-                value = scaled[kind, comp, :, part] + here * flux
-                if start < cols:
-                    image[comp, layer, :, part] = value
-                else:
-                    edge[comp] = value
-        cross, square, energy = carry
+                image[comp, layer, rows - 1 : rows, part] = (
+                    image[comp, layer, rows - 1 : rows, part] + repair[2 + comp, pl.ds(layer, 1), part]
+                )
+        quads, singles = carry
         for start, size in chunks:
             part = slice(start, start + size)
             stop = start + size
-            here = roots[layer, :, part]
-            right = roots[layer, :, stop : stop + LANES] if stop < cols else block[layer]
-            east = east_of(here, right)
-            south = south_of(here, line_of(below, layer, start, size))
-            beneath = roots[lower, :, part]
-            to_east, to_south, to_lower, size_sq, product = 0.0, 0.0, 0.0, 0.0, 0.0
-            for comp, (col_factor, row_factor) in enumerate(FACTORS):
+            east = to_east[layer, :, part]
+            south = faces[layer, :, part]
+            down = roots[layer, :, part] * roots[lower, :, part]
+            squares, falls = [], []
+            lows, length = None, None
+            for comp in range(2):
                 value = image[comp, layer, :, part]
                 right = image[comp, layer, :, stop : stop + LANES] if stop < cols else edge[comp]
                 step = value - east_of(value, right)
-                step = step * step
-                to_east += step if col_factor == 1.0 else col_factor * step
-                step = value - south_of(value, line_of(line.at[comp], layer, start, size))
-                step = step * step
-                to_south += step if row_factor == 1.0 else row_factor * step
+                squares.append(step * step)
+                step = value - south_rows(value, line[comp, pl.ds(layer, 1), part])
+                falls.append(step * step)
                 step = value - image[comp, lower, :, part]
-                to_lower += step * step
-                size_sq += value * value
-                product += value * force[comp, :, part]
-            faces = here * (east * to_east + south * to_south + beneath * (vertical_weight * to_lower))
-            cross += fold(product)
-            square += fold(size_sq)
-            energy += fold(faces + diag[kind, :, part] * size_sq)
-        return cross, square, energy
+                lows = step * step if lows is None else lows + step * step
+                length = value * value if length is None else length + value * value
+                totals[comp, :, part] += value
+            totals[2, :, part] += length
+            quads += fold(east * squares[0] + south * falls[1] + down * lows)
+            singles += fold(east * squares[1] + south * falls[0])
+        return quads, singles
 
     zero = jnp.zeros((8, LANES), F32)
-    cross, square, energy = lax.fori_loop(0, layers, layer_step, (zero, zero, zero))
+    quads, singles = lax.fori_loop(0, layers, layer_step, (zero, zero))
+    norm, cross, square, energy = zero, zero, zero, 4.0 * quads + singles
+    for start, size in chunks:
+        part = slice(start, start + size)
+        one, two = force[0, :, part], force[1, :, part]
+        norm += fold(one * one + two * two)
+        cross += fold(one * totals[0, :, part] + two * totals[1, :, part])
+        length = totals[2, :, part]
+        square += fold(length)
+        one, two = image[0, 0, :, part], image[1, 0, :, part]
+        energy += fold(relax(mask[:, part]) * length + fric[:, part] * (one * one + two * two))
     lane = lane_index(1, LANES)
     packed = jnp.zeros((1, LANES), F32)
-    for index, part in enumerate((layers * squares, cross, square, energy)):
+    for index, part in enumerate((layers * norm, cross, square, energy)):
         packed = jnp.where(lane == index, jnp.sum(part), packed)
     sums[...] = jnp.broadcast_to(packed[None], sums.shape)
 
@@ -673,24 +751,8 @@
         smem=(0,),
         far=range(1, 6),
     )(info, *raw)
+    message, late = lax.optimization_barrier((message, info))
     received = lax.ppermute(message, "hyd", swap)
-    roots, lines, force, fric, cover, fringe = call(
-        root_kernel,
-        [shape_of(layers, rows, cols), shape_of(3, FIELDS, cols), shape_of(2, rows, cols), shape_of(rows, cols), shape_of(rows, cols), shape_of(2, rows, cols)],
-        6,
-        scratch=buffers(cols) + [pltpu.VMEM((rows, cols), F32), pltpu.SemaphoreType.DMA((cols // FETCH, 6))],
-        far=range(6),
-    )(*placed_inputs[6:])
-    wide = cols + LANES
-    block, to_south, to_north = call(
-        unpack_kernel,
-        [shape_of(FIELDS, rows, LANES), shape_of(FIELDS + 16, wide), shape_of(2 * FIELDS + 16, wide)],
-        4,
-        smem=(0,),
-    )(info, received, lines, fringe)
-    to_south, to_north, late = lax.optimization_barrier((to_south, to_north, info))
-    above = moved(to_south, "ice", 1)
-    below = moved(to_north, "ice", -1)
     strip_rows, full = potential_prev.shape
     own, tile, pair, cross = call(
         strip_kernel,
@@ -710,21 +772,45 @@
         far=range(1, 13),
     )(late, *placed_inputs)
     pair_in = lax.ppermute(pair, "hyd", swap)
+    roots, lines, force, fric, cover, fringe = call(
+        root_kernel,
+        [shape_of(layers, rows, cols), shape_of(3, FIELDS, cols), shape_of(2, rows, cols), shape_of(rows, cols), shape_of(rows, cols), shape_of(2, rows, cols)],
+        6,
+        scratch=buffers(cols) + [pltpu.VMEM((rows, cols), F32), pltpu.SemaphoreType.DMA((cols // FETCH, 6))],
+        far=range(6),
+    )(*placed_inputs[6:])
+    wide = cols + LANES
+    block, to_south, to_north = call(
+        unpack_kernel,
+        [shape_of(FIELDS, rows, LANES), shape_of(FIELDS + 16, wide), shape_of(2 * FIELDS + 16, wide)],
+        4,
+        smem=(0,),
+    )(info, received, lines, fringe)
+    above = moved(to_south, "ice", 1)
+    below = moved(to_north, "ice", -1)
+    strip_rows, full = potential_prev.shape
     meet = [(2 * index + 1, 2 * index + 2) for index in range(bands - 1)]
     cross_in = lax.ppermute(cross, AXES, meet + [(high, low) for low, high in meet])
     count = lax.axis_size("ice") * lax.axis_size("hyd")
-    image, sums = call(
-        operator_kernel,
-        [shape_of(2, layers, rows, cols), shape_of(count, 1, LANES)],
-        8,
+    started, to_east, faces = call(
+        image_kernel,
+        [shape_of(2, layers, rows, cols), shape_of(layers, rows, cols), shape_of(layers, rows, cols)],
+        5,
+        scratch=[pltpu.VMEM((8, rows, cols), F32), pltpu.VMEM((2, 2, rows, cols), F32)],
+    )(roots, force, fric, cover, block)
+    image, faces, sums = call(
+        moment_kernel,
+        [shape_of(2, layers, rows, cols), shape_of(layers, rows, cols), shape_of(count, 1, LANES)],
+        11,
         scratch=[
-            pltpu.VMEM((8, rows, wide), F32),
-            pltpu.VMEM((2, 2, rows, wide), F32),
-            pltpu.VMEM((2, rows, cols), F32),
             pltpu.VMEM((2, FIELDS, cols), F32),
             pltpu.VMEM((2, rows, LANES), F32),
+            pltpu.VMEM((4, FIELDS, cols), F32),
+            pltpu.VMEM((FIELDS, cols), F32),
+            pltpu.VMEM((3, rows, cols), F32),
         ],
-    )(roots, force, fric, cover, block, above, below, lines)
+        input_output_aliases={8: 0, 10: 1},
+    )(roots, force, fric, cover, block, above, below, lines, started, to_east, faces)
     gathered = lax.all_to_all(sums, AXES, 0, 0, tiled=True)
     weights = call(weights_kernel, shape_of(2, 8, LANES), 1)(gathered)
     low, plan = call(

time: 80.1 us -> 94.5 us (1.18)
  waiting for transfers between devices: 2.07 us -> 21 us
  blocking collectives: 36 us -> 32.5 us
  Pallas kernels: 30.5 us -> 29.5 us
    ppermute x1, waiting for transfers between devices: 0.01 us -> 20.4 us  [body(): received = lax.ppermute(message, 'hyd', swap)]
    all_to_all x1, blocking collectives: 36 us -> 32.5 us  [body(): gathered = lax.all_to_all(sums, AXES, 0, 0, tiled=True)]
    ppermute x2, waiting for transfers between devices: 1.47 us -> 0.01 us  [moved(): lax.ppermute(value, axis, [(source, source + steps) for source in range(l...]
    ppermute x1, starting transfers between devices: 1.77 us -> 0.34 us  [body(): received = lax.ppermute(message, 'hyd', swap)]
    ppermute x1, starting transfers between devices: 0.42 us -> 1.77 us  [body(): pair_in = lax.ppermute(pair, 'hyd', swap)]
    pallas_call x1 -> x2, Pallas kernels: 13.2 us -> 12.3 us  [the longest x1 7.47 us: body(): call(moment_kernel, [shape_of(2, layers, rows, cols), shape_of(layers, ro...]
  transfers between devices with their start and end apart: 6 -> 6, of which waited for: 2 -> 2; matrix products, arithmetic and copies ran while one was open for 0% -> 0% of each run, Pallas kernels for 25% -> 21%
where the time goes in v4:
time: 94.5 us; the launch traced here: 94.2 us
  blocking collectives  32.5 us (34%)
  Pallas kernels  29.5 us (31%)
  waiting for transfers between devices  21 us (22%)
  starting transfers between devices  9.73 us (10%)
    all_to_all x1, blocking collectives, body(): gathered = lax.all_to_all(sums, AXES, 0, 0, tiled=True)  32.5 us
    ppermute x1, waiting for transfers between devices, body(): received = lax.ppermute(message, 'hyd', swap)  20.4 us
    pallas_call x1, Pallas kernels, body(): call(moment_kernel, [shape_of(2, layers, rows, cols), shape_of(layers, ro...  7.47 us
    ppermute x2, starting transfers between devices, moved(): lax.ppermute(value, axis, [(source, source + steps) for source in range(l...  6.29 us
    pallas_call x1, Pallas kernels, body(): call(image_kernel, [shape_of(2, layers, rows, cols), shape_of(layers, row...  4.8 us
    pallas_call x1, Pallas kernels, body(): call(strip_kernel, [shape_of(5, strip_rows, full), shape_of(5, rows, cols...  3.41 us
    pallas_call x1, Pallas kernels, body(): pl.pallas_call(velocity_kernel, out_shape=shape_of(2, layers, rows, cols)...  3.39 us
    pallas_call x1, Pallas kernels, body(): call(root_kernel, [shape_of(layers, rows, cols), shape_of(3, FIELDS, cols...  3.31 us
  transfers between devices with their start and end apart: 6, of which 2 were waited for; matrix products, arithmetic and copies ran while one was open for 0% of the time, Pallas kernels for 21%

profile of v4, /device:TPU:0, one launch (start us, length us, event | category | flops | bytes accessed | tf_op | source)
XLA Modules:
  0.0 94.2 jit_solution(1219687753319246469)
XLA Ops:
  0.6 0.1 pad_add_fusion.half.info
  0.7 1.6 %shard_map.148 = f32[16,128]{1,0:T(8,128)S(1)} custom-call(s32[3]{0:T(128)S(1)} %pad_add_fusion.half.info, bf16[20,16,3072]{2,1,0:T(8,128)(2,1)} %refs_6_.1, f32[2,16,3072]{2,1,0:T(8,128)} %refs_7_.1, s32[16,3072]{1,0:T(8,128)} %refs_8_.1, s32[16,3072]{1,0:T(8,128)} %refs_9_.1, f32[16,3072]{1,0:T(8,128)} %refs_10_.1), custom_call_target="tpu_custom_call" | custom-call | tf_op jit(solution)/shard_map/pallas_call | solution.py:746
  2.3 3.4 %shard_map.154 = (f32[5,8,6144]{2,1,0:T(8,128)S(1)}, f32[5,16,3072]{2,1,0:T(8,128)S(1)}, f32[16,16896]{1,0:T(8,128)S(1)}, f32[16,9216]{1,0:T(8,128)S(1)}) custom-call(s32[3]{0:T(128)S(1)} %pad_add_fusion.half.info, f32[8,6144]{1,0:T(8,128)} %refs_0_.1, f32[8,6144]{1,0:T(8,128)} %refs_1_.1, f32[8,6144]{1,0:T(8,128)} %refs_2_.1, s32[8,6144]{1,0:T(8,128)} %refs_3_.1, ...), custom_call_target="tpu_custom_call" | custom-call | tf_op jit(solution)/shard_map/pallas_call | solution.py:757
  5.8 1.8 %collective-permute-start.3 = (f32[16,16896]{1,0:T(8,128)S(1)}, f32[16,16896]{1,0:T(8,128)S(1)}, u32[]{:S(2)}, u32[]{:S(2)}) collective-permute-start(f32[16,16896]{1,0:T(8,128)S(1)} %get-tuple-element.48), channel_id=1, source_target_pairs={{0,1},{1,0},{2,3},{3,2},{4,5},{5,4},{6,7},{7,6},{8,9},{9,8},{10,11... | collective-permute-start | bytes 3244040 | tf_op jit(solution)/shard_map/ppermute | solution.py:774
  7.5 0.3 collective-permute-start
  7.9 3.3 %shard_map.147 = (f32[20,16,3072]{2,1,0:T(8,128)S(1)}, f32[3,24,3072]{2,1,0:T(8,128)S(1)}, f32[2,16,3072]{2,1,0:T(8,128)S(1)}, f32[16,3072]{1,0:T(8,128)S(1)}, f...) custom-call(bf16[20,16,3072]{2,1,0:T(8,128)(2,1)} %refs_6_.1, f32[2,16,3072]{2,1,0:T(8,128)} %refs_7_.1, ...), custom_call_target="tpu_custom_call" | custom-call | tf_op jit(solution)/shard_map/pallas_call | solution.py:775
  11.2 20.4 %collective-permute-done.message = f32[16,128]{1,0:T(8,128)S(1)} collective-permute-done((f32[16,128]{1,0:T(8,128)S(1)}, f32[16,128]{1,0:T(8,128)S(1)}, u32[]{:S(2)}, u32[]{:S(2)}) %collective-permute-start) | collective-permute-done | bytes 8224 | tf_op jit(solution)/shard_map/ppermute | solution.py:755
  31.6 0.7 shard_map.149
  32.2 1.3 %collective-permute-start.2 = (f32[64,3200]{1,0:T(8,128)S(1)}, f32[64,3200]{1,0:T(8,128)S(1)}, u32[]{:S(2)}, u32[]{:S(2)}) collective-permute-start(f32[64,3200]{1,0:T(8,128)S(1)} %get-tuple-element.39), channel_id=1, source_target_pairs={{2,0},{4,2},{6,4},{8,6},{10,8},{12,10},{14,12},{16,14},{18,16},{20... | collective-permute-start | bytes 2457608 | tf_op jit(solution)/shard_map/ppermute | solution.py:703
  33.5 0.7 collective-permute-start.4
  34.2 5.0 %collective-permute-start.1 = (f32[40,3200]{1,0:T(8,128)S(1)}, f32[40,3200]{1,0:T(8,128)S(1)}, u32[]{:S(2)}, u32[]{:S(2)}) collective-permute-start(f32[40,3200]{1,0:T(8,128)S(1)} %get-tuple-element.38), channel_id=1, source_target_pairs={{0,2},{2,4},{4,6},{6,8},{8,10},{10,12},{12,14},{14,16},{16,18},{18... | collective-permute-start | bytes 1536008 | tf_op jit(solution)/shard_map/ppermute | solution.py:703
  39.2 4.8 %shard_map.150 = (f32[2,20,16,3072]{3,2,1,0:T(8,128)S(1)}, f32[20,16,3072]{2,1,0:T(8,128)S(1)}, f32[20,16,3072]{2,1,0:T(8,128)S(1)}) custom-call(f32[20,16,3072]{2,1,0:T(8,128)S(1)} %get-tuple-element.30.roots, f32[2,16,3072]{2,1,0:T(8,128)S(1)} %get-tuple-element.31.force, f32[16,3072]{1,0:T(8,128)S(1)} %get-tuple-element.32.fric, ...), custom_call_target="tpu_custom_call" | custom-call | tf_op jit(solution)/shard_map/pallas_call | solution.py:795
  44.0 0.0 collective-permute-done.1.above
  44.1 0.0 collective-permute-done.2.below
  44.1 7.5 %shard_map.151 = (f32[2,20,16,3072]{3,2,1,0:T(8,128)S(1)}, f32[20,16,3072]{2,1,0:T(8,128)S(1)}, f32[128,1,128]{2,1,0:T(1,128)S(1)}) custom-call(f32[20,16,3072]{2,1,0:T(8,128)S(1)} %get-tuple-element.30.roots, f32[2,16,3072]{2,1,0:T(8,128)S(1)} %get-tuple-element.31.force, ...), custom_call_target="tpu_custom_call", output_to_operand_aliasing={{0}: (8, {}), {1}: (10, {})} | custom-call | tf_op jit(solution)/shard_map/pallas_call | solution.py:801
  51.5 32.5 %all_to_all.5.gathered = f32[128,1,128]{2,1,0:T(1,128)S(1)} all-to-all(f32[128,1,128]{2,1,0:T(1,128)S(1)} %get-tuple-element.43), channel_id=1, replica_groups=mesh['ice'=64,'hyd'=2] {'ice','hyd'}, dimensions={0} | all-to-all | bytes 131072 | tf_op jit(solution)/shard_map/all_to_all | solution.py:814
  84.0 0.2 shard_map.152.weights
  84.3 0.0 collective-permute-done.4.cross
  84.3 2.4 %shard_map.155 = (f32[6,16,6144]{2,1,0:T(8,128)S(1)}, f32[10,16,6144]{2,1,0:T(8,128)S(1)}) custom-call(s32[3]{0:T(128)S(1)} %pad_add_fusion.half.info, f32[5,8,6144]{2,1,0:T(8,128)S(1)} %get-tuple-element.46.own, f32[5,16,3072]{2,1,0:T(8,128)S(1)} %get-tuple-element.47.tile, f32[16,16896]{1,0:T(8,128)S(1)} %collective-permute-done.3.pair, ...), custom_call_target="tpu_custom_call" | custom-call | tf_op jit(solution)/shard_map/pallas_call | solution.py:816
  86.7 2.2 %shard_map.156 = (f32[8,6144]{1,0:T(8,128)}, f32[8,6144]{1,0:T(8,128)}, f32[8,3072]{1,0:T(8,128)S(1)}, f32[8,3072]{1,0:T(8,128)S(1)}) custom-call(s32[3]{0:T(128)S(1)} %pad_add_fusion.half.info, f32[2,8,128]{2,1,0:T(8,128)S(1)} %shard_map.152.weights, f32[6,16,6144]{2,1,0:T(8,128)S(1)} %get-tuple-element.50.low, f32[10,16,6144]{2,1,0:T(8,128)S(1)} %get-tuple-element.51.plan), custom_call_target="tpu_custom_call" | custom-call | tf_op jit(solution)/shard_map/pallas_call | solution.py:823
  88.9 0.6 collective-permute-start.5
  89.5 3.4 %shard_map.153 = f32[2,20,16,3072]{3,2,1,0:T(8,128)} custom-call(f32[2,8,128]{2,1,0:T(8,128)S(1)} %shard_map.152.weights, f32[2,16,3072]{2,1,0:T(8,128)S(1)} %get-tuple-element.31.force, f32[2,20,16,3072]{3,2,1,0:T(8,128)S(1)} %get-tuple-element.44.image), custom_call_target="tpu_custom_call" | custom-call | tf_op jit(solution)/shard_map/pallas_call | solution.py:836
  92.9 0.6 collective-permute-done.5
  93.5 0.7 pad_maximum_fusion
  (2 shorter events, 0.0 us)
Async XLA Ops:
  5.8 78.5 %collective-permute-start.3 = (f32[16,16896]{1,0:T(8,128)S(1)}, f32[16,16896]{1,0:T(8,128)S(1)}, u32[]{:S(2)}, u32[]{:S(2)}) collective-permute-start(f32[16,16896]{1,0:T(8,128)S(1)} %get-tuple-element.48), channel_id=1, source_target_pairs={{0,1},{1,0},{2,3},{3,2},{4,5},{5,4},{6,7},{7,6},{8,9},{9,8},{10,11... | collective-permute-start | bytes 3244040 | tf_op jit(solution)/shard_map/ppermute | solution.py:774
  7.5 24.0 %collective-permute-start = (f32[16,128]{1,0:T(8,128)S(1)}, f32[16,128]{1,0:T(8,128)S(1)}, u32[]{:S(2)}, u32[]{:S(2)}) collective-permute-start(f32[16,128]{1,0:T(8,128)S(1)} %shard_map.148), channel_id=1, source_target_pairs={{0,1},{1,0},{2,3},{3,2},{4,5},{5,4},{6,7},{7,6},{8,9},{9,8},{10,11... | collective-permute-start | bytes 24584 | tf_op jit(solution)/shard_map/ppermute | solution.py:755
  32.2 11.8 %collective-permute-start.2 = (f32[64,3200]{1,0:T(8,128)S(1)}, f32[64,3200]{1,0:T(8,128)S(1)}, u32[]{:S(2)}, u32[]{:S(2)}) collective-permute-start(f32[64,3200]{1,0:T(8,128)S(1)} %get-tuple-element.39), channel_id=1, source_target_pairs={{2,0},{4,2},{6,4},{8,6},{10,8},{12,10},{14,12},{16,14},{18,16},{20... | collective-permute-start | bytes 2457608 | tf_op jit(solution)/shard_map/ppermute | solution.py:703
  33.5 50.7 %collective-permute-start.4 = (f32[16,9216]{1,0:T(8,128)S(1)}, f32[16,9216]{1,0:T(8,128)S(1)}, u32[]{:S(2)}, u32[]{:S(2)}) collective-permute-start(f32[16,9216]{1,0:T(8,128)S(1)} %get-tuple-element.49), channel_id=1, source_target_pairs={{1,2},{3,4},{5,6},{7,8},{9,10},{11,12},{13,14},{15,16},{17,18},{19... | collective-permute-start | bytes 1769480 | tf_op jit(solution)/shard_map/ppermute | solution.py:793
  34.2 9.8 %collective-permute-start.1 = (f32[40,3200]{1,0:T(8,128)S(1)}, f32[40,3200]{1,0:T(8,128)S(1)}, u32[]{:S(2)}, u32[]{:S(2)}) collective-permute-start(f32[40,3200]{1,0:T(8,128)S(1)} %get-tuple-element.38), channel_id=1, source_target_pairs={{0,2},{2,4},{4,6},{6,8},{8,10},{10,12},{12,14},{14,16},{16,18},{18... | collective-permute-start | bytes 1536008 | tf_op jit(solution)/shard_map/ppermute | solution.py:703
  88.9 4.6 %collective-permute-start.5 = (f32[8,3072]{1,0:T(8,128)S(1)}, f32[8,3072]{1,0:T(8,128)S(1)}, u32[]{:S(2)}, u32[]{:S(2)}) collective-permute-start(f32[8,3072]{1,0:T(8,128)S(1)} %get-tuple-element.53), channel_id=1, source_target_pairs={{0,1},{1,0},{2,3},{3,2},{4,5},{5,4},{6,7},{7,6},{8,9},{9,8},{10,11... | collective-permute-start | bytes 294920 | tf_op jit(solution)/shard_map/ppermute | solution.py:835

commit v5 on v4

--- a/solution.py
+++ b/solution.py
@@ -1,5 +1,3 @@
-import functools
-
 import jax
 import jax.numpy as jnp
 from jax import lax
@@ -53,6 +51,26 @@
 def west_of(value, left):
     joined = jnp.concatenate([left, value], axis=1)
     return pltpu.roll(joined, 1, 1)[:, LANES:]
+
+
+LOW, HIGH = 2.0**9, 2.0**20
+SPLIT = 2.0**11
+TO_SOUTH, TO_NORTH = 24, 32
+
+
+def packed_pair(upper, lower):
+    return upper * HIGH + lower * LOW
+
+
+def unpacked_pair(value):
+    upper = jnp.floor(value * (1.0 / SPLIT))
+    lower = value - upper * SPLIT
+    return safe_root(upper * (1.0 / LOW)), safe_root(lower * (1.0 / LOW))
+
+
+def safe_root(weight):
+    present = weight > 0.0
+    return jnp.where(present, root(jnp.where(present, weight, 1.0)), 0.0)
 
 
 def root(weight):
@@ -79,7 +97,7 @@
     lane = lane_index(rows, LANES)
     keep = (lane >= first) & (lane < first + 2)
     cover = m[...].astype(F32)
-    fields = [root(w[layer]) * cover for layer in range(layers)]
+    fields = [w[layer].astype(F32) * cover for layer in range(layers)]
     fields += [d[comp] * cover for comp in range(2)]
     fields += [fr[...] * (cover * (1.0 - fl[...].astype(F32))), cover]
     total = jnp.zeros((rows, LANES), F32)
@@ -101,7 +119,8 @@
     force,
     fric,
     covers,
-    fringe,
+    to_south,
+    to_north,
     w,
     d,
     m,
@@ -139,46 +158,75 @@
             for comp in range(2):
                 force[comp, :, part] = pushes[comp]
 
-            def step(layer, carry, part=part, cover=cover):
-                value = root(w[layer, :, part]) * cover
-                roots[layer, :, part] = value
-                for slot, row in enumerate((0, 1, rows - 1)):
-                    lines[slot, pl.ds(layer, 1), part] = value[row : row + 1]
+            depth = layers // 2
+
+            def step(layer, carry, part=part, cover=cover, depth=depth):
+                pair = [w[index, :, part].astype(F32) for index in (layer, layer + depth)]
+                for weight, index in zip(pair, (layer, layer + depth)):
+                    value = root(weight) * cover
+                    roots[index, :, part] = value
+                    for slot, row in enumerate((0, rows - 1)):
+                        lines[slot, pl.ds(index, 1), part] = value[row : row + 1]
+                upper, lower = (weight * cover for weight in pair)
+
+                def packed(row):
+                    return packed_pair(upper[row : row + 1], lower[row : row + 1])
+
+                to_south[pl.ds(layer, 1), part] = packed(rows - 1)
+                to_north[pl.ds(layer, 1), part] = packed(0)
+                to_north[pl.ds(layer + depth + 4, 1), part] = packed(1)
                 return carry
 
-            lax.fori_loop(0, layers, step, 0, unroll=2)
-            for slot, row in enumerate((0, 1, rows - 1)):
+            lax.fori_loop(0, depth, step, 0, unroll=5)
+            lowest = roots[0, :, part]
+            given = [lowest, pushes[0], pushes[1], drag, geo[:, part]]
+            for slot, row in enumerate((0, rows - 1)):
                 for comp in range(2):
                     lines[slot, F0 + comp : F0 + comp + 1, part] = pushes[comp][row : row + 1]
-                lines[slot, FG : FG + 1, part] = drag[row : row + 1]
-                lines[slot, MASK : MASK + 1, part] = cover[row : row + 1]
-            fields = [roots[0, :, part], pushes[0], pushes[1], drag, geo[:, part]]
-            for slot, row in enumerate((0, rows - 3)):
-                parts = [placed(field, row, 3 * index) for index, field in enumerate(fields)]
-                fringe[slot, :, part] = functools.reduce(jnp.add, parts)
-
-
-def unpack_kernel(half, message, lines, fringe, block, to_south, to_north):
+
+            def send(target, place, fields, row, part=part):
+                for index, field in enumerate(fields):
+                    target[place + index : place + index + 1, part] = field[row : row + 1]
+
+            send(to_south, 10, given[1:], rows - 1)
+            send(to_south, 14, given, rows - 2)
+            send(to_south, 19, given[:3], rows - 3)
+            send(to_north, 10, given[1:], 0)
+            send(to_north, 24, given[1:], 1)
+            send(to_north, 28, given[:3], 2)
+            nothing = jnp.zeros((1, CHUNK), F32)
+            to_south[22:23, part] = nothing
+            to_south[23:24, part] = nothing
+            to_north[31:32, part] = nothing
+
+
+def unpack_kernel(half, message, south_rows_own, north_rows_own, block, to_south, to_north):
     rows = message.shape[0]
-    cols = lines.shape[2]
+    cols = south_rows_own.shape[1]
     first = jnp.where(half[0] == 0, 0, LANES - 2)
     lane = lane_index(rows, LANES)
     keep = (lane >= first) & (lane < first + 2)
     packed = message[...]
-    to_north[0:FIELDS, :cols] = lines[0]
-    to_north[FIELDS : 2 * FIELDS, :cols] = lines[1]
-    to_north[2 * FIELDS :, :cols] = fringe[0]
-    to_south[0:FIELDS, :cols] = lines[2]
-    to_south[FIELDS:, :cols] = fringe[1]
-    to_north[2 * FIELDS :, cols:] = jnp.zeros((16, LANES), F32)
-    to_south[FIELDS:, cols:] = jnp.zeros((16, LANES), F32)
+    to_south[:, :cols] = south_rows_own[...]
+    to_north[:, :cols] = north_rows_own[...]
+    to_south[:, cols:] = jnp.zeros((TO_SOUTH, LANES), F32)
+    to_north[:, cols:] = jnp.zeros((TO_NORTH, LANES), F32)
+    parts = []
     for index in range(FIELDS):
         part = pltpu.roll(packed, LANES - 2 * index, 1) if index else packed
-        part = jnp.where(keep, part, 0.0)
-        block[index] = part
-        to_north[index : index + 1, cols:] = part[0:1]
-        to_north[FIELDS + index : FIELDS + index + 1, cols:] = part[1:2]
-        to_south[index : index + 1, cols:] = part[rows - 1 : rows]
+        parts.append(jnp.where(keep, part, 0.0))
+        block[index] = safe_root(parts[index]) if index < F0 else parts[index]
+    depth = F0 // 2
+    for index in range(depth):
+        pair = packed_pair(parts[index], parts[index + depth])
+        to_south[index : index + 1, cols:] = pair[rows - 1 : rows]
+        to_north[index : index + 1, cols:] = pair[0:1]
+        to_north[depth + 4 + index : depth + 5 + index, cols:] = pair[1:2]
+    for comp in range(2):
+        push = parts[F0 + comp]
+        to_south[10 + comp : 11 + comp, cols:] = push[rows - 1 : rows]
+        to_north[10 + comp : 11 + comp, cols:] = push[0:1]
+        to_north[24 + comp : 25 + comp, cols:] = push[1:2]
 
 
 def line_of(ref, layer, start, size):
@@ -296,39 +344,50 @@
     repair,
     outer,
     totals,
+    over,
+    under,
+    beyond,
 ):
     layers, rows, cols = roots.shape
     chunks = [(start, CHUNK) for start in range(0, cols, CHUNK)]
     block_part = slice(cols, cols + LANES)
+
+    depth = layers // 2
+    for start, size in chunks + [(cols, LANES)]:
+        part = slice(start, start + size)
+        for source, place, target in ((above, 0, over), (below, 0, under), (below, depth + 4, beyond)):
+            target[0:depth, part], target[depth:layers, part] = unpacked_pair(
+                source[place : place + depth, part]
+            )
 
     for start, size in chunks:
         part = slice(start, start + size)
         stop = start + size
         before = slice(start - LANES, start) if start else block_part
         after = slice(stop, stop + LANES)
-        here = below[0:layers, part]
-        top = lines[0, 0:layers, part] * above[0:layers, part]
-        north = here * lines[2, 0:layers, part]
+        here = under[0:layers, part]
+        top = lines[0, 0:layers, part] * over[0:layers, part]
+        north = here * lines[1, 0:layers, part]
         outer[0:layers, part] = north
-        east = here * east_of(here, below[0:layers, after])
-        west = here * west_of(here, below[0:layers, before])
-        south = here * below[FIELDS : FIELDS + layers, part]
-        drag = jnp.where(row_index(layers, size) == 0, below[FG : FG + 1, part], 0.0)
-        full = relax(below[MASK : MASK + 1, part]) + drag
+        east = here * east_of(here, under[0:layers, after])
+        west = here * west_of(here, under[0:layers, before])
+        south = here * beyond[0:layers, part]
+        drag = jnp.where(row_index(layers, size) == 0, below[12:13, part], 0.0)
+        full = relax(jnp.where(here[0:1] > 0.0, 1.0, 0.0)) + drag
         for comp, (col_factor, row_factor) in enumerate(FACTORS):
             row = slice(F0 + comp, F0 + comp + 1)
-            under = slice(FIELDS + F0 + comp, FIELDS + F0 + comp + 1)
-            mid = below[row, part]
-            rise = row_factor * (mid - lines[2, row, part])
-            repair[comp, 0:layers, part] = top * (row_factor * (lines[0, row, part] - above[row, part]))
+            sent = slice(10 + comp, 11 + comp)
+            mid = below[sent, part]
+            rise = row_factor * (mid - lines[1, row, part])
+            repair[comp, 0:layers, part] = top * (row_factor * (lines[0, row, part] - above[sent, part]))
             repair[2 + comp, 0:layers, part] = north * (-rise)
             line[comp, 0:layers, part] = full * mid + (
                 col_factor
                 * (
-                    east * (mid - east_of(mid, below[row, after]))
-                    + west * (mid - west_of(mid, below[row, before]))
+                    east * (mid - east_of(mid, below[sent, after]))
+                    + west * (mid - west_of(mid, below[sent, before]))
                 )
-                + (row_factor * south * (mid - below[under, part]) + north * rise)
+                + (row_factor * south * (mid - below[24 + comp : 25 + comp, part]) + north * rise)
             )
         for index in range(3):
             totals[index, :, part] = jnp.zeros((rows, size), F32)
@@ -338,8 +397,8 @@
     for comp, (col_factor, row_factor) in enumerate(FACTORS):
         here = block[F0 + comp]
         left = force[comp, :, cols - LANES : cols]
-        up = above[F0 + comp : F0 + comp + 1, block_part]
-        down = below[F0 + comp : F0 + comp + 1, block_part]
+        up = above[10 + comp : 11 + comp, block_part]
+        down = below[10 + comp : 11 + comp, block_part]
         side_slopes.append(
             (
                 col_factor * (here - east_of(here, nothing)),
@@ -355,8 +414,8 @@
         here = block[layer]
         east = here * east_of(here, nothing)
         west = here * west_of(here, roots[layer, :, cols - LANES : cols])
-        south = here * south_rows(here, line_of(below, layer, cols, LANES))
-        north = here * north_rows(here, line_of(above, layer, cols, LANES))
+        south = here * south_rows(here, line_of(under, layer, cols, LANES))
+        north = here * north_rows(here, line_of(over, layer, cols, LANES))
         full = side_plain + jnp.where(layer == 0, 1.0, 0.0) * block[FG]
         for comp in range(2):
             slope = side_slopes[comp]
@@ -429,7 +488,8 @@
     norm_next = step_one * (step_one * square - 2.0 * cross) + norm
     lead = 1.0 + norm_next / norm
     curve = lead * lead * cross - 2.0 * lead * step_one * square + step_one * step_one * energy
-    step_two = norm_next / curve
+    sound = (norm_next > 0.0) & (curve > 0.0)
+    step_two = jnp.where(sound, norm_next / jnp.where(sound, curve, 1.0), 0.0)
     return step_one + step_two * lead, -step_two * step_one
 
 
@@ -450,7 +510,7 @@
     ]
     for copy in copies:
         copy.start()
-    for copy in copies:
+    for copy in copies[:6]:
         copy.wait()
     prev, burden, sheet, chan_east, chan_south, area, w, d, m, fl, fr, geo = buffers
     left = info[0] == 0
@@ -476,6 +536,8 @@
             last = tail if last is None else last + tail
         pair[:, part] = jnp.where(left, last, first)
         cross[:, part] = jnp.where(left, first, last)
+    for copy in copies[6:]:
+        copy.wait()
     for start in range(0, cols, CHUNK):
         part = slice(start, start + CHUNK)
 
@@ -535,19 +597,34 @@
         part = slice(start, start + CHUNK)
         middle = pair[:, wide + 2 * cols + start : wide + 2 * cols + start + CHUNK]
         outer = cross[:, wide + start : wide + start + CHUNK]
-        beyond = jnp.where(
-            left, above[FIELDS : FIELDS + 16, part], below[2 * FIELDS : 2 * FIELDS + 16, part]
-        )
+        first_north, _ = unpacked_pair(above[0:1, part])
+        first_south, _ = unpacked_pair(below[0:1, part])
+        second_south, _ = unpacked_pair(below[14:15, part])
+        nothing = jnp.zeros((1, CHUNK), F32)
         replaced = (left & in_north) | (jnp.logical_not(left) & in_south)
         for index in range(5):
             field = tile[index, :, part]
             swapped = jnp.concatenate([field[8:16], field[0:8]], axis=0)
             here = jnp.where(left, field, swapped)
-            far = jnp.where(
-                left,
-                pltpu.roll(beyond, (13 - 3 * index) % 16, 0),
-                pltpu.roll(beyond, (8 - 3 * index) % 16, 0),
-            )
+            if index == 0:
+                ups = above[19:20, part], above[14:15, part], first_north
+                downs = first_south, second_south, below[28:29, part]
+            else:
+                near, next_near, next_far = 9 + index, 14 + index, 23 + index
+                last = index < 3
+                ups = (
+                    above[19 + index : 20 + index, part] if last else nothing,
+                    above[next_near : next_near + 1, part],
+                    above[near : near + 1, part],
+                )
+                downs = (
+                    below[near : near + 1, part],
+                    below[next_far : next_far + 1, part],
+                    below[28 + index : 29 + index, part] if last else nothing,
+                )
+            north = jnp.where(row == 13, ups[0], jnp.where(row == 14, ups[1], ups[2]))
+            south = jnp.where(row == 8, downs[0], jnp.where(row == 9, downs[1], downs[2]))
+            far = jnp.where(left, north, south)
             here = jnp.where(replaced, far, here)
             if index < 4:
                 place = wide + (index // 2) * cols + start
@@ -772,9 +849,17 @@
         far=range(1, 13),
     )(late, *placed_inputs)
     pair_in = lax.ppermute(pair, "hyd", swap)
-    roots, lines, force, fric, cover, fringe = call(
+    roots, lines, force, fric, cover, south_own, north_own = call(
         root_kernel,
-        [shape_of(layers, rows, cols), shape_of(3, FIELDS, cols), shape_of(2, rows, cols), shape_of(rows, cols), shape_of(rows, cols), shape_of(2, rows, cols)],
+        [
+            shape_of(layers, rows, cols),
+            shape_of(2, FIELDS, cols),
+            shape_of(2, rows, cols),
+            shape_of(rows, cols),
+            shape_of(rows, cols),
+            shape_of(TO_SOUTH, cols),
+            shape_of(TO_NORTH, cols),
+        ],
         6,
         scratch=buffers(cols) + [pltpu.VMEM((rows, cols), F32), pltpu.SemaphoreType.DMA((cols // FETCH, 6))],
         far=range(6),
@@ -782,10 +867,10 @@
     wide = cols + LANES
     block, to_south, to_north = call(
         unpack_kernel,
-        [shape_of(FIELDS, rows, LANES), shape_of(FIELDS + 16, wide), shape_of(2 * FIELDS + 16, wide)],
+        [shape_of(FIELDS, rows, LANES), shape_of(TO_SOUTH, wide), shape_of(TO_NORTH, wide)],
         4,
         smem=(0,),
-    )(info, received, lines, fringe)
+    )(info, received, south_own, north_own)
     above = moved(to_south, "ice", 1)
     below = moved(to_north, "ice", -1)
     strip_rows, full = potential_prev.shape
@@ -808,7 +893,8 @@
             pltpu.VMEM((4, FIELDS, cols), F32),
             pltpu.VMEM((FIELDS, cols), F32),
             pltpu.VMEM((3, rows, cols), F32),
-        ],
+        ]
+        + [pltpu.VMEM((FIELDS, wide), F32)] * 3,
         input_output_aliases={8: 0, 10: 1},
     )(roots, force, fric, cover, block, above, below, lines, started, to_east, faces)
     gathered = lax.all_to_all(sums, AXES, 0, 0, tiled=True)

time: 94.5 us -> 99.3 us (1.051)
  waiting for transfers between devices: 21 us -> 31.3 us
  blocking collectives: 32.5 us -> 27.3 us
    ppermute x1, waiting for transfers between devices: 20.4 us -> 30.7 us  [body(): received = lax.ppermute(message, 'hyd', swap)]
    all_to_all x1, blocking collectives: 32.5 us -> 27.3 us  [body(): gathered = lax.all_to_all(sums, AXES, 0, 0, tiled=True)]
    ppermute x1, starting transfers between devices: 0.34 us -> 2.47 us  [body(): received = lax.ppermute(message, 'hyd', swap)]
    ppermute x2, starting transfers between devices: 6.29 us -> 4.34 us  [moved(): lax.ppermute(value, axis, [(source, source + steps) for source in range(l...]
  transfers between devices with their start and end apart: 6 -> 6, of which waited for: 2 -> 2; matrix products, arithmetic and copies ran while one was open for 0% -> 0% of each run, Pallas kernels for 21% -> 20%
where the time goes in v5:
time: 99.3 us; the launch traced here: 99 us
  waiting for transfers between devices  31.3 us (32%)
  Pallas kernels  29 us (29%)
  blocking collectives  27.3 us (27%)
  starting transfers between devices  9.9 us (10%)
    ppermute x1, waiting for transfers between devices, body(): received = lax.ppermute(message, 'hyd', swap)  30.7 us
    all_to_all x1, blocking collectives, body(): gathered = lax.all_to_all(sums, AXES, 0, 0, tiled=True)  27.3 us
    pallas_call x1, Pallas kernels, body(): call(moment_kernel, [shape_of(2, layers, rows, cols), shape_of(layers, ro...  7.84 us
    pallas_call x1, Pallas kernels, body(): call(image_kernel, [shape_of(2, layers, rows, cols), shape_of(layers, row...  4.81 us
    ppermute x2, starting transfers between devices, moved(): lax.ppermute(value, axis, [(source, source + steps) for source in range(l...  4.34 us
    pallas_call x1, Pallas kernels, body(): pl.pallas_call(velocity_kernel, out_shape=shape_of(2, layers, rows, cols)...  3.39 us
    pallas_call x1, Pallas kernels, body(): call(strip_kernel, [shape_of(5, strip_rows, full), shape_of(5, rows, cols...  3 us
    pallas_call x1, Pallas kernels, body(): call(root_kernel, [shape_of(layers, rows, cols), shape_of(2, FIELDS, cols...  2.85 us
  transfers between devices with their start and end apart: 6, of which 2 were waited for; matrix products, arithmetic and copies ran while one was open for 0% of the time, Pallas kernels for 20%

profile of v5, /device:TPU:0, one launch (start us, length us, event | category | flops | bytes accessed | tf_op | source)
XLA Modules:
  0.0 99.0 jit_solution(12375761263752790030)
XLA Ops:
  0.6 0.1 pad_add_fusion.half.info
  0.7 1.6 %shard_map.148 = f32[16,128]{1,0:T(8,128)S(1)} custom-call(s32[3]{0:T(128)S(1)} %pad_add_fusion.half.info, bf16[20,16,3072]{2,1,0:T(8,128)(2,1)} %refs_6_.1, f32[2,16,3072]{2,1,0:T(8,128)} %refs_7_.1, s32[16,3072]{1,0:T(8,128)} %refs_8_.1, s32[16,3072]{1,0:T(8,128)} %refs_9_.1, f32[16,3072]{1,0:T(8,128)} %refs_10_.1), custom_call_target="tpu_custom_call" | custom-call | tf_op jit(solution)/shard_map/pallas_call | solution.py:823
  2.3 3.0 %shard_map.154 = (f32[5,8,6144]{2,1,0:T(8,128)S(1)}, f32[5,16,3072]{2,1,0:T(8,128)S(1)}, f32[16,16896]{1,0:T(8,128)S(1)}, f32[16,9216]{1,0:T(8,128)S(1)}) custom-call(s32[3]{0:T(128)S(1)} %pad_add_fusion.half.info, f32[8,6144]{1,0:T(8,128)} %refs_0_.1, f32[8,6144]{1,0:T(8,128)} %refs_1_.1, f32[8,6144]{1,0:T(8,128)} %refs_2_.1, s32[8,6144]{1,0:T(8,128)} %refs_3_.1, ...), custom_call_target="tpu_custom_call" | custom-call | tf_op jit(solution)/shard_map/pallas_call | solution.py:834
  5.3 1.8 %collective-permute-start.3 = (f32[16,16896]{1,0:T(8,128)S(1)}, f32[16,16896]{1,0:T(8,128)S(1)}, u32[]{:S(2)}, u32[]{:S(2)}) collective-permute-start(f32[16,16896]{1,0:T(8,128)S(1)} %get-tuple-element.50), channel_id=1, source_target_pairs={{0,1},{1,0},{2,3},{3,2},{4,5},{5,4},{6,7},{7,6},{8,9},{9,8},{10,11... | collective-permute-start | bytes 3244040 | tf_op jit(solution)/shard_map/ppermute | solution.py:851
  7.1 0.7 collective-permute-start.4
  7.8 2.5 %collective-permute-start = (f32[16,128]{1,0:T(8,128)S(1)}, f32[16,128]{1,0:T(8,128)S(1)}, u32[]{:S(2)}, u32[]{:S(2)}) collective-permute-start(f32[16,128]{1,0:T(8,128)S(1)} %shard_map.148), channel_id=1, source_target_pairs={{0,1},{1,0},{2,3},{3,2},{4,5},{5,4},{6,7},{7,6},{8,9},{9,8},{10,11... | collective-permute-start | bytes 24584 | tf_op jit(solution)/shard_map/ppermute | solution.py:832
  10.3 2.8 %shard_map.147 = (f32[20,16,3072]{2,1,0:T(8,128)S(1)}, f32[2,24,3072]{2,1,0:T(8,128)S(1)}, f32[2,16,3072]{2,1,0:T(8,128)S(1)}, f32[16,3072]{1,0:T(8,128)S(1)}, f...) custom-call(bf16[20,16,3072]{2,1,0:T(8,128)(2,1)} %refs_6_.1, f32[2,16,3072]{2,1,0:T(8,128)} %refs_7_.1, ...), custom_call_target="tpu_custom_call" | custom-call | tf_op jit(solution)/shard_map/pallas_call | solution.py:852
  13.1 30.7 %collective-permute-done.message = f32[16,128]{1,0:T(8,128)S(1)} collective-permute-done((f32[16,128]{1,0:T(8,128)S(1)}, f32[16,128]{1,0:T(8,128)S(1)}, u32[]{:S(2)}, u32[]{:S(2)}) %collective-permute-start) | collective-permute-done | bytes 8224 | tf_op jit(solution)/shard_map/ppermute | solution.py:832
  43.8 0.7 shard_map.149
  44.4 1.3 %collective-permute-start.2 = (f32[32,3200]{1,0:T(8,128)S(1)}, f32[32,3200]{1,0:T(8,128)S(1)}, u32[]{:S(2)}, u32[]{:S(2)}) collective-permute-start(f32[32,3200]{1,0:T(8,128)S(1)} %get-tuple-element.40), channel_id=1, source_target_pairs={{2,0},{4,2},{6,4},{8,6},{10,8},{12,10},{14,12},{16,14},{18,16},{20... | collective-permute-start | bytes 1228808 | tf_op jit(solution)/shard_map/ppermute | solution.py:780
  45.7 3.0 %collective-permute-start.1 = (f32[24,3200]{1,0:T(8,128)S(1)}, f32[24,3200]{1,0:T(8,128)S(1)}, u32[]{:S(2)}, u32[]{:S(2)}) collective-permute-start(f32[24,3200]{1,0:T(8,128)S(1)} %get-tuple-element.39), channel_id=1, source_target_pairs={{0,2},{2,4},{4,6},{6,8},{8,10},{10,12},{12,14},{14,16},{16,18},{18... | collective-permute-start | bytes 921608 | tf_op jit(solution)/shard_map/ppermute | solution.py:780
  48.8 4.8 %shard_map.150 = (f32[2,20,16,3072]{3,2,1,0:T(8,128)S(1)}, f32[20,16,3072]{2,1,0:T(8,128)S(1)}, f32[20,16,3072]{2,1,0:T(8,128)S(1)}) custom-call(f32[20,16,3072]{2,1,0:T(8,128)S(1)} %get-tuple-element.31.roots, f32[2,16,3072]{2,1,0:T(8,128)S(1)} %get-tuple-element.32.force, f32[16,3072]{1,0:T(8,128)S(1)} %get-tuple-element.33.fric, ...), custom_call_target="tpu_custom_call" | custom-call | tf_op jit(solution)/shard_map/pallas_call | solution.py:880
  53.6 0.0 collective-permute-done.2.below
  53.6 7.8 %shard_map.151 = (f32[2,20,16,3072]{3,2,1,0:T(8,128)S(1)}, f32[20,16,3072]{2,1,0:T(8,128)S(1)}, f32[128,1,128]{2,1,0:T(1,128)S(1)}) custom-call(f32[20,16,3072]{2,1,0:T(8,128)S(1)} %get-tuple-element.31.roots, f32[2,16,3072]{2,1,0:T(8,128)S(1)} %get-tuple-element.32.force, ...), custom_call_target="tpu_custom_call", output_to_operand_aliasing={{0}: (8, {}), {1}: (10, {})} | custom-call | tf_op jit(solution)/shard_map/pallas_call | solution.py:886
  61.5 27.3 %all_to_all.5.gathered = f32[128,1,128]{2,1,0:T(1,128)S(1)} all-to-all(f32[128,1,128]{2,1,0:T(1,128)S(1)} %get-tuple-element.45), channel_id=1, replica_groups=mesh['ice'=64,'hyd'=2] {'ice','hyd'}, dimensions={0} | all-to-all | bytes 131072 | tf_op jit(solution)/shard_map/all_to_all | solution.py:900
  88.8 0.2 shard_map.152.weights
  89.1 0.0 collective-permute-done.4.cross
  89.1 0.0 collective-permute-done.3.pair
  89.1 2.4 %shard_map.155 = (f32[6,16,6144]{2,1,0:T(8,128)S(1)}, f32[10,16,6144]{2,1,0:T(8,128)S(1)}) custom-call(s32[3]{0:T(128)S(1)} %pad_add_fusion.half.info, f32[5,8,6144]{2,1,0:T(8,128)S(1)} %get-tuple-element.48.own, f32[5,16,3072]{2,1,0:T(8,128)S(1)} %get-tuple-element.49.tile, f32[16,16896]{1,0:T(8,128)S(1)} %collective-permute-done.3.pair, ...), custom_call_target="tpu_custom_call" | custom-call | tf_op jit(solution)/shard_map/pallas_call | solution.py:902
  91.5 2.2 %shard_map.156 = (f32[8,6144]{1,0:T(8,128)}, f32[8,6144]{1,0:T(8,128)}, f32[8,3072]{1,0:T(8,128)S(1)}, f32[8,3072]{1,0:T(8,128)S(1)}) custom-call(s32[3]{0:T(128)S(1)} %pad_add_fusion.half.info, f32[2,8,128]{2,1,0:T(8,128)S(1)} %shard_map.152.weights, f32[6,16,6144]{2,1,0:T(8,128)S(1)} %get-tuple-element.52.low, f32[10,16,6144]{2,1,0:T(8,128)S(1)} %get-tuple-element.53.plan), custom_call_target="tpu_custom_call" | custom-call | tf_op jit(solution)/shard_map/pallas_call | solution.py:909
  93.7 0.6 collective-permute-start.5
  94.3 3.4 %shard_map.153 = f32[2,20,16,3072]{3,2,1,0:T(8,128)} custom-call(f32[2,8,128]{2,1,0:T(8,128)S(1)} %shard_map.152.weights, f32[2,16,3072]{2,1,0:T(8,128)S(1)} %get-tuple-element.32.force, f32[2,20,16,3072]{3,2,1,0:T(8,128)S(1)} %get-tuple-element.46.image), custom_call_target="tpu_custom_call" | custom-call | tf_op jit(solution)/shard_map/pallas_call | solution.py:922
  97.7 0.6 collective-permute-done.5
  98.3 0.7 pad_maximum_fusion
  (2 shorter events, 0.0 us)
Async XLA Ops:
  5.3 83.7 %collective-permute-start.3 = (f32[16,16896]{1,0:T(8,128)S(1)}, f32[16,16896]{1,0:T(8,128)S(1)}, u32[]{:S(2)}, u32[]{:S(2)}) collective-permute-start(f32[16,16896]{1,0:T(8,128)S(1)} %get-tuple-element.50), channel_id=1, source_target_pairs={{0,1},{1,0},{2,3},{3,2},{4,5},{5,4},{6,7},{7,6},{8,9},{9,8},{10,11... | collective-permute-start | bytes 3244040 | tf_op jit(solution)/shard_map/ppermute | solution.py:851
  7.1 82.0 %collective-permute-start.4 = (f32[16,9216]{1,0:T(8,128)S(1)}, f32[16,9216]{1,0:T(8,128)S(1)}, u32[]{:S(2)}, u32[]{:S(2)}) collective-permute-start(f32[16,9216]{1,0:T(8,128)S(1)} %get-tuple-element.51), channel_id=1, source_target_pairs={{1,2},{3,4},{5,6},{7,8},{9,10},{11,12},{13,14},{15,16},{17,18},{19... | collective-permute-start | bytes 1769480 | tf_op jit(solution)/shard_map/ppermute | solution.py:878
  7.8 36.0 %collective-permute-start = (f32[16,128]{1,0:T(8,128)S(1)}, f32[16,128]{1,0:T(8,128)S(1)}, u32[]{:S(2)}, u32[]{:S(2)}) collective-permute-start(f32[16,128]{1,0:T(8,128)S(1)} %shard_map.148), channel_id=1, source_target_pairs={{0,1},{1,0},{2,3},{3,2},{4,5},{5,4},{6,7},{7,6},{8,9},{9,8},{10,11... | collective-permute-start | bytes 24584 | tf_op jit(solution)/shard_map/ppermute | solution.py:832
  44.4 9.2 %collective-permute-start.2 = (f32[32,3200]{1,0:T(8,128)S(1)}, f32[32,3200]{1,0:T(8,128)S(1)}, u32[]{:S(2)}, u32[]{:S(2)}) collective-permute-start(f32[32,3200]{1,0:T(8,128)S(1)} %get-tuple-element.40), channel_id=1, source_target_pairs={{2,0},{4,2},{6,4},{8,6},{10,8},{12,10},{14,12},{16,14},{18,16},{20... | collective-permute-start | bytes 1228808 | tf_op jit(solution)/shard_map/ppermute | solution.py:780
  45.7 7.9 %collective-permute-start.1 = (f32[24,3200]{1,0:T(8,128)S(1)}, f32[24,3200]{1,0:T(8,128)S(1)}, u32[]{:S(2)}, u32[]{:S(2)}) collective-permute-start(f32[24,3200]{1,0:T(8,128)S(1)} %get-tuple-element.39), channel_id=1, source_target_pairs={{0,2},{2,4},{4,6},{6,8},{8,10},{10,12},{12,14},{14,16},{16,18},{18... | collective-permute-start | bytes 921608 | tf_op jit(solution)/shard_map/ppermute | solution.py:780
  93.7 4.6 %collective-permute-start.5 = (f32[8,3072]{1,0:T(8,128)S(1)}, f32[8,3072]{1,0:T(8,128)S(1)}, u32[]{:S(2)}, u32[]{:S(2)}) collective-permute-start(f32[8,3072]{1,0:T(8,128)S(1)} %get-tuple-element.55), channel_id=1, source_target_pairs={{0,1},{1,0},{2,3},{3,2},{4,5},{5,4},{6,7},{7,6},{8,9},{9,8},{10,11... | collective-permute-start | bytes 294920 | tf_op jit(solution)/shard_map/ppermute | solution.py:921

commit v6 on v5

--- a/solution.py
+++ b/solution.py
@@ -200,15 +200,13 @@
             to_north[31:32, part] = nothing
 
 
-def unpack_kernel(half, message, south_rows_own, north_rows_own, block, to_south, to_north):
+def unpack_kernel(half, message, block, to_south, to_north):
     rows = message.shape[0]
-    cols = south_rows_own.shape[1]
+    cols = to_south.shape[1] - LANES
     first = jnp.where(half[0] == 0, 0, LANES - 2)
     lane = lane_index(rows, LANES)
     keep = (lane >= first) & (lane < first + 2)
     packed = message[...]
-    to_south[:, :cols] = south_rows_own[...]
-    to_north[:, :cols] = north_rows_own[...]
     to_south[:, cols:] = jnp.zeros((TO_SOUTH, LANES), F32)
     to_north[:, cols:] = jnp.zeros((TO_NORTH, LANES), F32)
     parts = []
@@ -227,6 +225,14 @@
         to_south[10 + comp : 11 + comp, cols:] = push[rows - 1 : rows]
         to_north[10 + comp : 11 + comp, cols:] = push[0:1]
         to_north[24 + comp : 25 + comp, cols:] = push[1:2]
+
+
+def opening_kernel(info, message, *refs):
+    inputs, outs, rest = refs[:6], refs[6:13], refs[13:]
+    roots, lines, force, fric, covers, to_south, to_north = outs[:7]
+    block, scratch = rest[0], rest[1:]
+    root_kernel(*inputs, roots, lines, force, fric, covers, to_south, to_north, *scratch)
+    unpack_kernel(info, message, block, to_south, to_north)
 
 
 def line_of(ref, layer, start, size):
@@ -321,7 +327,7 @@
                 )
         return carry
 
-    lax.fori_loop(0, layers, layer_step, 0)
+    lax.fori_loop(0, layers, layer_step, 0, unroll=2)
 
 
 def moment_kernel(
@@ -736,6 +742,12 @@
         give[:, part] = jnp.where(left, sides[1], sides[0])
 
 
+def closing_kernel(info, own, tile, pair, cross, above, below, weights, *refs):
+    outs, (low, plan, base, hyd), rest = refs[:4], refs[4:8], refs[8:]
+    assemble_kernel(info, own, tile, pair, cross, above, below, low, plan, base, hyd)
+    hydrology_kernel(info, weights, low, plan, *outs, *rest)
+
+
 def velocity_kernel(weights, force, image, out, staged, done):
     layers = image.shape[1]
     first, second = weights[0, 0:1, 0:1], weights[1, 0:1, 0:1]
@@ -799,6 +811,7 @@
     bands = lax.axis_size("ice")
     info = jnp.stack([side, (side == 0) & (band == 0), (side == 1) & (band == bands - 1)]).astype(jnp.int32)
     swap = [(0, 1), (1, 0)]
+    wide = cols + LANES
     fixed_inputs = (
         potential_prev,
         overburden,
@@ -849,28 +862,23 @@
         far=range(1, 13),
     )(late, *placed_inputs)
     pair_in = lax.ppermute(pair, "hyd", swap)
-    roots, lines, force, fric, cover, south_own, north_own = call(
-        root_kernel,
+    roots, lines, force, fric, cover, to_south, to_north, block = call(
+        opening_kernel,
         [
             shape_of(layers, rows, cols),
             shape_of(2, FIELDS, cols),
             shape_of(2, rows, cols),
             shape_of(rows, cols),
             shape_of(rows, cols),
-            shape_of(TO_SOUTH, cols),
-            shape_of(TO_NORTH, cols),
+            shape_of(TO_SOUTH, wide),
+            shape_of(TO_NORTH, wide),
+            shape_of(FIELDS, rows, LANES),
         ],
-        6,
+        8,
         scratch=buffers(cols) + [pltpu.VMEM((rows, cols), F32), pltpu.SemaphoreType.DMA((cols // FETCH, 6))],
-        far=range(6),
-    )(*placed_inputs[6:])
-    wide = cols + LANES
-    block, to_south, to_north = call(
-        unpack_kernel,
-        [shape_of(FIELDS, rows, LANES), shape_of(TO_SOUTH, wide), shape_of(TO_NORTH, wide)],
-        4,
         smem=(0,),
-    )(info, received, south_own, north_own)
+        far=range(2, 8),
+    )(info, received, *placed_inputs[6:])
     above = moved(to_south, "ice", 1)
     below = moved(to_north, "ice", -1)
     strip_rows, full = potential_prev.shape
@@ -899,25 +907,20 @@
     )(roots, force, fric, cover, block, above, below, lines, started, to_east, faces)
     gathered = lax.all_to_all(sums, AXES, 0, 0, tiled=True)
     weights = call(weights_kernel, shape_of(2, 8, LANES), 1)(gathered)
-    low, plan = call(
-        assemble_kernel,
-        [shape_of(6, rows, full), shape_of(10, rows, full)],
-        7,
-        scratch=[pltpu.VMEM((5, rows, full), F32), pltpu.VMEM((5, rows, full), F32)],
-        smem=(0,),
-    )(info, own, tile, pair_in, cross_in, above, below)
     potential, sheet_next, keep, give = call(
-        hydrology_kernel,
+        closing_kernel,
         [
             shape_of(strip_rows, full),
             shape_of(strip_rows, full),
             shape_of(strip_rows, cols),
             shape_of(strip_rows, cols),
         ],
-        4,
-        scratch=[pltpu.VMEM((rows, full), F32)] * 3 + [pltpu.VMEM((strip_rows, full), F32)],
+        8,
+        scratch=[pltpu.VMEM((count_of, rows, full), F32) for count_of in (6, 10, 5, 5)]
+        + [pltpu.VMEM((rows, full), F32)] * 3
+        + [pltpu.VMEM((strip_rows, full), F32)],
         smem=(0,),
-    )(info, weights, low, plan)
+    )(info, own, tile, pair_in, cross_in, above, below, weights)
     got = lax.ppermute(give, "hyd", swap)
     velocity = pl.pallas_call(
         velocity_kernel,

time: 99.3 us -> 102 us (1.027)
  waiting for transfers between devices: 31.3 us -> 34.1 us
    ppermute x1, waiting for transfers between devices: 30.7 us -> 33.5 us  [body(): received = lax.ppermute(message, 'hyd', swap)]
    pallas_call x4 -> x2, Pallas kernels: 8.09 us -> 7.64 us  [the longest x1 4.15 us: body(): call(closing_kernel, [shape_of(strip_rows, full), shape_of(strip_rows, fu...]
  transfers between devices with their start and end apart: 6 -> 6, of which waited for: 2 -> 2; matrix products, arithmetic and copies ran while one was open for 0% -> 0% of each run, Pallas kernels for 20% -> 19%
where the time goes in v6:
time: 102 us
  waiting for transfers between devices  34.1 us (33%)
  Pallas kernels  28.5 us (28%)
  blocking collectives  27.5 us (27%)
  starting transfers between devices  9.9 us (10%)
    ppermute x1, waiting for transfers between devices, body(): received = lax.ppermute(message, 'hyd', swap)  33.5 us
    all_to_all x1, blocking collectives, body(): gathered = lax.all_to_all(sums, AXES, 0, 0, tiled=True)  27.5 us
    pallas_call x1, Pallas kernels, body(): call(moment_kernel, [shape_of(2, layers, rows, cols), shape_of(layers, ro...  7.93 us
    pallas_call x1, Pallas kernels, body(): call(image_kernel, [shape_of(2, layers, rows, cols), shape_of(layers, row...  4.66 us
    ppermute x2, starting transfers between devices, moved(): lax.ppermute(value, axis, [(source, source + steps) for source in range(l...  4.34 us
    pallas_call x1, Pallas kernels, body(): call(closing_kernel, [shape_of(strip_rows, full), shape_of(strip_rows, fu...  4.15 us
    pallas_call x1, Pallas kernels, body(): call(opening_kernel, [shape_of(layers, rows, cols), shape_of(2, FIELDS, c...  3.49 us
    pallas_call x1, Pallas kernels, body(): pl.pallas_call(velocity_kernel, out_shape=shape_of(2, layers, rows, cols)...  3.39 us
  transfers between devices with their start and end apart: 6, of which 2 were waited for; matrix products, arithmetic and copies ran while one was open for 0% of the time, Pallas kernels for 19%

profile of v6, /device:TPU:0, one launch (start us, length us, event | category | flops | bytes accessed | tf_op | source)
XLA Modules:
  0.0 101.5 jit_solution(6887139181454944619)
XLA Ops:
  0.6 0.1 pad_add_fusion.half.info
  0.7 1.6 %shard_map.147 = f32[16,128]{1,0:T(8,128)S(1)} custom-call(s32[3]{0:T(128)S(1)} %pad_add_fusion.half.info, bf16[20,16,3072]{2,1,0:T(8,128)(2,1)} %refs_6_.1, f32[2,16,3072]{2,1,0:T(8,128)} %refs_7_.1, s32[16,3072]{1,0:T(8,128)} %refs_8_.1, s32[16,3072]{1,0:T(8,128)} %refs_9_.1, f32[16,3072]{1,0:T(8,128)} %refs_10_.1), custom_call_target="tpu_custom_call" | custom-call | tf_op jit(solution)/shard_map/pallas_call | solution.py:836
  2.3 3.0 %shard_map.153 = (f32[5,8,6144]{2,1,0:T(8,128)S(1)}, f32[5,16,3072]{2,1,0:T(8,128)S(1)}, f32[16,16896]{1,0:T(8,128)S(1)}, f32[16,9216]{1,0:T(8,128)S(1)}) custom-call(s32[3]{0:T(128)S(1)} %pad_add_fusion.half.info, f32[8,6144]{1,0:T(8,128)} %refs_0_.3, f32[8,6144]{1,0:T(8,128)} %refs_1_.3, f32[8,6144]{1,0:T(8,128)} %refs_2_.3, s32[8,6144]{1,0:T(8,128)} %refs_3_.3, ...), custom_call_target="tpu_custom_call" | custom-call | tf_op jit(solution)/shard_map/pallas_call | solution.py:847
  5.4 1.8 %collective-permute-start.3 = (f32[16,16896]{1,0:T(8,128)S(1)}, f32[16,16896]{1,0:T(8,128)S(1)}, u32[]{:S(2)}, u32[]{:S(2)}) collective-permute-start(f32[16,16896]{1,0:T(8,128)S(1)} %get-tuple-element.44), channel_id=1, source_target_pairs={{0,1},{1,0},{2,3},{3,2},{4,5},{5,4},{6,7},{7,6},{8,9},{9,8},{10,11... | collective-permute-start | bytes 3244040 | tf_op jit(solution)/shard_map/ppermute | solution.py:864
  7.1 0.7 collective-permute-start.4
  7.8 2.5 %collective-permute-start = (f32[16,128]{1,0:T(8,128)S(1)}, f32[16,128]{1,0:T(8,128)S(1)}, u32[]{:S(2)}, u32[]{:S(2)}) collective-permute-start(f32[16,128]{1,0:T(8,128)S(1)} %shard_map.147), channel_id=1, source_target_pairs={{0,1},{1,0},{2,3},{3,2},{4,5},{5,4},{6,7},{7,6},{8,9},{9,8},{10,11... | collective-permute-start | bytes 24584 | tf_op jit(solution)/shard_map/ppermute | solution.py:845
  10.3 33.5 %collective-permute-done.message = f32[16,128]{1,0:T(8,128)S(1)} collective-permute-done((f32[16,128]{1,0:T(8,128)S(1)}, f32[16,128]{1,0:T(8,128)S(1)}, u32[]{:S(2)}, u32[]{:S(2)}) %collective-permute-start) | collective-permute-done | bytes 8224 | tf_op jit(solution)/shard_map/ppermute | solution.py:845
  43.8 3.5 %shard_map.148 = (f32[20,16,3072]{2,1,0:T(8,128)S(1)}, f32[2,24,3072]{2,1,0:T(8,128)S(1)}, f32[2,16,3072]{2,1,0:T(8,128)S(1)}, f32[16,3072]{1,0:T(8,128)S(1)}, f...) custom-call(s32[3]{0:T(128)S(1)} %pad_add_fusion.half.info, ...), custom_call_target="tpu_custom_call" | custom-call | tf_op jit(solution)/shard_map/pallas_call | solution.py:865
  47.3 1.3 %collective-permute-start.2 = (f32[32,3200]{1,0:T(8,128)S(1)}, f32[32,3200]{1,0:T(8,128)S(1)}, u32[]{:S(2)}, u32[]{:S(2)}) collective-permute-start(f32[32,3200]{1,0:T(8,128)S(1)} %get-tuple-element.34), channel_id=1, source_target_pairs={{2,0},{4,2},{6,4},{8,6},{10,8},{12,10},{14,12},{16,14},{18,16},{20... | collective-permute-start | bytes 1228808 | tf_op jit(solution)/shard_map/ppermute | solution.py:792
  48.6 3.0 %collective-permute-start.1 = (f32[24,3200]{1,0:T(8,128)S(1)}, f32[24,3200]{1,0:T(8,128)S(1)}, u32[]{:S(2)}, u32[]{:S(2)}) collective-permute-start(f32[24,3200]{1,0:T(8,128)S(1)} %get-tuple-element.33), channel_id=1, source_target_pairs={{0,2},{2,4},{4,6},{6,8},{8,10},{10,12},{12,14},{14,16},{16,18},{18... | collective-permute-start | bytes 921608 | tf_op jit(solution)/shard_map/ppermute | solution.py:792
  51.7 4.7 %shard_map.149 = (f32[2,20,16,3072]{3,2,1,0:T(8,128)S(1)}, f32[20,16,3072]{2,1,0:T(8,128)S(1)}, f32[20,16,3072]{2,1,0:T(8,128)S(1)}) custom-call(f32[20,16,3072]{2,1,0:T(8,128)S(1)} %get-tuple-element.28.roots, f32[2,16,3072]{2,1,0:T(8,128)S(1)} %get-tuple-element.29.force, f32[16,3072]{1,0:T(8,128)S(1)} %get-tuple-element.30.fric, ...), custom_call_target="tpu_custom_call" | custom-call | tf_op jit(solution)/shard_map/pallas_call | solution.py:888
  56.3 0.0 collective-permute-done.1.above
  56.3 0.0 collective-permute-done.2.below
  56.3 7.9 %shard_map.150 = (f32[2,20,16,3072]{3,2,1,0:T(8,128)S(1)}, f32[20,16,3072]{2,1,0:T(8,128)S(1)}, f32[128,1,128]{2,1,0:T(1,128)S(1)}) custom-call(f32[20,16,3072]{2,1,0:T(8,128)S(1)} %get-tuple-element.28.roots, f32[2,16,3072]{2,1,0:T(8,128)S(1)} %get-tuple-element.29.force, ...), custom_call_target="tpu_custom_call", output_to_operand_aliasing={{0}: (8, {}), {1}: (10, {})} | custom-call | tf_op jit(solution)/shard_map/pallas_call | solution.py:894
  64.3 27.5 %all_to_all.5.gathered = f32[128,1,128]{2,1,0:T(1,128)S(1)} all-to-all(f32[128,1,128]{2,1,0:T(1,128)S(1)} %get-tuple-element.39), channel_id=1, replica_groups=mesh['ice'=64,'hyd'=2] {'ice','hyd'}, dimensions={0} | all-to-all | bytes 131072 | tf_op jit(solution)/shard_map/all_to_all | solution.py:908
  91.8 0.2 shard_map.151.weights
  92.0 0.0 collective-permute-done.4.cross
  92.0 0.0 collective-permute-done.3.pair
  92.0 4.2 %shard_map.154 = (f32[8,6144]{1,0:T(8,128)}, f32[8,6144]{1,0:T(8,128)}, f32[8,3072]{1,0:T(8,128)S(1)}, f32[8,3072]{1,0:T(8,128)S(1)}) custom-call(s32[3]{0:T(128)S(1)} %pad_add_fusion.half.info, f32[5,8,6144]{2,1,0:T(8,128)S(1)} %get-tuple-element.42.own, f32[5,16,3072]{2,1,0:T(8,128)S(1)} %get-tuple-element.43.tile, ...), custom_call_target="tpu_custom_call" | custom-call | tf_op jit(solution)/shard_map/pallas_call | solution.py:910
  96.2 0.6 collective-permute-start.5
  96.8 3.4 %shard_map.152 = f32[2,20,16,3072]{3,2,1,0:T(8,128)} custom-call(f32[2,8,128]{2,1,0:T(8,128)S(1)} %shard_map.151.weights, f32[2,16,3072]{2,1,0:T(8,128)S(1)} %get-tuple-element.29.force, f32[2,20,16,3072]{3,2,1,0:T(8,128)S(1)} %get-tuple-element.40.image), custom_call_target="tpu_custom_call" | custom-call | tf_op jit(solution)/shard_map/pallas_call | solution.py:925
  100.2 0.6 collective-permute-done.5
  100.8 0.7 pad_maximum_fusion
  (1 shorter events, 0.0 us)
Async XLA Ops:
  5.4 86.7 %collective-permute-start.3 = (f32[16,16896]{1,0:T(8,128)S(1)}, f32[16,16896]{1,0:T(8,128)S(1)}, u32[]{:S(2)}, u32[]{:S(2)}) collective-permute-start(f32[16,16896]{1,0:T(8,128)S(1)} %get-tuple-element.44), channel_id=1, source_target_pairs={{0,1},{1,0},{2,3},{3,2},{4,5},{5,4},{6,7},{7,6},{8,9},{9,8},{10,11... | collective-permute-start | bytes 3244040 | tf_op jit(solution)/shard_map/ppermute | solution.py:864
  7.1 84.9 %collective-permute-start.4 = (f32[16,9216]{1,0:T(8,128)S(1)}, f32[16,9216]{1,0:T(8,128)S(1)}, u32[]{:S(2)}, u32[]{:S(2)}) collective-permute-start(f32[16,9216]{1,0:T(8,128)S(1)} %get-tuple-element.45), channel_id=1, source_target_pairs={{1,2},{3,4},{5,6},{7,8},{9,10},{11,12},{13,14},{15,16},{17,18},{19... | collective-permute-start | bytes 1769480 | tf_op jit(solution)/shard_map/ppermute | solution.py:886
  7.8 36.0 %collective-permute-start = (f32[16,128]{1,0:T(8,128)S(1)}, f32[16,128]{1,0:T(8,128)S(1)}, u32[]{:S(2)}, u32[]{:S(2)}) collective-permute-start(f32[16,128]{1,0:T(8,128)S(1)} %shard_map.147), channel_id=1, source_target_pairs={{0,1},{1,0},{2,3},{3,2},{4,5},{5,4},{6,7},{7,6},{8,9},{9,8},{10,11... | collective-permute-start | bytes 24584 | tf_op jit(solution)/shard_map/ppermute | solution.py:845
  47.3 9.0 %collective-permute-start.2 = (f32[32,3200]{1,0:T(8,128)S(1)}, f32[32,3200]{1,0:T(8,128)S(1)}, u32[]{:S(2)}, u32[]{:S(2)}) collective-permute-start(f32[32,3200]{1,0:T(8,128)S(1)} %get-tuple-element.34), channel_id=1, source_target_pairs={{2,0},{4,2},{6,4},{8,6},{10,8},{12,10},{14,12},{16,14},{18,16},{20... | collective-permute-start | bytes 1228808 | tf_op jit(solution)/shard_map/ppermute | solution.py:792
  48.6 7.7 %collective-permute-start.1 = (f32[24,3200]{1,0:T(8,128)S(1)}, f32[24,3200]{1,0:T(8,128)S(1)}, u32[]{:S(2)}, u32[]{:S(2)}) collective-permute-start(f32[24,3200]{1,0:T(8,128)S(1)} %get-tuple-element.33), channel_id=1, source_target_pairs={{0,2},{2,4},{4,6},{6,8},{8,10},{10,12},{12,14},{14,16},{16,18},{18... | collective-permute-start | bytes 921608 | tf_op jit(solution)/shard_map/ppermute | solution.py:792
  96.2 4.6 %collective-permute-start.5 = (f32[8,3072]{1,0:T(8,128)S(1)}, f32[8,3072]{1,0:T(8,128)S(1)}, u32[]{:S(2)}, u32[]{:S(2)}) collective-permute-start(f32[8,3072]{1,0:T(8,128)S(1)} %get-tuple-element.47), channel_id=1, source_target_pairs={{0,1},{1,0},{2,3},{3,2},{4,5},{5,4},{6,7},{7,6},{8,9},{9,8},{10,11... | collective-permute-start | bytes 294920 | tf_op jit(solution)/shard_map/ppermute | solution.py:924
